TPU v7x, 32 devices: a whole 2x2x4 slice. The times are simulated.
32 devices in a mesh: region: 8 (over y, x, core), cuts: 4 (over z).
Axes of the slice: x: 2, y: 2, z: 4, core: 2. Of those that a mesh axis runs over, the one named last changes fastest.
Arguments:
- history: bfloat16 [8, 8192, 128], P(None, ('region', 'cuts')), may hold values from -6 to 6
- incident: bfloat16 [4, 8192, 128], P(None, ('region', 'cuts')), may hold values from -6 to 6
- self_inverse: bfloat16 [8192, 256], P(('region', 'cuts')), may hold values from -0.375 to 0.375
- lag_kernels: bfloat16 [384, 8, 256, 256], P(('region', 'cuts')), may hold values from -0.02734375 to 0.02734375
- pair_partner: int32 [384], P(('region', 'cuts')), may hold values from 0 to 11
- pair_lags: int32 [384], P(('region', 'cuts')), may hold values from 1 to 8
Outputs:
- densities: bfloat16 [4, 8192, 128], P(None, ('region', 'cuts'))
Inputs may be any that keep to these rules, and one draw needn't show every extreme that they name: `pair_partner`: codes below 4 name a block of the region before the owner's, codes from 8 on one of the region after it, the others one of the owner's region; the same block may be named by several pairs, and a pair's partner may be its owner. Pair p uses lag matrices 1 to pair_lags[p]; the rest are stored but unused.
All inputs are finite; a program needn't handle non-finite values.
Results may differ from a plain program's by a relative error of at most 0.0095.
Values may be sent and summed in bfloat16 or wider, within the bound.
No kernel may reach another device: no remote copies, remote signals or barrier semaphores. Data moves between devices by JAX's collectives and lax.ppermute only.
A program may use at most 128 MiB of HBM per device.

v0:
```python
import jax
import jax.numpy as jnp
from jax import lax
from jax.sharding import PartitionSpec as P


def padded(block, sides, width):
    for axis, dim in sides:
        count = lax.axis_size(axis)
        forward = [(i, i + 1) for i in range(count - 1)]
        forward.append((count - 1, 0))
        backward = [(target, source) for source, target in forward]
        low = lax.ppermute(
            lax.slice_in_dim(block, block.shape[dim] - width, None, axis=dim), axis, forward
        )
        high = lax.ppermute(lax.slice_in_dim(block, 0, width, axis=dim), axis, backward)
        block = jnp.concatenate([low, block, high], axis=dim)
    return block


def shifted(block, axis, distance):
    devices = range(lax.axis_size(axis))
    route = [((i - distance) % len(devices), i) for i in devices]
    return lax.ppermute(block, axis, route)


def lag_gate(pair_lags, lag_total):
    lag_ids = lax.iota(jnp.int32, lag_total) + 1
    return (lag_ids[None, :] <= pair_lags[:, None]).astype(jnp.bfloat16)


def near_field(lag_kernels, window, recent, pair_partner, gate_table, cut_count, own_cut):
    partner_hist = jnp.take(window, pair_partner, axis=1)
    partner_hist = partner_hist * jnp.transpose(gate_table)[:, :, None, None]
    forward = jnp.einsum(
        "plij,lpjr->ir", lag_kernels, partner_hist, preferred_element_type=jnp.float32
    )
    own_hist = gate_table[:, :, None, None] * recent[None]
    backward = jnp.einsum(
        "plij,plir->pjr", lag_kernels, own_hist, preferred_element_type=jnp.float32
    )
    slot_codes = lax.iota(jnp.int32, 3 * cut_count)
    select = (slot_codes[:, None] == pair_partner[None, :]).astype(jnp.float32)
    spread = jnp.einsum("qp,pjr->qjr", select, backward, precision=lax.Precision.HIGHEST)
    own_slot = (slot_codes == cut_count + own_cut).astype(jnp.float32)
    return spread + own_slot[:, None, None] * forward[None]


def on_device(history, incident, self_inverse, lag_kernels, pair_partner, pair_lags):
    lag_total = history.shape[0]
    step_total = incident.shape[0]
    panel_count = history.shape[1]
    column_count = history.shape[2]
    cut_count = lax.axis_size("cuts")
    own_cut = lax.axis_index("cuts")
    gate_table = lag_gate(pair_lags, lag_total)
    recent = history
    window = history
    outputs = []
    for step_now in range(step_total):
        stacked = lax.all_gather(recent[:, None, None], "cuts", axis=2, tiled=True)
        bordered = padded(stacked, (("region", 1),), 1)
        window = bordered.reshape(lag_total, 3 * cut_count, panel_count, column_count)
        partial_field = near_field(
            lag_kernels, window, recent, pair_partner, gate_table, cut_count, own_cut
        )
        grouped = partial_field.reshape(3, cut_count, panel_count, column_count)
        from_above = shifted(grouped[0].astype(jnp.bfloat16), "region", -1).astype(jnp.float32)
        from_below = shifted(grouped[2].astype(jnp.bfloat16), "region", 1).astype(jnp.float32)
        field_sum = lax.psum_scatter(
            grouped[1] + from_above + from_below, "cuts", scatter_dimension=0, tiled=True
        )[0]
        excess = (incident[step_now].astype(jnp.float32) - field_sum).astype(jnp.bfloat16)
        density = jnp.dot(self_inverse, excess, preferred_element_type=jnp.float32).astype(
            jnp.bfloat16
        )
        outputs.append(density)
        recent = jnp.concatenate([density[None], recent[:-1]], axis=0)
    return jnp.stack(outputs)


def solution(mesh):
    return jax.shard_map(
        on_device,
        mesh=mesh,
        in_specs=(
            P(None, ("region", "cuts"), None),
            P(None, ("region", "cuts"), None),
            P(("region", "cuts"), None),
            P(("region", "cuts"), None, None, None),
            P(("region", "cuts")),
            P(("region", "cuts")),
        ),
        out_specs=P(None, ("region", "cuts"), None),
        check_vma=False,
    )
```

profile of v0, /device:TPU:0, one launch (start us, length us, event | category | flops | bytes accessed | tf_op | source)
XLA Modules:
  0.0 628.2 jit_solution(11969034751456141057)
XLA Ops:
  9.3 48.0 %all-gather.9.cloned.1.call-done = bf16[8,1024,128]{2,1,0:T(8,128)(2,1)} async-done(((bf16[8,256,128]{2,1,0:T(8,128)(2,1)}), bf16[8,1024,128]{2,1,0:T(8,128)(2,1)}) %all-gather.9.cloned.1.call-update) | async-done | bytes 2097168 | tf_op jit(solution)/shard_map/all_gather | solution.py:61
  57.3 1.7 collective-permute-start.1
  59.0 7.6 %fusion.28 = f32[12,256,128]{1,2,0:T(8,128)} fusion(bf16[12,8,256,256]{3,2,1,0:T(8,128)(2,1)} %param.11, bf16[8,256,128]{1,2,0:T(8,128)(2,1)S(1)} %copy.43, bf16[12,8]{1,0:T(8,128)(2,1)S(1)} %compare_convert_fusion.1), kind=kOutput, calls=%fused_computation.44 | convolution fusion | flops 1613758464 | bytes 14680256 | tf_op jit(solution)/shard_map/plij,plir->pjr/dot_general | solution.py:39
  66.6 2.1 copy.44
  68.9 35.7 %collective-permute-done.1 = bf16[8,1,4,256,128]{4,3,2,1,0:T(8,128)(2,1)} collective-permute-done((bf16[8,1,4,256,128]{4,3,2,1,0:T(8,128)(2,1)}, bf16[8,1,4,256,128]{4,3,2,1,0:T(8,128)(2,1)}, u32[]{:S(2)}, u32[]{:S(2)}) %collective-permute-start.1) | collective-permute-done | bytes 2097184 | tf_op jit(solution)/shard_map/ppermute | solution.py:16
  104.6 1.9 collective-permute-done
  106.5 6.5 %pad_maximum_fusion = bf16[8,3,4,256,128]{4,3,2,1,0:T(8,128)(2,1)} fusion(bf16[8,1,4,256,128]{4,3,2,1,0:T(8,128)(2,1)} %collective-permute-done.1, bf16[8,1,4,256,128]{4,3,2,1,0:T(8,128)(2,1)} %bitcast.128, bf16[8,1,4,256,128]{4,3,2,1,0:T(8,128)(2,1)} %collective-permute-done), kind=kLoop, calls=%fused_computation.12 | loop fusion | flops 6291456 | bytes 12582912 | tf_op jit(solution)/shard_map/concatenate | solution.py:17
  113.0 7.0 %gather_fusion = bf16[12,8,256,128]{3,2,1,0:T(8,128)(2,1)} fusion(bf16[8,12,256,128]{3,2,1,0:T(8,128)(2,1)} %bitcast.123, s32[1024]{0:T(1024)S(1)} %pad_clamp_fusion), kind=kCustom, calls=%fused_computation.clone | custom fusion | bytes 12582960 | tf_op jit(solution)/shard_map/jit(_take)/gather | solution.py:33
  119.9 12.1 %fusion.40 = f32[256,128]{0,1:T(8,128)S(1)} fusion(bf16[12,8,256,256]{3,2,1,0:T(8,128)(2,1)} %param.11, bf16[12,8,256,128]{3,2,1,0:T(8,128)(2,1)} %gather_fusion, pred[12]{0:T(512)(128)(4,1)S(1)} %compare_and_fusion, bf16[8,12]{0,1:T(8,128)(2,1)S(1)} %compare_convert_fusion), kind=kOutput, calls=%fused_computation.48 | convolution fusion | flops 1616904192 | bytes 19005644 | tf_op jit(solution)/shard_map/plij,lpjr->ir/dot_general | solution.py:35
  133.7 2.6 collective-permute-start.2
  136.3 6.2 collective-permute-done.3
  143.7 19.7 %reduce-scatter.5.cloned.1.call-done = f32[1,256,128]{2,1,0:T(8,128)} async-done(((f32[4,256,128]{2,1,0:T(8,128)}), f32[1,256,128]{2,1,0:T(8,128)}) %reduce-scatter.5.cloned.1.call-update) | async-done | bytes 131088 | tf_op jit(solution)/shard_map/reduce_scatter | solution.py:70
  165.6 44.0 %all-gather.11.cloned.1.call-done = bf16[8,1024,128]{2,1,0:T(8,128)(2,1)} async-done(((bf16[8,256,128]{2,1,0:T(8,128)(2,1)}), bf16[8,1024,128]{2,1,0:T(8,128)(2,1)}) %all-gather.11.cloned.1.call-update) | async-done | bytes 2097168 | tf_op jit(solution)/shard_map/all_gather | solution.py:61
  209.6 1.7 collective-permute-start.5
  212.6 7.6 %fusion.31 = f32[12,256,128]{1,2,0:T(8,128)} fusion(bf16[12,8,256,256]{3,2,1,0:T(8,128)(2,1)} %param.11, bf16[8,256,128]{1,2,0:T(8,128)(2,1)S(1)} %copy.50, bf16[12,8]{1,0:T(8,128)(2,1)S(1)} %compare_convert_fusion.1), kind=kOutput, calls=%fused_computation.45 | convolution fusion | flops 1613758464 | bytes 14680256 | tf_op jit(solution)/shard_map/plij,plir->pjr/dot_general | solution.py:39
  220.2 2.1 copy.51
  222.4 34.6 %collective-permute-done.5 = bf16[8,1,4,256,128]{4,3,2,1,0:T(8,128)(2,1)} collective-permute-done((bf16[8,1,4,256,128]{4,3,2,1,0:T(8,128)(2,1)}, bf16[8,1,4,256,128]{4,3,2,1,0:T(8,128)(2,1)}, u32[]{:S(2)}, u32[]{:S(2)}) %collective-permute-start.5) | collective-permute-done | bytes 2097184 | tf_op jit(solution)/shard_map/ppermute | solution.py:16
  257.0 1.8 collective-permute-done.4
  258.7 6.5 %pad_maximum_fusion.1 = bf16[8,3,4,256,128]{4,3,2,1,0:T(8,128)(2,1)} fusion(bf16[8,1,4,256,128]{4,3,2,1,0:T(8,128)(2,1)} %collective-permute-done.5, bf16[8,1,4,256,128]{4,3,2,1,0:T(8,128)(2,1)} %bitcast.134, bf16[8,1,4,256,128]{4,3,2,1,0:T(8,128)(2,1)} %collective-permute-done.4), kind=kLoop, calls=%fused_computation.13 | loop fusion | flops 6291456 | bytes 12582912 | tf_op jit(solution)/shard_map/concatenate | solution.py:17
  265.2 7.0 %gather_fusion.1 = bf16[12,8,256,128]{3,2,1,0:T(8,128)(2,1)} fusion(bf16[8,12,256,128]{3,2,1,0:T(8,128)(2,1)} %bitcast.124, s32[1024]{0:T(1024)S(1)} %pad_clamp_fusion), kind=kCustom, calls=%fused_computation.1.clone | custom fusion | bytes 12582960 | tf_op jit(solution)/shard_map/jit(_take)/gather | solution.py:33
  272.2 12.1 %fusion.45 = f32[256,128]{0,1:T(8,128)S(1)} fusion(bf16[12,8,256,256]{3,2,1,0:T(8,128)(2,1)} %param.11, bf16[12,8,256,128]{3,2,1,0:T(8,128)(2,1)} %gather_fusion.1, pred[12]{0:T(512)(128)(4,1)S(1)} %copy-done.9, bf16[8,12]{0,1:T(8,128)(2,1)S(1)} %copy-done.5), kind=kOutput, calls=%fused_computation.49 | convolution fusion | flops 1616904192 | bytes 19005644 | tf_op jit(solution)/shard_map/plij,lpjr->ir/dot_general | solution.py:35
  285.9 2.6 collective-permute-start.6
  288.6 6.2 collective-permute-done.7
  296.0 19.4 %reduce-scatter.7.cloned.1.call-done = f32[1,256,128]{2,1,0:T(8,128)} async-done(((f32[4,256,128]{2,1,0:T(8,128)}), f32[1,256,128]{2,1,0:T(8,128)}) %reduce-scatter.7.cloned.1.call-update) | async-done | bytes 131088 | tf_op jit(solution)/shard_map/reduce_scatter | solution.py:70
  317.5 44.1 %all-gather.13.cloned.1.call-done = bf16[8,1024,128]{2,1,0:T(8,128)(2,1)} async-done(((bf16[8,256,128]{2,1,0:T(8,128)(2,1)}), bf16[8,1024,128]{2,1,0:T(8,128)(2,1)}) %all-gather.13.cloned.1.call-update) | async-done | bytes 2097168 | tf_op jit(solution)/shard_map/all_gather | solution.py:61
  361.5 1.7 collective-permute-start.9
  364.7 7.6 %fusion.34 = f32[12,256,128]{1,2,0:T(8,128)} fusion(bf16[12,8,256,256]{3,2,1,0:T(8,128)(2,1)} %param.11, bf16[8,256,128]{1,2,0:T(8,128)(2,1)S(1)} %copy.57, bf16[12,8]{1,0:T(8,128)(2,1)S(1)} %compare_convert_fusion.1), kind=kOutput, calls=%fused_computation.46 | convolution fusion | flops 1613758464 | bytes 14680256 | tf_op jit(solution)/shard_map/plij,plir->pjr/dot_general | solution.py:39
  372.3 2.1 copy.58
  374.4 34.6 %collective-permute-done.9 = bf16[8,1,4,256,128]{4,3,2,1,0:T(8,128)(2,1)} collective-permute-done((bf16[8,1,4,256,128]{4,3,2,1,0:T(8,128)(2,1)}, bf16[8,1,4,256,128]{4,3,2,1,0:T(8,128)(2,1)}, u32[]{:S(2)}, u32[]{:S(2)}) %collective-permute-start.9) | collective-permute-done | bytes 2097184 | tf_op jit(solution)/shard_map/ppermute | solution.py:16
  409.0 1.7 collective-permute-done.8
  410.7 6.5 %pad_maximum_fusion.2 = bf16[8,3,4,256,128]{4,3,2,1,0:T(8,128)(2,1)} fusion(bf16[8,1,4,256,128]{4,3,2,1,0:T(8,128)(2,1)} %collective-permute-done.9, bf16[8,1,4,256,128]{4,3,2,1,0:T(8,128)(2,1)} %bitcast.137, bf16[8,1,4,256,128]{4,3,2,1,0:T(8,128)(2,1)} %collective-permute-done.8), kind=kLoop, calls=%fused_computation.14 | loop fusion | flops 6291456 | bytes 12582912 | tf_op jit(solution)/shard_map/concatenate | solution.py:17
  417.2 7.0 %gather_fusion.2 = bf16[12,8,256,128]{3,2,1,0:T(8,128)(2,1)} fusion(bf16[8,12,256,128]{3,2,1,0:T(8,128)(2,1)} %bitcast.125, s32[1024]{0:T(1024)S(1)} %pad_clamp_fusion), kind=kCustom, calls=%fused_computation.2.clone | custom fusion | bytes 12582960 | tf_op jit(solution)/shard_map/jit(_take)/gather | solution.py:33
  424.2 12.1 %fusion.50 = f32[256,128]{0,1:T(8,128)S(1)} fusion(bf16[12,8,256,256]{3,2,1,0:T(8,128)(2,1)} %param.11, bf16[12,8,256,128]{3,2,1,0:T(8,128)(2,1)} %gather_fusion.2, pred[12]{0:T(512)(128)(4,1)S(1)} %copy-done.10, bf16[8,12]{0,1:T(8,128)(2,1)S(1)} %copy-done.6), kind=kOutput, calls=%fused_computation.50 | convolution fusion | flops 1616904192 | bytes 19005644 | tf_op jit(solution)/shard_map/plij,lpjr->ir/dot_general | solution.py:35
  437.9 2.6 collective-permute-start.10
  440.5 6.2 collective-permute-done.11
  447.9 19.3 %reduce-scatter.9.cloned.1.call-done = f32[1,256,128]{2,1,0:T(8,128)} async-done(((f32[4,256,128]{2,1,0:T(8,128)}), f32[1,256,128]{2,1,0:T(8,128)}) %reduce-scatter.9.cloned.1.call-update) | async-done | bytes 131088 | tf_op jit(solution)/shard_map/reduce_scatter | solution.py:70
  469.4 44.0 %all-gather.15.cloned.1.call-done = bf16[8,1024,128]{2,1,0:T(8,128)(2,1)} async-done(((bf16[8,256,128]{2,1,0:T(8,128)(2,1)}), bf16[8,1024,128]{2,1,0:T(8,128)(2,1)}) %all-gather.15.cloned.1.call-update) | async-done | bytes 2097168 | tf_op jit(solution)/shard_map/all_gather | solution.py:61
  513.4 1.7 collective-permute-start.13
  516.5 7.6 %fusion.37 = f32[12,256,128]{1,2,0:T(8,128)} fusion(bf16[12,8,256,256]{3,2,1,0:T(8,128)(2,1)} %param.11, bf16[8,256,128]{1,2,0:T(8,128)(2,1)S(1)} %copy.64, bf16[12,8]{1,0:T(8,128)(2,1)S(1)} %compare_convert_fusion.1), kind=kOutput, calls=%fused_computation.47 | convolution fusion | flops 1613758464 | bytes 14680256 | tf_op jit(solution)/shard_map/plij,plir->pjr/dot_general | solution.py:39
  524.1 2.1 copy.65
  526.3 34.6 %collective-permute-done.13 = bf16[8,1,4,256,128]{4,3,2,1,0:T(8,128)(2,1)} collective-permute-done((bf16[8,1,4,256,128]{4,3,2,1,0:T(8,128)(2,1)}, bf16[8,1,4,256,128]{4,3,2,1,0:T(8,128)(2,1)}, u32[]{:S(2)}, u32[]{:S(2)}) %collective-permute-start.13) | collective-permute-done | bytes 2097184 | tf_op jit(solution)/shard_map/ppermute | solution.py:16
  560.9 1.7 collective-permute-done.12
  562.6 6.5 %pad_maximum_fusion.3 = bf16[8,3,4,256,128]{4,3,2,1,0:T(8,128)(2,1)} fusion(bf16[8,1,4,256,128]{4,3,2,1,0:T(8,128)(2,1)} %collective-permute-done.13, bf16[8,1,4,256,128]{4,3,2,1,0:T(8,128)(2,1)} %bitcast.131, bf16[8,1,4,256,128]{4,3,2,1,0:T(8,128)(2,1)} %collective-permute-done.12), kind=kLoop, calls=%fused_computation.15 | loop fusion | flops 6291456 | bytes 12582912 | tf_op jit(solution)/shard_map/concatenate | solution.py:17
  569.0 7.0 %gather_fusion.3 = bf16[12,8,256,128]{3,2,1,0:T(8,128)(2,1)} fusion(bf16[8,12,256,128]{3,2,1,0:T(8,128)(2,1)} %bitcast.122, s32[1024]{0:T(1024)S(1)} %pad_clamp_fusion), kind=kCustom, calls=%fused_computation.3.clone | custom fusion | bytes 12582960 | tf_op jit(solution)/shard_map/jit(_take)/gather | solution.py:33
  576.0 12.1 %fusion.55 = f32[256,128]{0,1:T(8,128)S(1)} fusion(bf16[12,8,256,256]{3,2,1,0:T(8,128)(2,1)} %param.11, bf16[12,8,256,128]{3,2,1,0:T(8,128)(2,1)} %gather_fusion.3, pred[12]{0:T(512)(128)(4,1)S(1)} %copy-done.10, bf16[8,12]{0,1:T(8,128)(2,1)S(1)} %copy-done.6), kind=kOutput, calls=%fused_computation.51 | convolution fusion | flops 1616904192 | bytes 19005644 | tf_op jit(solution)/shard_map/plij,lpjr->ir/dot_general | solution.py:35
  589.7 2.6 collective-permute-start.14
  592.4 6.2 collective-permute-done.15
  599.7 19.3 %reduce-scatter.11.cloned.1.call-done = f32[1,256,128]{2,1,0:T(8,128)} async-done(((f32[4,256,128]{2,1,0:T(8,128)}), f32[1,256,128]{2,1,0:T(8,128)}) %reduce-scatter.11.cloned.1.call-update) | async-done | bytes 131088 | tf_op jit(solution)/shard_map/reduce_scatter | solution.py:70
  (96 shorter events, 26.7 us)
Async XLA Ops:
  6.5 156.9 %copy-start = (bf16[256,256]{1,0:T(8,128)(2,1)S(1)}, bf16[256,256]{1,0:T(8,128)(2,1)}, u32[]{:S(2)}) copy-start(bf16[256,256]{1,0:T(8,128)(2,1)} %param.10) | copy-start | bytes 393220
  6.5 50.8 %all-gather.9.cloned.1.call-start = ((), (), s32[]{:S(2)}) async-start(), calls=%async_computation.8 | async-start | bytes 2621440 | tf_op jit(solution)/shard_map/all_gather | solution.py:61
  7.3 156.1 %reduce-scatter.5.cloned.1.call-start = ((), (), s32[]{:S(2)}) async-start(), calls=%async_computation.4 | async-start | bytes 655360 | tf_op jit(solution)/shard_map/reduce_scatter | solution.py:70
  57.3 11.4 %copy-start.3 = (s32[12]{0:T(128)S(1)}, s32[12]{0:T(128)}, u32[]{:S(2)}) copy-start(s32[12]{0:T(128)} %param.12) | copy-start | bytes 148
  57.3 11.5 %copy-start.7 = (s32[12]{0:T(128)S(1)}, s32[12]{0:T(128)}, u32[]{:S(2)}) copy-start(s32[12]{0:T(128)} %param.13) | copy-start | bytes 148
  57.3 47.2 %collective-permute-start.1 = (bf16[8,1,4,256,128]{4,3,2,1,0:T(8,128)(2,1)}, bf16[8,1,4,256,128]{4,3,2,1,0:T(8,128)(2,1)}, u32[]{:S(2)}, u32[]{:S(2)}) collective-permute-start(bf16[8,1,4,256,128]{4,3,2,1,0:T(8,128)(2,1)} %bitcast.126), channel_id=1, source_target_pairs={{4,0},{8,4},{12,8},{16,12},{20,16},{24,20},{28,24},{0,28},{5,1},{9... | collective-permute-start | bytes 6291464 | tf_op jit(solution)/shard_map/ppermute | solution.py:16
  59.0 47.5 %collective-permute-start = (bf16[8,1,4,256,128]{4,3,2,1,0:T(8,128)(2,1)}, bf16[8,1,4,256,128]{4,3,2,1,0:T(8,128)(2,1)}, u32[]{:S(2)}, u32[]{:S(2)}) collective-permute-start(bf16[8,1,4,256,128]{4,3,2,1,0:T(8,128)(2,1)} %bitcast.127), channel_id=1, source_target_pairs={{0,4},{4,8},{8,12},{12,16},{16,20},{20,24},{24,28},{28,0},{1,5},{5... | collective-permute-start | bytes 6291464 | tf_op jit(solution)/shard_map/ppermute | solution.py:13
  68.8 51.1 %copy-start.8 = (pred[12]{0:T(512)(128)(4,1)}, pred[12]{0:T(512)(128)(4,1)S(1)}, u32[]{:S(2)}) copy-start(pred[12]{0:T(512)(128)(4,1)S(1)} %compare_and_fusion) | copy-start | bytes 40
  68.9 51.0 %copy-start.4 = (bf16[8,12]{0,1:T(8,128)(2,1)}, bf16[8,12]{0,1:T(8,128)(2,1)S(1)}, u32[]{:S(2)}) copy-start(bf16[8,12]{0,1:T(8,128)(2,1)S(1)} %compare_convert_fusion) | copy-start | bytes 580
  132.0 11.7 %copy-start.1 = (bf16[8,256,128]{2,1,0:T(8,128)(2,1)S(1)}, bf16[8,256,128]{2,1,0:T(8,128)(2,1)}, u32[]{:S(2)}) copy-start(bf16[8,256,128]{2,1,0:T(8,128)(2,1)} %param.8) | copy-start | bytes 1572868
  132.0 31.4 %copy-start.2 = (bf16[4,256,128]{2,1,0:T(8,128)(2,1)S(1)}, bf16[4,256,128]{2,1,0:T(8,128)(2,1)}, u32[]{:S(2)}) copy-start(bf16[4,256,128]{2,1,0:T(8,128)(2,1)} %param.9) | copy-start | bytes 786436
  133.6 8.9 %collective-permute-start.3 = (bf16[4,256,128]{2,0,1:T(4,128)(2,1)S(1)}, bf16[4,256,128]{2,0,1:T(4,128)(2,1)S(1)}, u32[]{:S(2)}, u32[]{:S(2)}) collective-permute-start(bf16[4,256,128]{2,0,1:T(4,128)(2,1)S(1)} %get-tuple-element.13), channel_id=1, source_target_pairs={{28,0},{0,4},{4,8},{8,12},{12,16},{16,20},{20,24},{24,28},{29,1},{... | collective-permute-start | bytes 786440 | tf_op jit(solution)/shard_map/ppermute | solution.py:24
  133.7 8.8 %collective-permute-start.2 = (bf16[4,256,128]{2,0,1:T(4,128)(2,1)S(1)}, bf16[4,256,128]{2,0,1:T(4,128)(2,1)S(1)}, u32[]{:S(2)}, u32[]{:S(2)}) collective-permute-start(bf16[4,256,128]{2,0,1:T(4,128)(2,1)S(1)} %get-tuple-element.12), channel_id=1, source_target_pairs={{4,0},{8,4},{12,8},{16,12},{20,16},{24,20},{28,24},{0,28},{5,1},{9... | collective-permute-start | bytes 786440 | tf_op jit(solution)/shard_map/ppermute | solution.py:24
  143.6 65.9 %all-gather.11.cloned.1.call-start = ((), (), s32[]{:S(2)}) async-start(), calls=%async_computation.9 | async-start | bytes 2621440 | tf_op jit(solution)/shard_map/all_gather | solution.py:61
  165.5 149.8 %reduce-scatter.7.cloned.1.call-start = ((), (), s32[]{:S(2)}) async-start(), calls=%async_computation.5 | async-start | bytes 655360 | tf_op jit(solution)/shard_map/reduce_scatter | solution.py:70
  209.6 47.4 %collective-permute-start.5 = (bf16[8,1,4,256,128]{4,3,2,1,0:T(8,128)(2,1)}, bf16[8,1,4,256,128]{4,3,2,1,0:T(8,128)(2,1)}, u32[]{:S(2)}, u32[]{:S(2)}) collective-permute-start(bf16[8,1,4,256,128]{4,3,2,1,0:T(8,128)(2,1)} %bitcast.132), channel_id=1, source_target_pairs={{4,0},{8,4},{12,8},{16,12},{20,16},{24,20},{28,24},{0,28},{5,1},{9... | collective-permute-start | bytes 6291464 | tf_op jit(solution)/shard_map/ppermute | solution.py:16
  211.2 47.5 %collective-permute-start.4 = (bf16[8,1,4,256,128]{4,3,2,1,0:T(8,128)(2,1)}, bf16[8,1,4,256,128]{4,3,2,1,0:T(8,128)(2,1)}, u32[]{:S(2)}, u32[]{:S(2)}) collective-permute-start(bf16[8,1,4,256,128]{4,3,2,1,0:T(8,128)(2,1)} %bitcast.133), channel_id=1, source_target_pairs={{0,4},{4,8},{8,12},{12,16},{16,20},{20,24},{24,28},{28,0},{1,5},{5... | collective-permute-start | bytes 6291464 | tf_op jit(solution)/shard_map/ppermute | solution.py:13
  265.2 7.0 %copy-start.5 = (bf16[8,12]{0,1:T(8,128)(2,1)S(1)}, bf16[8,12]{0,1:T(8,128)(2,1)}, u32[]{:S(2)}) copy-start(bf16[8,12]{0,1:T(8,128)(2,1)} %copy-done.4) | copy-start | bytes 580
  265.2 7.0 %copy-start.9 = (pred[12]{0:T(512)(128)(4,1)S(1)}, pred[12]{0:T(512)(128)(4,1)}, u32[]{:S(2)}) copy-start(pred[12]{0:T(512)(128)(4,1)} %copy-done.8) | copy-start | bytes 40
  285.9 8.9 %collective-permute-start.7 = (bf16[4,256,128]{2,0,1:T(4,128)(2,1)S(1)}, bf16[4,256,128]{2,0,1:T(4,128)(2,1)S(1)}, u32[]{:S(2)}, u32[]{:S(2)}) collective-permute-start(bf16[4,256,128]{2,0,1:T(4,128)(2,1)S(1)} %get-tuple-element.11), channel_id=1, source_target_pairs={{28,0},{0,4},{4,8},{8,12},{12,16},{16,20},{20,24},{24,28},{29,1},{... | collective-permute-start | bytes 786440 | tf_op jit(solution)/shard_map/ppermute | solution.py:24
  285.9 8.8 %collective-permute-start.6 = (bf16[4,256,128]{2,0,1:T(4,128)(2,1)S(1)}, bf16[4,256,128]{2,0,1:T(4,128)(2,1)S(1)}, u32[]{:S(2)}, u32[]{:S(2)}) collective-permute-start(bf16[4,256,128]{2,0,1:T(4,128)(2,1)S(1)} %get-tuple-element.10), channel_id=1, source_target_pairs={{4,0},{8,4},{12,8},{16,12},{20,16},{24,20},{28,24},{0,28},{5,1},{9... | collective-permute-start | bytes 786440 | tf_op jit(solution)/shard_map/ppermute | solution.py:24
  295.9 65.7 %all-gather.13.cloned.1.call-start = ((), (), s32[]{:S(2)}) async-start(), calls=%async_computation.10 | async-start | bytes 2621440 | tf_op jit(solution)/shard_map/all_gather | solution.py:61
  317.4 149.8 %reduce-scatter.9.cloned.1.call-start = ((), (), s32[]{:S(2)}) async-start(), calls=%async_computation.6 | async-start | bytes 655360 | tf_op jit(solution)/shard_map/reduce_scatter | solution.py:70
  361.5 47.4 %collective-permute-start.9 = (bf16[8,1,4,256,128]{4,3,2,1,0:T(8,128)(2,1)}, bf16[8,1,4,256,128]{4,3,2,1,0:T(8,128)(2,1)}, u32[]{:S(2)}, u32[]{:S(2)}) collective-permute-start(bf16[8,1,4,256,128]{4,3,2,1,0:T(8,128)(2,1)} %bitcast.135), channel_id=1, source_target_pairs={{4,0},{8,4},{12,8},{16,12},{20,16},{24,20},{28,24},{0,28},{5,1},{9... | collective-permute-start | bytes 6291464 | tf_op jit(solution)/shard_map/ppermute | solution.py:16
  363.2 47.5 %collective-permute-start.8 = (bf16[8,1,4,256,128]{4,3,2,1,0:T(8,128)(2,1)}, bf16[8,1,4,256,128]{4,3,2,1,0:T(8,128)(2,1)}, u32[]{:S(2)}, u32[]{:S(2)}) collective-permute-start(bf16[8,1,4,256,128]{4,3,2,1,0:T(8,128)(2,1)} %bitcast.136), channel_id=1, source_target_pairs={{0,4},{4,8},{8,12},{12,16},{16,20},{20,24},{24,28},{28,0},{1,5},{5... | collective-permute-start | bytes 6291464 | tf_op jit(solution)/shard_map/ppermute | solution.py:13
  417.2 7.0 %copy-start.6 = (bf16[8,12]{0,1:T(8,128)(2,1)S(1)}, bf16[8,12]{0,1:T(8,128)(2,1)}, u32[]{:S(2)}) copy-start(bf16[8,12]{0,1:T(8,128)(2,1)} %copy-done.4) | copy-start | bytes 580
  417.2 7.0 %copy-start.10 = (pred[12]{0:T(512)(128)(4,1)S(1)}, pred[12]{0:T(512)(128)(4,1)}, u32[]{:S(2)}) copy-start(pred[12]{0:T(512)(128)(4,1)} %copy-done.8) | copy-start | bytes 40
  437.9 8.9 %collective-permute-start.11 = (bf16[4,256,128]{2,0,1:T(4,128)(2,1)S(1)}, bf16[4,256,128]{2,0,1:T(4,128)(2,1)S(1)}, u32[]{:S(2)}, u32[]{:S(2)}) collective-permute-start(bf16[4,256,128]{2,0,1:T(4,128)(2,1)S(1)} %get-tuple-element.9), channel_id=1, source_target_pairs={{28,0},{0,4},{4,8},{8,12},{12,16},{16,20},{20,24},{24,28},{29,1},{... | collective-permute-start | bytes 786440 | tf_op jit(solution)/shard_map/ppermute | solution.py:24
  437.9 8.8 %collective-permute-start.10 = (bf16[4,256,128]{2,0,1:T(4,128)(2,1)S(1)}, bf16[4,256,128]{2,0,1:T(4,128)(2,1)S(1)}, u32[]{:S(2)}, u32[]{:S(2)}) collective-permute-start(bf16[4,256,128]{2,0,1:T(4,128)(2,1)S(1)} %get-tuple-element.8), channel_id=1, source_target_pairs={{4,0},{8,4},{12,8},{16,12},{20,16},{24,20},{28,24},{0,28},{5,1},{9... | collective-permute-start | bytes 786440 | tf_op jit(solution)/shard_map/ppermute | solution.py:24
  447.8 65.5 %all-gather.15.cloned.1.call-start = ((), (), s32[]{:S(2)}) async-start(), calls=%async_computation.11 | async-start | bytes 2621440 | tf_op jit(solution)/shard_map/all_gather | solution.py:61
  469.3 149.6 %reduce-scatter.11.cloned.1.call-start = ((), (), s32[]{:S(2)}) async-start(), calls=%async_computation.7 | async-start | bytes 655360 | tf_op jit(solution)/shard_map/reduce_scatter | solution.py:70
  513.4 47.5 %collective-permute-start.13 = (bf16[8,1,4,256,128]{4,3,2,1,0:T(8,128)(2,1)}, bf16[8,1,4,256,128]{4,3,2,1,0:T(8,128)(2,1)}, u32[]{:S(2)}, u32[]{:S(2)}) collective-permute-start(bf16[8,1,4,256,128]{4,3,2,1,0:T(8,128)(2,1)} %bitcast.129), channel_id=1, source_target_pairs={{4,0},{8,4},{12,8},{16,12},{20,16},{24,20},{28,24},{0,28},{5,1},{9... | collective-permute-start | bytes 6291464 | tf_op jit(solution)/shard_map/ppermute | solution.py:16
  515.0 47.5 %collective-permute-start.12 = (bf16[8,1,4,256,128]{4,3,2,1,0:T(8,128)(2,1)}, bf16[8,1,4,256,128]{4,3,2,1,0:T(8,128)(2,1)}, u32[]{:S(2)}, u32[]{:S(2)}) collective-permute-start(bf16[8,1,4,256,128]{4,3,2,1,0:T(8,128)(2,1)} %bitcast.130), channel_id=1, source_target_pairs={{0,4},{4,8},{8,12},{12,16},{16,20},{20,24},{24,28},{28,0},{1,5},{5... | collective-permute-start | bytes 6291464 | tf_op jit(solution)/shard_map/ppermute | solution.py:13
  589.7 8.9 %collective-permute-start.15 = (bf16[4,256,128]{2,0,1:T(4,128)(2,1)S(1)}, bf16[4,256,128]{2,0,1:T(4,128)(2,1)S(1)}, u32[]{:S(2)}, u32[]{:S(2)}) collective-permute-start(bf16[4,256,128]{2,0,1:T(4,128)(2,1)S(1)} %get-tuple-element.7), channel_id=1, source_target_pairs={{28,0},{0,4},{4,8},{8,12},{12,16},{16,20},{20,24},{24,28},{29,1},{... | collective-permute-start | bytes 786440 | tf_op jit(solution)/shard_map/ppermute | solution.py:24
  589.7 8.8 %collective-permute-start.14 = (bf16[4,256,128]{2,0,1:T(4,128)(2,1)S(1)}, bf16[4,256,128]{2,0,1:T(4,128)(2,1)S(1)}, u32[]{:S(2)}, u32[]{:S(2)}) collective-permute-start(bf16[4,256,128]{2,0,1:T(4,128)(2,1)S(1)} %get-tuple-element.6), channel_id=1, source_target_pairs={{4,0},{8,4},{12,8},{16,12},{20,16},{24,20},{28,24},{0,28},{5,1},{9... | collective-permute-start | bytes 786440 | tf_op jit(solution)/shard_map/ppermute | solution.py:24
Sparse Core Ops, SparseCore 0:
  8.9 48.3 all-gather.8
  143.8 19.5 reduce-scatter.4
  165.6 43.8 all-gather.10
  296.0 19.2 reduce-scatter.6
  317.6 43.9 all-gather.12
  448.0 19.2 reduce-scatter.8
  469.4 43.8 all-gather.14
  599.8 19.0 reduce-scatter.10
where the time goes:
time: 636 us; the launch traced here: 628 us
  waiting for transfers between devices  430 us (68%)
  matrix products  88.6 us (14%)
  local copies, waits for them, and re-layouts  47 us (7%)
  other arithmetic  30.2 us (5%)
  starting transfers between devices  18.3 us (3%)
  between operations  14.4 us (2%)
    all_gather x4, waiting for transfers between devices, on_device(): stacked = lax.all_gather(recent[:, None, None], 'cuts', axis=2, tiled=True)  180 us
    ppermute x4, waiting for transfers between devices, padded(): lax.ppermute(lax.slice_in_dim(block, 0, width, axis=dim), axis, backward)  139 us
    reduce_scatter x4, waiting for transfers between devices, on_device(): lax.psum_scatter(grouped[1] + from_above + from_below, 'cuts', scatter_di...  77.6 us
    dot_general x4, matrix products, near_field(): jnp.einsum('plij,lpjr->ir', lag_kernels, partner_hist, preferred_element_...  48.4 us
    dot_general x4, matrix products, near_field(): jnp.einsum('plij,plir->pjr', lag_kernels, own_hist, preferred_element_typ...  30.4 us
    gather x4, local copies, waits for them, and re-layouts, near_field(): partner_hist = jnp.take(window, pair_partner, axis=1)  27.9 us
    concatenate x4, other arithmetic, padded(): block = jnp.concatenate([low, block, high], axis=dim)  25.8 us
    ppermute x8, waiting for transfers between devices, shifted(): return lax.ppermute(block, axis, route)  24.9 us
  transfers between devices with their start and end apart: 24, of which 20 were waited for; matrix products, arithmetic and copies ran while one was open for 7% of the time, Pallas kernels for 0%

commit v1 on v0

v1 whole, which is shorter than its diff:
```python
import functools

import jax
import jax.numpy as jnp
from jax import lax
from jax.experimental import pallas as pl
from jax.experimental.pallas import tpu as pltpu
from jax.sharding import PartitionSpec as P


F32 = jnp.float32
BF16 = jnp.bfloat16
IN_VMEM = pl.BlockSpec(memory_space=pltpu.VMEM)
IN_SMEM = pl.BlockSpec(memory_space=pltpu.SMEM)


def dot_nn(a, b):
    return lax.dot_general(a, b, (((1,), (0,)), ((), ())), preferred_element_type=F32)


def dot_nt(a, b):
    return lax.dot_general(a, b, (((1,), (1,)), ((), ())), preferred_element_type=F32)


def even_exchange(value):
    count = lax.axis_size("region")
    return lax.ppermute(value, "region", [(i, i ^ 1) for i in range(count)])


def odd_exchange(value):
    count = lax.axis_size("region")
    route = [(i, (i + 1) % count if i % 2 else (i - 1) % count) for i in range(count)]
    return lax.ppermute(value, "region", route)


def cut_exchange(value, j):
    count = lax.axis_size("cuts")
    return lax.ppermute(value, "cuts", [(i, i ^ j) for i in range(count)])


def cut_pieces(value):
    count = lax.axis_size("cuts")
    if count != 4:
        return [cut_exchange(value, j) for j in range(1, count)]
    inner = [(1, 2), (2, 1)]
    outward = [(1, 0), (2, 3)]
    first = cut_exchange(value, 1)
    across = lax.ppermute(value, "cuts", inner)
    far = lax.ppermute(across, "cuts", outward)
    passed = lax.ppermute(first, "cuts", inner)
    last = lax.ppermute(passed, "cuts", outward)
    return [first, passed + far, across + last]


def call(body, scalars, args, outs, scratch, flops, read, aliases=None, far=(), limit=8):
    return pl.pallas_call(
        body,
        out_shape=outs,
        in_specs=[IN_SMEM] * len(scalars)
        + [pl.BlockSpec(memory_space=pltpu.HBM) if i in far else IN_VMEM for i in range(len(args))],
        input_output_aliases={len(scalars) + i: o for i, o in (aliases or {}).items()},
        out_specs=jax.tree.map(lambda _: IN_VMEM, outs),
        scratch_shapes=scratch,
        compiler_params=pltpu.CompilerParams(vmem_limit_bytes=limit * 1024 * 1024),
        cost_estimate=pl.CostEstimate(
            flops=int(flops) // 1000, bytes_accessed=int(read) // 1000, transcendentals=0
        ),
    )(*scalars, *args)


def gated(kern, lag, last):
    return kern * jnp.where(lag <= last, 1.0, 0.0).astype(BF16)


def lag_chain(dot, block, kern, p, last, steps, add):
    lags = kern.shape[1]
    rows, panels = block.shape[-2:]

    def term(l):
        count = min(steps, l)
        x = block[l - count : l].reshape(count * rows, panels)
        return dot(x, gated(kern[p, l - 1], l, last) if l > 1 else kern[p, l - 1])

    full = None
    for l in range(steps, lags + 1):
        y = term(l)
        full = y if full is None else full + y
    add(0, full)
    for l in range(1, steps):
        add(steps - l, term(l))


def turn_body(value, out):
    for i in range(value.shape[0]):
        out[i] = value[i].T


def enter_body(cuts, codes, history, turned, loc):
    turn_body(history, turned)

    @pl.when(pl.program_id(0) == 0)
    def _():
        odd_region = lax.rem(lax.axis_index("region"), 2)
        own_cut = lax.axis_index("cuts")
        for p in range(codes.shape[0]):
            shift = lax.div(codes[p], cuts) - 1
            side = jnp.where((shift == 1) == (odd_region == 0), 1, 2)
            side = jnp.where(shift == 0, 0, side)
            loc[p] = side * cuts + (lax.rem(codes[p], cuts) ^ own_cut)


def enter(codes, history, cuts):
    count, panels, rows = history.shape
    parts = 2 if count % 2 == 0 else 1
    return pl.pallas_call(
        functools.partial(enter_body, cuts),
        name="enter",
        grid=(parts,),
        in_specs=[
            IN_SMEM,
            pl.BlockSpec((count // parts, panels, rows), lambda i: (i, 0, 0)),
        ],
        out_specs=(pl.BlockSpec((count // parts, rows, panels), lambda i: (i, 0, 0)), IN_SMEM),
        out_shape=(
            jax.ShapeDtypeStruct((count, rows, panels), history.dtype),
            jax.ShapeDtypeStruct(codes.shape, codes.dtype),
        ),
        compiler_params=pltpu.CompilerParams(vmem_limit_bytes=8 * 1024 * 1024),
        cost_estimate=pl.CostEstimate(flops=0, bytes_accessed=4096, transcendentals=0),
    )(codes, history)


def history_back_body(
    steps, cuts, loc, used, hist, given, stored, incoming, own, even, odd, *sums
):
    rows = hist.shape[1]
    begun, (first, kern, done) = sums[:-3], sums[-3:]
    heaps = list(begun[::-1]) + [first]
    copies = [
        pltpu.make_async_copy(stored.at[p], kern.at[p], done.at[p])
        for p in range(kern.shape[0])
    ]
    for copy in copies:
        copy.start()
    for heap in heaps:
        heap[...] = jnp.zeros_like(heap)
    turn_body(given, incoming)

    def pair(p, carry):
        slot = loc[p]
        pltpu.make_async_copy(stored.at[p], kern.at[p], done.at[p]).wait()

        def add(low, y):
            for i in range(low, steps):
                heaps[i][slot] += y[(i - low) * rows : (i - low + 1) * rows]

        lag_chain(dot_nn, hist, kern, p, used[p], steps, add)
        return carry

    lax.fori_loop(0, kern.shape[0], pair, 0)
    own[...] = first[:cuts]
    even[...] = first[cuts : 2 * cuts].astype(BF16)
    odd[...] = first[2 * cuts :].astype(BF16)


def history_back(loc, used, hist, incident, kern, cuts):
    steps = incident.shape[0]
    pairs, lags, panels, _ = kern.shape
    rows = hist.shape[1]
    part = (cuts, rows, panels)
    heap = (3 * cuts, rows, panels)
    outs = (
        jax.ShapeDtypeStruct((steps, rows, panels), BF16),
        jax.ShapeDtypeStruct(part, F32),
        jax.ShapeDtypeStruct(part, BF16),
        jax.ShapeDtypeStruct(part, BF16),
    ) + (jax.ShapeDtypeStruct(heap, F32),) * (steps - 1)
    return call(
        functools.partial(history_back_body, steps, cuts),
        (loc, used),
        (hist, incident, kern),
        outs,
        [
            pltpu.VMEM(heap, F32),
            pltpu.VMEM(kern.shape, BF16),
            pltpu.SemaphoreType.DMA((pairs,)),
        ],
        2 * pairs * lags * steps * rows * panels * panels,
        2 * kern.size,
        far=(2,),
        limit=36,
    )


def history_front_body(slots, steps, has_before, loc, used, kern, *refs):
    blocks = refs[: len(slots)]
    refs = refs[len(slots) :]
    after, near = refs[-2:]
    rows = near.shape[2]
    for i, block in enumerate(blocks):
        near[i] = block[...]
    after[...] = refs[0][...] if has_before else jnp.zeros_like(after)

    def pair(p, carry):
        slot = loc[p]
        at = jnp.int32(-1)
        for i, s in enumerate(slots):
            at = jnp.where(slot == s, i, at)

        @pl.when(at >= 0)
        def _():
            def add(low, y):
                after[low:] += y.reshape(steps - low, rows, y.shape[-1])

            lag_chain(dot_nt, near.at[at], kern, p, used[p], steps, add)

        return carry

    lax.fori_loop(0, kern.shape[0], pair, 0)


def history_front(loc, used, kern, near, before, steps):
    pairs, lags, panels, _ = kern.shape
    slots = tuple(near)
    blocks = [near[s] for s in slots]
    rows = blocks[0].shape[1]
    share = len(slots) / 12
    return call(
        functools.partial(history_front_body, slots, steps, before is not None),
        (loc, used),
        [kern] + blocks + ([] if before is None else [before]),
        jax.ShapeDtypeStruct((steps, rows, panels), F32),
        [pltpu.VMEM((len(slots), lags, rows, panels), BF16)],
        share * 2 * pairs * lags * steps * rows * panels * panels,
        share * 2 * kern.size,
    )


def fill_near(near, own, side, even, odd):
    cuts = even.shape[0]
    near[0] = own[...]
    near[1:cuts] = side[...]
    near[cuts : 2 * cuts] = even[...]
    near[2 * cuts :] = odd[...]


def step_body(n, at, cuts, pairs, has_front, has_back, loc, *refs):
    refs = list(refs)
    ahead, mine, moved, incoming, inverse, kern = refs[:6]
    refs = refs[6:]
    total = ahead[at] + mine[...]
    for j in range(cuts - 1):
        total = total + moved[j].astype(F32)
    if has_front:
        near = refs[-1]
        fill_near(near, *refs[:4])
        refs = refs[4:]
        for p in range(pairs):
            total = total + dot_nt(near[loc[p]], kern[p, 0])
    excess = (incoming[n].astype(F32) - total).astype(BF16)
    density = dot_nt(excess, inverse[...]).astype(BF16)
    if has_back:
        _, out, out_own, out_even, out_odd, sums = refs[:6]
        out[...] = density
        for p in range(pairs):
            sums[loc[p]] += dot_nn(density, kern[p, 0])
        out_own[...] = sums[:cuts]
        out_even[...] = sums[cuts : 2 * cuts].astype(BF16)
        out_odd[...] = sums[2 * cuts :].astype(BF16)
    else:
        earlier, out = refs[: n], refs[n]
        for m in range(n):
            out[m] = earlier[m][...].astype(F32).T.astype(BF16)
        out[n] = density.astype(F32).T.astype(BF16)


def step_call(n, steps, loc, ahead, mine, moved, incoming, inverse, kern, near, begun, earlier):
    pairs, _, panels, _ = kern.shape
    cuts = moved.shape[0] + 1
    rows = mine.shape[0]
    has_front = near is not None
    has_back = n + 1 < steps
    part = (cuts, rows, panels)
    heap = (3 * cuts, rows, panels)
    ahead, at = ahead
    args = [ahead, mine, moved, incoming, inverse, kern]
    scratch = []
    aliases = {}
    if has_front:
        args += list(near)
    if has_back:
        args.append(begun)
        outs = (
            jax.ShapeDtypeStruct((rows, panels), BF16),
            jax.ShapeDtypeStruct(part, F32),
            jax.ShapeDtypeStruct(part, BF16),
            jax.ShapeDtypeStruct(part, BF16),
            jax.ShapeDtypeStruct(heap, F32),
        )
        aliases[len(args) - 1] = 4
    else:
        args += earlier
        outs = jax.ShapeDtypeStruct((steps, panels, rows), BF16)
    if has_front:
        scratch.append(pltpu.VMEM(heap, BF16))
    return call(
        functools.partial(step_body, n, at, cuts, pairs, has_front, has_back),
        (loc,),
        args,
        outs,
        scratch,
        4 * pairs * rows * panels * panels,
        2 * pairs * panels * panels,
        aliases=aliases,
    )


def later_body(back, front, loc, used, kern, *refs):
    refs = list(refs)
    has_near = bool(front)
    near = refs.pop() if has_near else None
    news = refs[len(refs) - len(back) - len(front) :]
    density = refs.pop(0) if back else None
    if has_near:
        fill_near(near, *refs[:4])
        refs = refs[4:]
    rows = [refs[len(back) + i][at] for i, (_, at) in enumerate(front)]
    for p in range(kern.shape[0]):
        slot = loc[p]
        last = used[p]
        for i, lag in enumerate(back):
            news[i][slot] += dot_nn(density[...], gated(kern[p, lag - 1], lag, last))
        for i, (lag, _) in enumerate(front):
            rows[i] += dot_nt(near[slot], gated(kern[p, lag - 1], lag, last))
    for i in range(len(front)):
        news[len(back) + i][0] = rows[i]


def later_call(loc, used, kern, cuts, density, back, near, front):
    pairs, _, panels, _ = kern.shape
    args = [kern]
    scratch = []
    if back:
        args.append(density)
    if front:
        args += list(near)
        scratch.append(pltpu.VMEM((3 * cuts,) + near[0].shape, BF16))
    args += [sums for _, sums in back] + [sums for _, (sums, _) in front]
    rows = (density if back else near[0]).shape[0]
    outs = [jax.ShapeDtypeStruct(sums.shape, F32) for _, sums in back]
    outs += [jax.ShapeDtypeStruct((1, rows, panels), F32) for _ in front]
    terms = len(back) + len(front)
    return call(
        functools.partial(
            later_body, [lag for lag, _ in back], [(lag, at) for lag, (_, at) in front]
        ),
        (loc, used),
        args,
        tuple(outs),
        scratch,
        2 * terms * pairs * rows * panels * panels,
        2 * terms * pairs * panels * panels,
        aliases={len(args) - len(back) - len(front) + i: i for i in range(len(back))},
    )


def gather_near(value):
    cuts = lax.axis_size("cuts")
    side = []
    for j in range(1, cuts):
        side.append(cut_exchange(value, j))
    side = jnp.stack(side)
    region = jnp.concatenate([value[None], side])
    odd = odd_exchange(region)
    even = even_exchange(region)
    return value, side, even, odd


def sum_parts(own, even, odd):
    cuts = lax.axis_size("cuts")
    odd = odd_exchange(odd)
    even = even_exchange(even)
    total = own + even.astype(F32) + odd.astype(F32)
    part = total[1:].astype(BF16)
    moved = []
    for j in range(1, cuts):
        moved.append(cut_exchange(part[j - 1], j))
    return total[0], jnp.stack(moved)


def every_step(history, incident, self_inverse, lag_kernels, pair_partner, pair_lags):
    steps = incident.shape[0]
    cuts = lax.axis_size("cuts")
    hist, loc = enter(pair_partner, history, cuts)
    incoming, own, even, odd, *begun = history_back(
        loc, pair_lags, hist, incident, lag_kernels, cuts
    )
    begun = dict(enumerate(begun, 1))
    mine, moved = sum_parts(own, even, odd)

    pieces = [hist] + cut_pieces(hist)
    evens, odds = [], []
    for piece in pieces:
        odds.append(odd_exchange(piece))
        evens.append(even_exchange(piece))
    sums = None
    for group in range(1, cuts + 1):
        near = {}
        if group < cuts:
            own_slots = range(group + 1) if group == 1 else [group]
            near.update({j: pieces[j] for j in own_slots})
        near[cuts + group - 1] = evens[group - 1]
        near[2 * cuts + group - 1] = odds[group - 1]
        sums = history_front(loc, pair_lags, lag_kernels, near, sums, steps)
    ahead = {n: (sums, steps - 1 - n) for n in range(steps)}

    near = None
    densities = []
    for n in range(steps - 1):
        density, own, even, odd, _ = step_call(
            n, steps, loc, ahead[n], mine, moved, incoming, self_inverse, lag_kernels,
            near, begun.get(n + 1), None,
        )
        densities.append(density)
        before, near = near, gather_near(density)
        mine, moved = sum_parts(own, even, odd)
        back = [(m - n, begun[m]) for m in range(n + 2, steps)]
        front = [(m - n + 1, ahead[m]) for m in range(n + 1, steps)] if n else []
        if back or front:
            news = later_call(loc, pair_lags, lag_kernels, cuts, density, back, before, front)
            for i, m in enumerate(range(n + 2, steps)):
                begun[m] = news[i]
            if n:
                for i, m in enumerate(range(n + 1, steps)):
                    ahead[m] = (news[len(back) + i], 0)
    return step_call(
        steps - 1, steps, loc, ahead[steps - 1], mine, moved, incoming, self_inverse,
        lag_kernels, near, None, densities,
    )


def solution(mesh):
    return jax.shard_map(
        every_step,
        mesh=mesh,
        in_specs=(
            P(None, ("region", "cuts"), None),
            P(None, ("region", "cuts"), None),
            P(("region", "cuts"), None),
            P(("region", "cuts"), None, None, None),
            P(("region", "cuts")),
            P(("region", "cuts")),
        ),
        out_specs=P(None, ("region", "cuts"), None),
        check_vma=False,
    )
```

time: 636 us -> 171 us (0.27); the launches traced: 628 us -> 171 us
  waiting for transfers between devices: 430 us -> 82.9 us
  matrix products: 88.6 us -> 0 us
  local copies, waits for them, and re-layouts: 47 us -> 3.41 us
  Pallas kernels: 0 us -> 34.5 us
  starting transfers between devices: 18.3 us -> 48.9 us
  other arithmetic: 30.2 us -> 0.98 us
  between operations: 14.4 us -> 0.46 us
    all_gather x4 -> x0, waiting for transfers between devices: 180 us -> none  [on_device(): stacked = lax.all_gather(recent[:, None, None], 'cuts', axis=2, tiled=True)]
    dot_general x16 -> x0, matrix products: 88.6 us -> none  [the longest x4 48.4 us: near_field(): jnp.einsum('plij,lpjr->ir', lag_kernels, partner_hist, preferred_element_...]
    ppermute x16 -> x48, waiting for transfers between devices: 171 us -> 82.9 us  [the longest x22 42.9 us: cut_exchange(): return lax.ppermute(value, 'cuts', [(i, i ^ j) for i in range(count)])]
    reduce_scatter x4 -> x0, waiting for transfers between devices: 77.6 us -> none  [on_device(): lax.psum_scatter(grouped[1] + from_above + from_below, 'cuts', scatter_di...]
    pallas_call x0 -> x13, Pallas kernels: none -> 34.5 us  [the longest x12 33 us: call(): pl.pallas_call(body, out_shape=outs, in_specs=[IN_SMEM] * len(scalars) +...]
    ppermute x16 -> x48, starting transfers between devices: 18 us -> 48.9 us  [the longest x22 31.8 us: cut_exchange(): return lax.ppermute(value, 'cuts', [(i, i ^ j) for i in range(count)])]
    concatenate x9 -> x3, other arithmetic: 28.5 us -> 0.11 us  [gather_near(): region = jnp.concatenate([value[None], side])]
    gather x4 -> x0, local copies, waits for them, and re-layouts: 27.9 us -> none  [near_field(): partner_hist = jnp.take(window, pair_partner, axis=1)]
  transfers between devices with their start and end apart: 24 -> 48, of which waited for: 20 -> 26; matrix products, arithmetic and copies ran while one was open for 7% -> 1% of each run, Pallas kernels for 0% -> 14%
where the time goes in v1:
time: 171 us
  waiting for transfers between devices  82.9 us (48%)
  starting transfers between devices  48.9 us (29%)
  Pallas kernels  34.5 us (20%)
  local copies, waits for them, and re-layouts  3.41 us (2%)
    ppermute x22, waiting for transfers between devices, cut_exchange(): return lax.ppermute(value, 'cuts', [(i, i ^ j) for i in range(count)])  42.9 us
    pallas_call x12, Pallas kernels, call(): pl.pallas_call(body, out_shape=outs, in_specs=[IN_SMEM] * len(scalars) +...  33 us
    ppermute x11, waiting for transfers between devices, odd_exchange(): return lax.ppermute(value, 'region', route)  32 us
    ppermute x22, starting transfers between devices, cut_exchange(): return lax.ppermute(value, 'cuts', [(i, i ^ j) for i in range(count)])  31.8 us
    ppermute x11, starting transfers between devices, odd_exchange(): return lax.ppermute(value, 'region', route)  9.59 us
    ppermute x1, waiting for transfers between devices, cut_pieces(): last = lax.ppermute(passed, 'cuts', outward)  7.89 us
  transfers between devices with their start and end apart: 48, of which 26 were waited for; matrix products, arithmetic and copies ran while one was open for 1% of the time, Pallas kernels for 14%

profile of v1, /device:TPU:0, one launch (start us, length us, event | category | flops | bytes accessed | tf_op | source)
XLA Modules:
  0.0 171.1 jit_solution(3825216307340603924)
XLA Ops:
  1.7 1.5 enter.1
  3.2 3.1 %collective-permute-start.1 = (bf16[8,128,256]{2,1,0:T(8,128)(2,1)S(1)}, bf16[8,128,256]{2,1,0:T(8,128)(2,1)S(1)}, u32[]{:S(2)}, u32[]{:S(2)}) collective-permute-start(bf16[8,128,256]{2,1,0:T(8,128)(2,1)S(1)} %get-tuple-element.32.refs_0_.hist), channel_id=1, source_target_pairs={{0,1},{1,0},{2,3},{3,2},{4,5},{5,4},{6,7},{7,6},{8,9},{9,8},{10,11... | collective-permute-start | bytes 1572872 | tf_op jit(solution)/shard_map/ppermute | solution.py:38
  7.9 9.8 %shard_map.68 = (bf16[4,128,256]{2,1,0:T(8,128)(2,1)S(1)}, f32[4,128,256]{2,1,0:T(8,128)S(1)}, bf16[4,128,256]{2,1,0:T(8,128)(2,1)S(1)}, bf16[4,128,256]{2,1,0:T...) custom-call(s32[12]{0:T(128)S(1)} %get-tuple-element.31.loc, ...), custom_call_target="tpu_custom_call" | custom-call | flops 6442450 | bytes 12582 | tf_op jit(solution)/shard_map/pallas_call | solution.py:56
  17.8 2.5 %collective-permute-start.14 = (bf16[4,128,256]{2,1,0:T(8,128)(2,1)S(1)}, bf16[4,128,256]{2,1,0:T(8,128)(2,1)S(1)}, u32[]{:S(2)}, u32[]{:S(2)}) collective-permute-start(bf16[4,128,256]{2,1,0:T(8,128)(2,1)S(1)} %get-tuple-element.35), channel_id=1, source_target_pairs={{0,28},{4,8},{8,4},{12,16},{16,12},{20,24},{24,20},{28,0},{1,29},{... | collective-permute-start | bytes 786440 | tf_op jit(solution)/shard_map/ppermute | solution.py:33
  21.8 4.9 %collective-permute-done.14 = bf16[4,128,256]{2,1,0:T(8,128)(2,1)S(1)} collective-permute-done((bf16[4,128,256]{2,1,0:T(8,128)(2,1)S(1)}, bf16[4,128,256]{2,1,0:T(8,128)(2,1)S(1)}, u32[]{:S(2)}, u32[]{:S(2)}) %collective-permute-start.14) | collective-permute-done | bytes 262176 | tf_op jit(solution)/shard_map/ppermute | solution.py:33
  27.6 3.4 %collective-permute-start.17 = (bf16[128,256]{1,0:T(8,128)(2,1)S(1)}, bf16[128,256]{1,0:T(8,128)(2,1)S(1)}, u32[]{:S(2)}, u32[]{:S(2)}) collective-permute-start(bf16[128,256]{1,0:T(8,128)(2,1)S(1)} %get-tuple-element.75), channel_id=1, source_target_pairs={{0,3},{1,2},{2,1},{3,0},{4,7},{5,6},{6,5},{7,4},{8,11},{9,10},{10,... | collective-permute-start | bytes 196616 | tf_op jit(solution)/shard_map/ppermute | solution.py:38
  31.0 1.3 collective-permute-start.6
  33.4 1.5 collective-permute-start.3
  35.2 17.8 %collective-permute-done.16 = bf16[128,256]{1,0:T(8,128)(2,1)S(1)} collective-permute-done((bf16[128,256]{1,0:T(8,128)(2,1)S(1)}, bf16[128,256]{1,0:T(8,128)(2,1)S(1)}, u32[]{:S(2)}, u32[]{:S(2)}) %collective-permute-start.16) | collective-permute-done | bytes 65568 | tf_op jit(solution)/shard_map/ppermute | solution.py:38
  54.1 2.0 %collective-permute-start.8 = (bf16[8,128,256]{2,1,0:T(8,128)(2,1)S(1)}, bf16[8,128,256]{2,1,0:T(8,128)(2,1)S(1)}, u32[]{:S(2)}, u32[]{:S(2)}) collective-permute-start(bf16[8,128,256]{2,1,0:T(8,128)(2,1)S(1)} %add.31.refs_0_), channel_id=1, source_target_pairs={{0,28},{4,8},{8,4},{12,16},{16,12},{20,24},{24,20},{28,0},{1,29},{... | collective-permute-start | bytes 1572872 | tf_op jit(solution)/shard_map/ppermute | solution.py:33
  56.1 7.9 %collective-permute-done.3 = bf16[8,128,256]{2,1,0:T(8,128)(2,1)S(1)} collective-permute-done((bf16[8,128,256]{2,1,0:T(8,128)(2,1)S(1)}, bf16[8,128,256]{2,1,0:T(8,128)(2,1)S(1)}, u32[]{:S(2)}, u32[]{:S(2)}) %collective-permute-start.3) | collective-permute-done | bytes 524320 | tf_op jit(solution)/shard_map/ppermute | solution.py:51
  64.1 2.5 %collective-permute-start.5 = (bf16[8,128,256]{2,1,0:T(8,128)(2,1)S(1)}, bf16[8,128,256]{2,1,0:T(8,128)(2,1)S(1)}, u32[]{:S(2)}, u32[]{:S(2)}) collective-permute-start(bf16[8,128,256]{2,1,0:T(8,128)(2,1)S(1)} %add.30.refs_0_), channel_id=1, source_target_pairs={{0,28},{4,8},{8,4},{12,16},{16,12},{20,24},{24,20},{28,0},{1,29},{... | collective-permute-start | bytes 1572872 | tf_op jit(solution)/shard_map/ppermute | solution.py:33
  66.7 1.5 collective-permute-done.10.refs_2_
  68.2 2.2 %shard_map.64.refs_3_ = f32[4,128,256]{2,1,0:T(8,128)S(1)} custom-call(s32[12]{0:T(128)S(1)} %get-tuple-element.31.loc, s32[12]{0:T(128)S(1)} %copy-done.4, bf16[12,8,256,256]{3,2,1,0:T(8,128)(2,1)S(1)} %copy-done, bf16[8,128,256]{2,1,0:T(8,128)(2,1)S(1)} %get-tuple-element.32.refs_0_.hist, bf16[8,128,256]{2,1,0:T(8,128)(2,1)S(1)} %collective-permute-done.1.refs_1_, ...), custom_call_target="tpu_custom_call" | custom-call | flops 2147483 | bytes 4194 | tf_op jit(solution)/shard_map/pallas_call | solution.py:56
  70.5 2.2 %shard_map.65.refs_3_ = f32[4,128,256]{2,1,0:T(8,128)S(1)} custom-call(s32[12]{0:T(128)S(1)} %get-tuple-element.31.loc, s32[12]{0:T(128)S(1)} %copy-done.4, bf16[12,8,256,256]{3,2,1,0:T(8,128)(2,1)S(1)} %copy-done, bf16[8,128,256]{2,1,0:T(8,128)(2,1)S(1)} %add.31.refs_0_, bf16[8,128,256]{2,1,0:T(8,128)(2,1)S(1)} %collective-permute-done.9.refs_1_, ...), custom_call_target="tpu_custom_call" | custom-call | flops 1610612 | bytes 3145 | tf_op jit(solution)/shard_map/pallas_call | solution.py:56
  72.6 6.7 %collective-permute-done.8.refs_2_ = bf16[8,128,256]{2,1,0:T(8,128)(2,1)S(1)} collective-permute-done((bf16[8,128,256]{2,1,0:T(8,128)(2,1)S(1)}, bf16[8,128,256]{2,1,0:T(8,128)(2,1)S(1)}, u32[]{:S(2)}, u32[]{:S(2)}) %collective-permute-start.8) | collective-permute-done | bytes 524320 | tf_op jit(solution)/shard_map/ppermute | solution.py:33
  79.4 4.8 %shard_map.66.refs_2_ = f32[4,128,256]{2,1,0:T(8,128)S(1)} custom-call(s32[12]{0:T(128)S(1)} %get-tuple-element.31.loc, s32[12]{0:T(128)S(1)} %copy-done.4, bf16[12,8,256,256]{3,2,1,0:T(8,128)(2,1)S(1)} %copy-done, bf16[8,128,256]{2,1,0:T(8,128)(2,1)S(1)} %add.30.refs_0_, bf16[8,128,256]{2,1,0:T(8,128)(2,1)S(1)} %collective-permute-done.7.refs_1_, ...), custom_call_target="tpu_custom_call" | custom-call | flops 1610612 | bytes 3145 | tf_op jit(solution)/shard_map/pallas_call | solution.py:56
  84.2 6.1 %collective-permute-done.5.refs_1_ = bf16[8,128,256]{2,1,0:T(8,128)(2,1)S(1)} collective-permute-done((bf16[8,128,256]{2,1,0:T(8,128)(2,1)S(1)}, bf16[8,128,256]{2,1,0:T(8,128)(2,1)S(1)}, u32[]{:S(2)}, u32[]{:S(2)}) %collective-permute-start.5) | collective-permute-done | bytes 524320 | tf_op jit(solution)/shard_map/ppermute | solution.py:33
  90.3 2.1 %shard_map.67.refs_0_.refs_6_.refs_7_ = f32[4,128,256]{2,1,0:T(8,128)S(1)} custom-call(s32[12]{0:T(128)S(1)} %get-tuple-element.31.loc, s32[12]{0:T(128)S(1)} %copy-done.4, bf16[12,8,256,256]{3,2,1,0:T(8,128)(2,1)S(1)} %copy-done, bf16[8,128,256]{2,1,0:T(8,128)(2,1)S(1)} %collective-permute-done.4.refs_0_, ...), custom_call_target="tpu_custom_call" | custom-call | flops 1073741 | bytes 2097 | tf_op jit(solution)/shard_map/pallas_call | solution.py:56
  93.7 1.5 collective-permute-start.25
  95.2 2.1 %collective-permute-start.24 = (bf16[128,256]{1,0:T(8,128)(2,1)S(1)}, bf16[128,256]{1,0:T(8,128)(2,1)S(1)}, u32[]{:S(2)}, u32[]{:S(2)}) collective-permute-start(bf16[128,256]{1,0:T(8,128)(2,1)S(1)} %get-tuple-element.41.refs_0_.refs_6_.refs_1_.refs_10_), channel_id=1, source_target_pairs={{0,2},{1,3},{2,0},{3,1},{4,6},{5,7},{6,4},{7,5},{8,10},{9,11},{10,... | collective-permute-start | bytes 196616 | tf_op jit(solution)/shard_map/ppermute | solution.py:38
  99.9 1.5 collective-permute-done.24
  102.3 1.6 collective-permute-start.26
  103.9 3.6 %collective-permute-done.19 = bf16[4,128,256]{2,1,0:T(8,128)(2,1)S(1)} collective-permute-done((bf16[4,128,256]{2,1,0:T(8,128)(2,1)S(1)}, bf16[4,128,256]{2,1,0:T(8,128)(2,1)S(1)}, u32[]{:S(2)}, u32[]{:S(2)}) %collective-permute-start.19) | collective-permute-done | bytes 262176 | tf_op jit(solution)/shard_map/ppermute | solution.py:33
  107.7 1.3 collective-permute-start.20
  109.0 2.8 %collective-permute-start.22 = (bf16[128,256]{1,0:T(8,128)(2,1)S(1)}, bf16[128,256]{1,0:T(8,128)(2,1)S(1)}, u32[]{:S(2)}, u32[]{:S(2)}) collective-permute-start(bf16[128,256]{1,0:T(8,128)(2,1)S(1)} %get-tuple-element.72), channel_id=1, source_target_pairs={{0,3},{1,2},{2,1},{3,0},{4,7},{5,6},{6,5},{7,4},{8,11},{9,10},{10,... | collective-permute-start | bytes 196616 | tf_op jit(solution)/shard_map/ppermute | solution.py:38
  112.0 3.7 %collective-permute-done.22 = bf16[128,256]{1,0:T(8,128)(2,1)S(1)} collective-permute-done((bf16[128,256]{1,0:T(8,128)(2,1)S(1)}, bf16[128,256]{1,0:T(8,128)(2,1)S(1)}, u32[]{:S(2)}, u32[]{:S(2)}) %collective-permute-start.22) | collective-permute-done | bytes 65568 | tf_op jit(solution)/shard_map/ppermute | solution.py:38
  115.7 2.0 %collective-permute-done.21 = bf16[128,256]{1,0:T(8,128)(2,1)S(1)} collective-permute-done((bf16[128,256]{1,0:T(8,128)(2,1)S(1)}, bf16[128,256]{1,0:T(8,128)(2,1)S(1)}, u32[]{:S(2)}, u32[]{:S(2)}) %collective-permute-start.21) | collective-permute-done | bytes 65568 | tf_op jit(solution)/shard_map/ppermute | solution.py:38
  117.7 2.1 %shard_map.71 = (bf16[128,256]{1,0:T(8,128)(2,1)S(1)}, f32[4,128,256]{2,1,0:T(8,128)S(1)}, bf16[4,128,256]{2,1,0:T(8,128)(2,1)S(1)}, bf16[4,128,256]{2,1,0:T(8,128)(2,1)S(1)}, f32[12,128,256]{2,1,0:T(8,128)S(1)}) custom-call(s32[12]{0:T(128)S(1)} %get-tuple-element.31.loc, ...), custom_call_target="tpu_custom_call", output_to_operand_aliasing={{4}: (11, {})} | custom-call | flops 402653 | bytes 1572 | tf_op jit(solution)/shard_map/pallas_call | solution.py:56
  119.8 2.2 %collective-permute-start.30 = (bf16[128,256]{1,0:T(8,128)(2,1)S(1)}, bf16[128,256]{1,0:T(8,128)(2,1)S(1)}, u32[]{:S(2)}, u32[]{:S(2)}) collective-permute-start(bf16[128,256]{1,0:T(8,128)(2,1)S(1)} %get-tuple-element.45.refs_0_.refs_6_.refs_11_), channel_id=1, source_target_pairs={{0,3},{1,2},{2,1},{3,0},{4,7},{5,6},{6,5},{7,4},{8,11},{9,10},{10,... | collective-permute-start | bytes 196616 | tf_op jit(solution)/shard_map/ppermute | solution.py:38
  122.0 2.2 %collective-permute-start.28 = (bf16[128,256]{1,0:T(8,128)(2,1)S(1)}, bf16[128,256]{1,0:T(8,128)(2,1)S(1)}, u32[]{:S(2)}, u32[]{:S(2)}) collective-permute-start(bf16[128,256]{1,0:T(8,128)(2,1)S(1)} %get-tuple-element.45.refs_0_.refs_6_.refs_11_), channel_id=1, source_target_pairs={{0,1},{1,0},{2,3},{3,2},{4,5},{5,4},{6,7},{7,6},{8,9},{9,8},{10,11... | collective-permute-start | bytes 196616 | tf_op jit(solution)/shard_map/ppermute | solution.py:38
  124.4 1.9 %shard_map.72 = (f32[12,128,256]{2,1,0:T(8,128)S(1)}, f32[1,128,256]{2,1,0:T(8,128)S(1)}, f32[1,128,256]{2,1,0:T(8,128)S(1)}) custom-call(s32[12]{0:T(128)S(1)} %get-tuple-element.31.loc, s32[12]{0:T(128)S(1)} %copy-done.4, bf16[12,8,256,256]{3,2,1,0:T(8,128)(2,1)S(1)} %copy-done, ...), custom_call_target="tpu_custom_call", output_to_operand_aliasing={{0}: (8, {})} | custom-call | flops 603979 | bytes 4718 | tf_op jit(solution)/shard_map/pallas_call | solution.py:56
  126.7 1.8 %collective-permute-done.29 = bf16[128,256]{1,0:T(8,128)(2,1)S(1)} collective-permute-done((bf16[128,256]{1,0:T(8,128)(2,1)S(1)}, bf16[128,256]{1,0:T(8,128)(2,1)S(1)}, u32[]{:S(2)}, u32[]{:S(2)}) %collective-permute-start.29) | collective-permute-done | bytes 65568 | tf_op jit(solution)/shard_map/ppermute | solution.py:38
  129.2 4.6 %collective-permute-done.34 = bf16[4,128,256]{2,1,0:T(8,128)(2,1)S(1)} collective-permute-done((bf16[4,128,256]{2,1,0:T(8,128)(2,1)S(1)}, bf16[4,128,256]{2,1,0:T(8,128)(2,1)S(1)}, u32[]{:S(2)}, u32[]{:S(2)}) %collective-permute-start.34) | collective-permute-done | bytes 262176 | tf_op jit(solution)/shard_map/ppermute | solution.py:33
  134.0 2.2 %collective-permute-start.37 = (bf16[128,256]{1,0:T(8,128)(2,1)S(1)}, bf16[128,256]{1,0:T(8,128)(2,1)S(1)}, u32[]{:S(2)}, u32[]{:S(2)}) collective-permute-start(bf16[128,256]{1,0:T(8,128)(2,1)S(1)} %get-tuple-element.69), channel_id=1, source_target_pairs={{0,3},{1,2},{2,1},{3,0},{4,7},{5,6},{6,5},{7,4},{8,11},{9,10},{10,... | collective-permute-start | bytes 196616 | tf_op jit(solution)/shard_map/ppermute | solution.py:38
  136.2 1.3 collective-permute-start.36
  138.3 2.3 %collective-permute-done.37 = bf16[128,256]{1,0:T(8,128)(2,1)S(1)} collective-permute-done((bf16[128,256]{1,0:T(8,128)(2,1)S(1)}, bf16[128,256]{1,0:T(8,128)(2,1)S(1)}, u32[]{:S(2)}, u32[]{:S(2)}) %collective-permute-start.37) | collective-permute-done | bytes 65568 | tf_op jit(solution)/shard_map/ppermute | solution.py:38
  140.6 2.7 %collective-permute-done.36 = bf16[128,256]{1,0:T(8,128)(2,1)S(1)} collective-permute-done((bf16[128,256]{1,0:T(8,128)(2,1)S(1)}, bf16[128,256]{1,0:T(8,128)(2,1)S(1)}, u32[]{:S(2)}, u32[]{:S(2)}) %collective-permute-start.36) | collective-permute-done | bytes 65568 | tf_op jit(solution)/shard_map/ppermute | solution.py:38
  143.3 2.1 %shard_map.74 = (bf16[128,256]{1,0:T(8,128)(2,1)S(1)}, f32[4,128,256]{2,1,0:T(8,128)S(1)}, bf16[4,128,256]{2,1,0:T(8,128)(2,1)S(1)}, bf16[4,128,256]{2,1,0:T(8,128)(2,1)S(1)}, f32[12,128,256]{2,1,0:T(8,128)S(1)}) custom-call(s32[12]{0:T(128)S(1)} %get-tuple-element.31.loc, ...), custom_call_target="tpu_custom_call", output_to_operand_aliasing={{4}: (11, {})} | custom-call | flops 402653 | bytes 1572 | tf_op jit(solution)/shard_map/pallas_call | solution.py:56
  145.5 2.0 %collective-permute-start.45 = (bf16[128,256]{1,0:T(8,128)(2,1)S(1)}, bf16[128,256]{1,0:T(8,128)(2,1)S(1)}, u32[]{:S(2)}, u32[]{:S(2)}) collective-permute-start(bf16[128,256]{1,0:T(8,128)(2,1)S(1)} %get-tuple-element.56.refs_6_.refs_12_), channel_id=1, source_target_pairs={{0,3},{1,2},{2,1},{3,0},{4,7},{5,6},{6,5},{7,4},{8,11},{9,10},{10,... | collective-permute-start | bytes 196616 | tf_op jit(solution)/shard_map/ppermute | solution.py:38
  147.5 2.5 %collective-permute-start.43 = (bf16[128,256]{1,0:T(8,128)(2,1)S(1)}, bf16[128,256]{1,0:T(8,128)(2,1)S(1)}, u32[]{:S(2)}, u32[]{:S(2)}) collective-permute-start(bf16[128,256]{1,0:T(8,128)(2,1)S(1)} %get-tuple-element.56.refs_6_.refs_12_), channel_id=1, source_target_pairs={{0,1},{1,0},{2,3},{3,2},{4,5},{5,4},{6,7},{7,6},{8,9},{9,8},{10,11... | collective-permute-start | bytes 196616 | tf_op jit(solution)/shard_map/ppermute | solution.py:38
  152.2 1.3 collective-permute-done.44
  154.9 4.5 %collective-permute-done.39 = bf16[4,128,256]{2,1,0:T(8,128)(2,1)S(1)} collective-permute-done((bf16[4,128,256]{2,1,0:T(8,128)(2,1)S(1)}, bf16[4,128,256]{2,1,0:T(8,128)(2,1)S(1)}, u32[]{:S(2)}, u32[]{:S(2)}) %collective-permute-start.39) | collective-permute-done | bytes 262176 | tf_op jit(solution)/shard_map/ppermute | solution.py:33
  159.6 2.0 %collective-permute-start.42 = (bf16[128,256]{1,0:T(8,128)(2,1)S(1)}, bf16[128,256]{1,0:T(8,128)(2,1)S(1)}, u32[]{:S(2)}, u32[]{:S(2)}) collective-permute-start(bf16[128,256]{1,0:T(8,128)(2,1)S(1)} %get-tuple-element.66), channel_id=1, source_target_pairs={{0,3},{1,2},{2,1},{3,0},{4,7},{5,6},{6,5},{7,4},{8,11},{9,10},{10,... | collective-permute-start | bytes 196616 | tf_op jit(solution)/shard_map/ppermute | solution.py:38
  161.6 1.5 collective-permute-start.41
  163.9 2.3 %collective-permute-done.42 = bf16[128,256]{1,0:T(8,128)(2,1)S(1)} collective-permute-done((bf16[128,256]{1,0:T(8,128)(2,1)S(1)}, bf16[128,256]{1,0:T(8,128)(2,1)S(1)}, u32[]{:S(2)}, u32[]{:S(2)}) %collective-permute-start.42) | collective-permute-done | bytes 65568 | tf_op jit(solution)/shard_map/ppermute | solution.py:38
  166.2 2.7 %collective-permute-done.41 = bf16[128,256]{1,0:T(8,128)(2,1)S(1)} collective-permute-done((bf16[128,256]{1,0:T(8,128)(2,1)S(1)}, bf16[128,256]{1,0:T(8,128)(2,1)S(1)}, u32[]{:S(2)}, u32[]{:S(2)}) %collective-permute-start.41) | collective-permute-done | bytes 65568 | tf_op jit(solution)/shard_map/ppermute | solution.py:38
  169.0 2.2 %shard_map.75 = bf16[4,256,128]{2,1,0:T(8,128)(2,1)} custom-call(s32[12]{0:T(128)S(1)} %get-tuple-element.31.loc, f32[1,128,256]{2,1,0:T(8,128)S(1)} %shard_map.73.refs_0_, f32[128,256]{1,0:T(8,128)S(1)} %slice_bitcast_fusion.refs_1_, bf16[3,128,256]{2,1,0:T(8,128)(2,1)S(1)} %pad_maximum_fusion.8.refs_2_, ...), custom_call_target="tpu_custom_call" | custom-call | flops 402653 | bytes 1572 | tf_op jit(solution)/shard_map/pallas_call | solution.py:56
  (97 shorter events, 20.1 us)
Async XLA Ops:
  3.2 17.9 %collective-permute-start.1 = (bf16[8,128,256]{2,1,0:T(8,128)(2,1)S(1)}, bf16[8,128,256]{2,1,0:T(8,128)(2,1)S(1)}, u32[]{:S(2)}, u32[]{:S(2)}) collective-permute-start(bf16[8,128,256]{2,1,0:T(8,128)(2,1)S(1)} %get-tuple-element.32.refs_0_.hist), channel_id=1, source_target_pairs={{0,1},{1,0},{2,3},{3,2},{4,5},{5,4},{6,7},{7,6},{8,9},{9,8},{10,11... | collective-permute-start | bytes 1572872 | tf_op jit(solution)/shard_map/ppermute | solution.py:38
  17.8 4.0 %collective-permute-start.13 = (bf16[4,128,256]{2,1,0:T(8,128)(2,1)S(1)}, bf16[4,128,256]{2,1,0:T(8,128)(2,1)S(1)}, u32[]{:S(2)}, u32[]{:S(2)}) collective-permute-start(bf16[4,128,256]{2,1,0:T(8,128)(2,1)S(1)} %get-tuple-element.34), channel_id=1, source_target_pairs={{0,4},{4,0},{8,12},{12,8},{16,20},{20,16},{24,28},{28,24},{1,5},{5... | collective-permute-start | bytes 786440 | tf_op jit(solution)/shard_map/ppermute | solution.py:27
  17.8 8.9 %collective-permute-start.14 = (bf16[4,128,256]{2,1,0:T(8,128)(2,1)S(1)}, bf16[4,128,256]{2,1,0:T(8,128)(2,1)S(1)}, u32[]{:S(2)}, u32[]{:S(2)}) collective-permute-start(bf16[4,128,256]{2,1,0:T(8,128)(2,1)S(1)} %get-tuple-element.35), channel_id=1, source_target_pairs={{0,28},{4,8},{8,4},{12,16},{16,12},{20,24},{24,20},{28,0},{1,29},{... | collective-permute-start | bytes 786440 | tf_op jit(solution)/shard_map/ppermute | solution.py:33
  20.4 10.6 %collective-permute-start = (bf16[8,128,256]{2,1,0:T(8,128)(2,1)S(1)}, bf16[8,128,256]{2,1,0:T(8,128)(2,1)S(1)}, u32[]{:S(2)}, u32[]{:S(2)}) collective-permute-start(bf16[8,128,256]{2,1,0:T(8,128)(2,1)S(1)} %get-tuple-element.32.refs_0_.hist), channel_id=1, source_target_pairs={{1,2},{2,1},{5,6},{6,5},{9,10},{10,9},{13,14},{14,13},{17,18},{18,... | collective-permute-start | bytes 1572872 | tf_op jit(solution)/shard_map/ppermute | solution.py:48
  21.1 12.3 %collective-permute-start.2 = (bf16[8,128,256]{2,1,0:T(8,128)(2,1)S(1)}, bf16[8,128,256]{2,1,0:T(8,128)(2,1)S(1)}, u32[]{:S(2)}, u32[]{:S(2)}) collective-permute-start(bf16[8,128,256]{2,1,0:T(8,128)(2,1)S(1)} %collective-permute-done.1.refs_1_), channel_id=1, source_target_pairs={{1,2},{2,1},{5,6},{6,5},{9,10},{10,9},{13,14},{14,13},{17,18},{18,... | collective-permute-start | bytes 1572872 | tf_op jit(solution)/shard_map/ppermute | solution.py:50
  26.9 5.4 %collective-permute-start.15 = (bf16[128,256]{1,0:T(8,128)(2,1)S(1)}, bf16[128,256]{1,0:T(8,128)(2,1)S(1)}, u32[]{:S(2)}, u32[]{:S(2)}) collective-permute-start(bf16[128,256]{1,0:T(8,128)(2,1)S(1)} %get-tuple-element.74), channel_id=1, source_target_pairs={{0,1},{1,0},{2,3},{3,2},{4,5},{5,4},{6,7},{7,6},{8,9},{9,8},{10,11... | collective-permute-start | bytes 196616 | tf_op jit(solution)/shard_map/ppermute | solution.py:38
  27.6 7.6 %collective-permute-start.17 = (bf16[128,256]{1,0:T(8,128)(2,1)S(1)}, bf16[128,256]{1,0:T(8,128)(2,1)S(1)}, u32[]{:S(2)}, u32[]{:S(2)}) collective-permute-start(bf16[128,256]{1,0:T(8,128)(2,1)S(1)} %get-tuple-element.75), channel_id=1, source_target_pairs={{0,3},{1,2},{2,1},{3,0},{4,7},{5,6},{6,5},{7,4},{8,11},{9,10},{10,... | collective-permute-start | bytes 196616 | tf_op jit(solution)/shard_map/ppermute | solution.py:38
  31.0 22.0 %collective-permute-start.16 = (bf16[128,256]{1,0:T(8,128)(2,1)S(1)}, bf16[128,256]{1,0:T(8,128)(2,1)S(1)}, u32[]{:S(2)}, u32[]{:S(2)}) collective-permute-start(bf16[128,256]{1,0:T(8,128)(2,1)S(1)} %get-tuple-element.76), channel_id=1, source_target_pairs={{0,2},{1,3},{2,0},{3,1},{4,6},{5,7},{6,4},{7,5},{8,10},{9,11},{10,... | collective-permute-start | bytes 196616 | tf_op jit(solution)/shard_map/ppermute | solution.py:38
  31.0 22.4 %collective-permute-start.6 = (bf16[8,128,256]{2,1,0:T(8,128)(2,1)S(1)}, bf16[8,128,256]{2,1,0:T(8,128)(2,1)S(1)}, u32[]{:S(2)}, u32[]{:S(2)}) collective-permute-start(bf16[8,128,256]{2,1,0:T(8,128)(2,1)S(1)} %collective-permute-done), channel_id=1, source_target_pairs={{1,0},{2,3},{5,4},{6,7},{9,8},{10,11},{13,12},{14,15},{17,16},{18,... | collective-permute-start | bytes 1572872 | tf_op jit(solution)/shard_map/ppermute | solution.py:49
  32.3 21.8 %collective-permute-start.12 = (bf16[8,128,256]{2,1,0:T(8,128)(2,1)S(1)}, bf16[8,128,256]{2,1,0:T(8,128)(2,1)S(1)}, u32[]{:S(2)}, u32[]{:S(2)}) collective-permute-start(bf16[8,128,256]{2,1,0:T(8,128)(2,1)S(1)} %get-tuple-element.32.refs_0_.hist), channel_id=1, source_target_pairs={{0,28},{4,8},{8,4},{12,16},{16,12},{20,24},{24,20},{28,0},{1,29},{... | collective-permute-start | bytes 1572872 | tf_op jit(solution)/shard_map/ppermute | solution.py:33
  33.4 30.6 %collective-permute-start.3 = (bf16[8,128,256]{2,1,0:T(8,128)(2,1)S(1)}, bf16[8,128,256]{2,1,0:T(8,128)(2,1)S(1)}, u32[]{:S(2)}, u32[]{:S(2)}) collective-permute-start(bf16[8,128,256]{2,1,0:T(8,128)(2,1)S(1)} %collective-permute-done.2), channel_id=1, source_target_pairs={{1,0},{2,3},{5,4},{6,7},{9,8},{10,11},{13,12},{14,15},{17,16},{18,... | collective-permute-start | bytes 1572872 | tf_op jit(solution)/shard_map/ppermute | solution.py:51
  35.2 28.9 %collective-permute-start.11 = (bf16[8,128,256]{2,1,0:T(8,128)(2,1)S(1)}, bf16[8,128,256]{2,1,0:T(8,128)(2,1)S(1)}, u32[]{:S(2)}, u32[]{:S(2)}) collective-permute-start(bf16[8,128,256]{2,1,0:T(8,128)(2,1)S(1)} %get-tuple-element.32.refs_0_.hist), channel_id=1, source_target_pairs={{0,4},{4,0},{8,12},{12,8},{16,20},{20,16},{24,28},{28,24},{1,5},{5... | collective-permute-start | bytes 1572872 | tf_op jit(solution)/shard_map/ppermute | solution.py:27
  53.0 15.1 %collective-permute-start.10 = (bf16[8,128,256]{2,1,0:T(8,128)(2,1)S(1)}, bf16[8,128,256]{2,1,0:T(8,128)(2,1)S(1)}, u32[]{:S(2)}, u32[]{:S(2)}) collective-permute-start(bf16[8,128,256]{2,1,0:T(8,128)(2,1)S(1)} %collective-permute-done.1.refs_1_), channel_id=1, source_target_pairs={{0,28},{4,8},{8,4},{12,16},{16,12},{20,24},{24,20},{28,0},{1,29},{... | collective-permute-start | bytes 1572872 | tf_op jit(solution)/shard_map/ppermute | solution.py:33
  53.4 17.0 %collective-permute-start.9 = (bf16[8,128,256]{2,1,0:T(8,128)(2,1)S(1)}, bf16[8,128,256]{2,1,0:T(8,128)(2,1)S(1)}, u32[]{:S(2)}, u32[]{:S(2)}) collective-permute-start(bf16[8,128,256]{2,1,0:T(8,128)(2,1)S(1)} %collective-permute-done.1.refs_1_), channel_id=1, source_target_pairs={{0,4},{4,0},{8,12},{12,8},{16,20},{20,16},{24,28},{28,24},{1,5},{5... | collective-permute-start | bytes 1572872 | tf_op jit(solution)/shard_map/ppermute | solution.py:27
  54.1 25.3 %collective-permute-start.8 = (bf16[8,128,256]{2,1,0:T(8,128)(2,1)S(1)}, bf16[8,128,256]{2,1,0:T(8,128)(2,1)S(1)}, u32[]{:S(2)}, u32[]{:S(2)}) collective-permute-start(bf16[8,128,256]{2,1,0:T(8,128)(2,1)S(1)} %add.31.refs_0_), channel_id=1, source_target_pairs={{0,28},{4,8},{8,4},{12,16},{16,12},{20,24},{24,20},{28,0},{1,29},{... | collective-permute-start | bytes 1572872 | tf_op jit(solution)/shard_map/ppermute | solution.py:33
  64.0 15.4 %collective-permute-start.7 = (bf16[8,128,256]{2,1,0:T(8,128)(2,1)S(1)}, bf16[8,128,256]{2,1,0:T(8,128)(2,1)S(1)}, u32[]{:S(2)}, u32[]{:S(2)}) collective-permute-start(bf16[8,128,256]{2,1,0:T(8,128)(2,1)S(1)} %add.31.refs_0_), channel_id=1, source_target_pairs={{0,4},{4,0},{8,12},{12,8},{16,20},{20,16},{24,28},{28,24},{1,5},{5... | collective-permute-start | bytes 1572872 | tf_op jit(solution)/shard_map/ppermute | solution.py:27
  64.1 26.2 %collective-permute-start.5 = (bf16[8,128,256]{2,1,0:T(8,128)(2,1)S(1)}, bf16[8,128,256]{2,1,0:T(8,128)(2,1)S(1)}, u32[]{:S(2)}, u32[]{:S(2)}) collective-permute-start(bf16[8,128,256]{2,1,0:T(8,128)(2,1)S(1)} %add.30.refs_0_), channel_id=1, source_target_pairs={{0,28},{4,8},{8,4},{12,16},{16,12},{20,24},{24,20},{28,0},{1,29},{... | collective-permute-start | bytes 1572872 | tf_op jit(solution)/shard_map/ppermute | solution.py:33
  68.1 22.2 %collective-permute-start.4 = (bf16[8,128,256]{2,1,0:T(8,128)(2,1)S(1)}, bf16[8,128,256]{2,1,0:T(8,128)(2,1)S(1)}, u32[]{:S(2)}, u32[]{:S(2)}) collective-permute-start(bf16[8,128,256]{2,1,0:T(8,128)(2,1)S(1)} %add.30.refs_0_), channel_id=1, source_target_pairs={{0,4},{4,0},{8,12},{12,8},{16,20},{20,16},{24,28},{28,24},{1,5},{5... | collective-permute-start | bytes 1572872 | tf_op jit(solution)/shard_map/ppermute | solution.py:27
  93.7 6.2 %collective-permute-start.25 = (bf16[128,256]{1,0:T(8,128)(2,1)S(1)}, bf16[128,256]{1,0:T(8,128)(2,1)S(1)}, u32[]{:S(2)}, u32[]{:S(2)}) collective-permute-start(bf16[128,256]{1,0:T(8,128)(2,1)S(1)} %get-tuple-element.41.refs_0_.refs_6_.refs_1_.refs_10_), channel_id=1, source_target_pairs={{0,3},{1,2},{2,1},{3,0},{4,7},{5,6},{6,5},{7,4},{8,11},{9,10},{10,... | collective-permute-start | bytes 196616 | tf_op jit(solution)/shard_map/ppermute | solution.py:38
  95.2 6.3 %collective-permute-start.24 = (bf16[128,256]{1,0:T(8,128)(2,1)S(1)}, bf16[128,256]{1,0:T(8,128)(2,1)S(1)}, u32[]{:S(2)}, u32[]{:S(2)}) collective-permute-start(bf16[128,256]{1,0:T(8,128)(2,1)S(1)} %get-tuple-element.41.refs_0_.refs_6_.refs_1_.refs_10_), channel_id=1, source_target_pairs={{0,2},{1,3},{2,0},{3,1},{4,6},{5,7},{6,4},{7,5},{8,10},{9,11},{10,... | collective-permute-start | bytes 196616 | tf_op jit(solution)/shard_map/ppermute | solution.py:38
  97.3 4.9 %collective-permute-start.23 = (bf16[128,256]{1,0:T(8,128)(2,1)S(1)}, bf16[128,256]{1,0:T(8,128)(2,1)S(1)}, u32[]{:S(2)}, u32[]{:S(2)}) collective-permute-start(bf16[128,256]{1,0:T(8,128)(2,1)S(1)} %get-tuple-element.41.refs_0_.refs_6_.refs_1_.refs_10_), channel_id=1, source_target_pairs={{0,1},{1,0},{2,3},{3,2},{4,5},{5,4},{6,7},{7,6},{8,9},{9,8},{10,11... | collective-permute-start | bytes 196616 | tf_op jit(solution)/shard_map/ppermute | solution.py:38
  98.1 5.8 %collective-permute-start.18 = (bf16[4,128,256]{2,1,0:T(8,128)(2,1)S(1)}, bf16[4,128,256]{2,1,0:T(8,128)(2,1)S(1)}, u32[]{:S(2)}, u32[]{:S(2)}) collective-permute-start(bf16[4,128,256]{2,1,0:T(8,128)(2,1)S(1)} %get-tuple-element.39), channel_id=1, source_target_pairs={{0,4},{4,0},{8,12},{12,8},{16,20},{20,16},{24,28},{28,24},{1,5},{5... | collective-permute-start | bytes 786440 | tf_op jit(solution)/shard_map/ppermute | solution.py:27
  98.1 9.4 %collective-permute-start.19 = (bf16[4,128,256]{2,1,0:T(8,128)(2,1)S(1)}, bf16[4,128,256]{2,1,0:T(8,128)(2,1)S(1)}, u32[]{:S(2)}, u32[]{:S(2)}) collective-permute-start(bf16[4,128,256]{2,1,0:T(8,128)(2,1)S(1)} %get-tuple-element.40), channel_id=1, source_target_pairs={{0,28},{4,8},{8,4},{12,16},{16,12},{20,24},{24,20},{28,0},{1,29},{... | collective-permute-start | bytes 786440 | tf_op jit(solution)/shard_map/ppermute | solution.py:33
  102.2 15.5 %collective-permute-start.27 = (bf16[4,128,256]{2,1,0:T(8,128)(2,1)S(1)}, bf16[4,128,256]{2,1,0:T(8,128)(2,1)S(1)}, u32[]{:S(2)}, u32[]{:S(2)}) collective-permute-start(bf16[4,128,256]{2,1,0:T(8,128)(2,1)S(1)} %pad_maximum_fusion), channel_id=1, source_target_pairs={{0,28},{4,8},{8,4},{12,16},{16,12},{20,24},{24,20},{28,0},{1,29},{... | collective-permute-start | bytes 786440 | tf_op jit(solution)/shard_map/ppermute | solution.py:33
  102.3 15.4 %collective-permute-start.26 = (bf16[4,128,256]{2,1,0:T(8,128)(2,1)S(1)}, bf16[4,128,256]{2,1,0:T(8,128)(2,1)S(1)}, u32[]{:S(2)}, u32[]{:S(2)}) collective-permute-start(bf16[4,128,256]{2,1,0:T(8,128)(2,1)S(1)} %pad_maximum_fusion), channel_id=1, source_target_pairs={{0,4},{4,0},{8,12},{12,8},{16,20},{20,16},{24,28},{28,24},{1,5},{5... | collective-permute-start | bytes 786440 | tf_op jit(solution)/shard_map/ppermute | solution.py:27
  107.7 4.3 %collective-permute-start.20 = (bf16[128,256]{1,0:T(8,128)(2,1)S(1)}, bf16[128,256]{1,0:T(8,128)(2,1)S(1)}, u32[]{:S(2)}, u32[]{:S(2)}) collective-permute-start(bf16[128,256]{1,0:T(8,128)(2,1)S(1)} %get-tuple-element.71), channel_id=1, source_target_pairs={{0,1},{1,0},{2,3},{3,2},{4,5},{5,4},{6,7},{7,6},{8,9},{9,8},{10,11... | collective-permute-start | bytes 196616 | tf_op jit(solution)/shard_map/ppermute | solution.py:38
  109.0 6.7 %collective-permute-start.22 = (bf16[128,256]{1,0:T(8,128)(2,1)S(1)}, bf16[128,256]{1,0:T(8,128)(2,1)S(1)}, u32[]{:S(2)}, u32[]{:S(2)}) collective-permute-start(bf16[128,256]{1,0:T(8,128)(2,1)S(1)} %get-tuple-element.72), channel_id=1, source_target_pairs={{0,3},{1,2},{2,1},{3,0},{4,7},{5,6},{6,5},{7,4},{8,11},{9,10},{10,... | collective-permute-start | bytes 196616 | tf_op jit(solution)/shard_map/ppermute | solution.py:38
  111.8 5.8 %collective-permute-start.21 = (bf16[128,256]{1,0:T(8,128)(2,1)S(1)}, bf16[128,256]{1,0:T(8,128)(2,1)S(1)}, u32[]{:S(2)}, u32[]{:S(2)}) collective-permute-start(bf16[128,256]{1,0:T(8,128)(2,1)S(1)} %get-tuple-element.73), channel_id=1, source_target_pairs={{0,2},{1,3},{2,0},{3,1},{4,6},{5,7},{6,4},{7,5},{8,10},{9,11},{10,... | collective-permute-start | bytes 196616 | tf_op jit(solution)/shard_map/ppermute | solution.py:38
  119.8 6.8 %collective-permute-start.30 = (bf16[128,256]{1,0:T(8,128)(2,1)S(1)}, bf16[128,256]{1,0:T(8,128)(2,1)S(1)}, u32[]{:S(2)}, u32[]{:S(2)}) collective-permute-start(bf16[128,256]{1,0:T(8,128)(2,1)S(1)} %get-tuple-element.45.refs_0_.refs_6_.refs_11_), channel_id=1, source_target_pairs={{0,3},{1,2},{2,1},{3,0},{4,7},{5,6},{6,5},{7,4},{8,11},{9,10},{10,... | collective-permute-start | bytes 196616 | tf_op jit(solution)/shard_map/ppermute | solution.py:38
  122.0 6.5 %collective-permute-start.29 = (bf16[128,256]{1,0:T(8,128)(2,1)S(1)}, bf16[128,256]{1,0:T(8,128)(2,1)S(1)}, u32[]{:S(2)}, u32[]{:S(2)}) collective-permute-start(bf16[128,256]{1,0:T(8,128)(2,1)S(1)} %get-tuple-element.45.refs_0_.refs_6_.refs_11_), channel_id=1, source_target_pairs={{0,2},{1,3},{2,0},{3,1},{4,6},{5,7},{6,4},{7,5},{8,10},{9,11},{10,... | collective-permute-start | bytes 196616 | tf_op jit(solution)/shard_map/ppermute | solution.py:38
  122.0 6.5 %collective-permute-start.28 = (bf16[128,256]{1,0:T(8,128)(2,1)S(1)}, bf16[128,256]{1,0:T(8,128)(2,1)S(1)}, u32[]{:S(2)}, u32[]{:S(2)}) collective-permute-start(bf16[128,256]{1,0:T(8,128)(2,1)S(1)} %get-tuple-element.45.refs_0_.refs_6_.refs_11_), channel_id=1, source_target_pairs={{0,1},{1,0},{2,3},{3,2},{4,5},{5,4},{6,7},{7,6},{8,9},{9,8},{10,11... | collective-permute-start | bytes 196616 | tf_op jit(solution)/shard_map/ppermute | solution.py:38
  124.3 4.9 %collective-permute-start.33 = (bf16[4,128,256]{2,1,0:T(8,128)(2,1)S(1)}, bf16[4,128,256]{2,1,0:T(8,128)(2,1)S(1)}, u32[]{:S(2)}, u32[]{:S(2)}) collective-permute-start(bf16[4,128,256]{2,1,0:T(8,128)(2,1)S(1)} %get-tuple-element.50), channel_id=1, source_target_pairs={{0,4},{4,0},{8,12},{12,8},{16,20},{20,16},{24,28},{28,24},{1,5},{5... | collective-permute-start | bytes 786440 | tf_op jit(solution)/shard_map/ppermute | solution.py:27
  124.3 9.5 %collective-permute-start.34 = (bf16[4,128,256]{2,1,0:T(8,128)(2,1)S(1)}, bf16[4,128,256]{2,1,0:T(8,128)(2,1)S(1)}, u32[]{:S(2)}, u32[]{:S(2)}) collective-permute-start(bf16[4,128,256]{2,1,0:T(8,128)(2,1)S(1)} %get-tuple-element.51), channel_id=1, source_target_pairs={{0,28},{4,8},{8,4},{12,16},{16,12},{20,24},{24,20},{28,0},{1,29},{... | collective-permute-start | bytes 786440 | tf_op jit(solution)/shard_map/ppermute | solution.py:33
  128.6 14.8 %collective-permute-start.32 = (bf16[4,128,256]{2,1,0:T(8,128)(2,1)S(1)}, bf16[4,128,256]{2,1,0:T(8,128)(2,1)S(1)}, u32[]{:S(2)}, u32[]{:S(2)}) collective-permute-start(bf16[4,128,256]{2,1,0:T(8,128)(2,1)S(1)} %pad_maximum_fusion.1), channel_id=1, source_target_pairs={{0,28},{4,8},{8,4},{12,16},{16,12},{20,24},{24,20},{28,0},{1,29},{... | collective-permute-start | bytes 786440 | tf_op jit(solution)/shard_map/ppermute | solution.py:33
  129.0 14.4 %collective-permute-start.31 = (bf16[4,128,256]{2,1,0:T(8,128)(2,1)S(1)}, bf16[4,128,256]{2,1,0:T(8,128)(2,1)S(1)}, u32[]{:S(2)}, u32[]{:S(2)}) collective-permute-start(bf16[4,128,256]{2,1,0:T(8,128)(2,1)S(1)} %pad_maximum_fusion.1), channel_id=1, source_target_pairs={{0,4},{4,0},{8,12},{12,8},{16,20},{20,16},{24,28},{28,24},{1,5},{5... | collective-permute-start | bytes 786440 | tf_op jit(solution)/shard_map/ppermute | solution.py:27
  133.9 4.3 %collective-permute-start.35 = (bf16[128,256]{1,0:T(8,128)(2,1)S(1)}, bf16[128,256]{1,0:T(8,128)(2,1)S(1)}, u32[]{:S(2)}, u32[]{:S(2)}) collective-permute-start(bf16[128,256]{1,0:T(8,128)(2,1)S(1)} %get-tuple-element.68), channel_id=1, source_target_pairs={{0,1},{1,0},{2,3},{3,2},{4,5},{5,4},{6,7},{7,6},{8,9},{9,8},{10,11... | collective-permute-start | bytes 196616 | tf_op jit(solution)/shard_map/ppermute | solution.py:38
  134.0 6.6 %collective-permute-start.37 = (bf16[128,256]{1,0:T(8,128)(2,1)S(1)}, bf16[128,256]{1,0:T(8,128)(2,1)S(1)}, u32[]{:S(2)}, u32[]{:S(2)}) collective-permute-start(bf16[128,256]{1,0:T(8,128)(2,1)S(1)} %get-tuple-element.69), channel_id=1, source_target_pairs={{0,3},{1,2},{2,1},{3,0},{4,7},{5,6},{6,5},{7,4},{8,11},{9,10},{10,... | collective-permute-start | bytes 196616 | tf_op jit(solution)/shard_map/ppermute | solution.py:38
  136.2 7.1 %collective-permute-start.36 = (bf16[128,256]{1,0:T(8,128)(2,1)S(1)}, bf16[128,256]{1,0:T(8,128)(2,1)S(1)}, u32[]{:S(2)}, u32[]{:S(2)}) collective-permute-start(bf16[128,256]{1,0:T(8,128)(2,1)S(1)} %get-tuple-element.70), channel_id=1, source_target_pairs={{0,2},{1,3},{2,0},{3,1},{4,6},{5,7},{6,4},{7,5},{8,10},{9,11},{10,... | collective-permute-start | bytes 196616 | tf_op jit(solution)/shard_map/ppermute | solution.py:38
  145.5 6.8 %collective-permute-start.45 = (bf16[128,256]{1,0:T(8,128)(2,1)S(1)}, bf16[128,256]{1,0:T(8,128)(2,1)S(1)}, u32[]{:S(2)}, u32[]{:S(2)}) collective-permute-start(bf16[128,256]{1,0:T(8,128)(2,1)S(1)} %get-tuple-element.56.refs_6_.refs_12_), channel_id=1, source_target_pairs={{0,3},{1,2},{2,1},{3,0},{4,7},{5,6},{6,5},{7,4},{8,11},{9,10},{10,... | collective-permute-start | bytes 196616 | tf_op jit(solution)/shard_map/ppermute | solution.py:38
  147.5 6.1 %collective-permute-start.44 = (bf16[128,256]{1,0:T(8,128)(2,1)S(1)}, bf16[128,256]{1,0:T(8,128)(2,1)S(1)}, u32[]{:S(2)}, u32[]{:S(2)}) collective-permute-start(bf16[128,256]{1,0:T(8,128)(2,1)S(1)} %get-tuple-element.56.refs_6_.refs_12_), channel_id=1, source_target_pairs={{0,2},{1,3},{2,0},{3,1},{4,6},{5,7},{6,4},{7,5},{8,10},{9,11},{10,... | collective-permute-start | bytes 196616 | tf_op jit(solution)/shard_map/ppermute | solution.py:38
  147.5 6.1 %collective-permute-start.43 = (bf16[128,256]{1,0:T(8,128)(2,1)S(1)}, bf16[128,256]{1,0:T(8,128)(2,1)S(1)}, u32[]{:S(2)}, u32[]{:S(2)}) collective-permute-start(bf16[128,256]{1,0:T(8,128)(2,1)S(1)} %get-tuple-element.56.refs_6_.refs_12_), channel_id=1, source_target_pairs={{0,1},{1,0},{2,3},{3,2},{4,5},{5,4},{6,7},{7,6},{8,9},{9,8},{10,11... | collective-permute-start | bytes 196616 | tf_op jit(solution)/shard_map/ppermute | solution.py:38
  149.9 5.0 %collective-permute-start.38 = (bf16[4,128,256]{2,1,0:T(8,128)(2,1)S(1)}, bf16[4,128,256]{2,1,0:T(8,128)(2,1)S(1)}, u32[]{:S(2)}, u32[]{:S(2)}) collective-permute-start(bf16[4,128,256]{2,1,0:T(8,128)(2,1)S(1)} %get-tuple-element.54), channel_id=1, source_target_pairs={{0,4},{4,0},{8,12},{12,8},{16,20},{20,16},{24,28},{28,24},{1,5},{5... | collective-permute-start | bytes 786440 | tf_op jit(solution)/shard_map/ppermute | solution.py:27
  149.9 9.5 %collective-permute-start.39 = (bf16[4,128,256]{2,1,0:T(8,128)(2,1)S(1)}, bf16[4,128,256]{2,1,0:T(8,128)(2,1)S(1)}, u32[]{:S(2)}, u32[]{:S(2)}) collective-permute-start(bf16[4,128,256]{2,1,0:T(8,128)(2,1)S(1)} %get-tuple-element.55), channel_id=1, source_target_pairs={{0,28},{4,8},{8,4},{12,16},{16,12},{20,24},{24,20},{28,0},{1,29},{... | collective-permute-start | bytes 786440 | tf_op jit(solution)/shard_map/ppermute | solution.py:33
  153.6 15.4 %collective-permute-start.47 = (bf16[4,128,256]{2,1,0:T(8,128)(2,1)S(1)}, bf16[4,128,256]{2,1,0:T(8,128)(2,1)S(1)}, u32[]{:S(2)}, u32[]{:S(2)}) collective-permute-start(bf16[4,128,256]{2,1,0:T(8,128)(2,1)S(1)} %pad_maximum_fusion.2), channel_id=1, source_target_pairs={{0,28},{4,8},{8,4},{12,16},{16,12},{20,24},{24,20},{28,0},{1,29},{... | collective-permute-start | bytes 786440 | tf_op jit(solution)/shard_map/ppermute | solution.py:33
  153.9 15.0 %collective-permute-start.46 = (bf16[4,128,256]{2,1,0:T(8,128)(2,1)S(1)}, bf16[4,128,256]{2,1,0:T(8,128)(2,1)S(1)}, u32[]{:S(2)}, u32[]{:S(2)}) collective-permute-start(bf16[4,128,256]{2,1,0:T(8,128)(2,1)S(1)} %pad_maximum_fusion.2), channel_id=1, source_target_pairs={{0,4},{4,0},{8,12},{12,8},{16,20},{20,16},{24,28},{28,24},{1,5},{5... | collective-permute-start | bytes 786440 | tf_op jit(solution)/shard_map/ppermute | solution.py:27
  159.6 4.3 %collective-permute-start.40 = (bf16[128,256]{1,0:T(8,128)(2,1)S(1)}, bf16[128,256]{1,0:T(8,128)(2,1)S(1)}, u32[]{:S(2)}, u32[]{:S(2)}) collective-permute-start(bf16[128,256]{1,0:T(8,128)(2,1)S(1)} %get-tuple-element.65), channel_id=1, source_target_pairs={{0,1},{1,0},{2,3},{3,2},{4,5},{5,4},{6,7},{7,6},{8,9},{9,8},{10,11... | collective-permute-start | bytes 196616 | tf_op jit(solution)/shard_map/ppermute | solution.py:38
  159.6 6.6 %collective-permute-start.42 = (bf16[128,256]{1,0:T(8,128)(2,1)S(1)}, bf16[128,256]{1,0:T(8,128)(2,1)S(1)}, u32[]{:S(2)}, u32[]{:S(2)}) collective-permute-start(bf16[128,256]{1,0:T(8,128)(2,1)S(1)} %get-tuple-element.66), channel_id=1, source_target_pairs={{0,3},{1,2},{2,1},{3,0},{4,7},{5,6},{6,5},{7,4},{8,11},{9,10},{10,... | collective-permute-start | bytes 196616 | tf_op jit(solution)/shard_map/ppermute | solution.py:38
  161.6 7.3 %collective-permute-start.41 = (bf16[128,256]{1,0:T(8,128)(2,1)S(1)}, bf16[128,256]{1,0:T(8,128)(2,1)S(1)}, u32[]{:S(2)}, u32[]{:S(2)}) collective-permute-start(bf16[128,256]{1,0:T(8,128)(2,1)S(1)} %get-tuple-element.67), channel_id=1, source_target_pairs={{0,2},{1,3},{2,0},{3,1},{4,6},{5,7},{6,4},{7,5},{8,10},{9,11},{10,... | collective-permute-start | bytes 196616 | tf_op jit(solution)/shard_map/ppermute | solution.py:38
  (6 other events, 71.8 us)

commit v2 on v1

v2 whole, which is shorter than its diff:
```python
import functools

import jax
import jax.numpy as jnp
from jax import lax
from jax.experimental import pallas as pl
from jax.experimental.pallas import tpu as pltpu
from jax.sharding import PartitionSpec as P


F32 = jnp.float32
BF16 = jnp.bfloat16
IN_VMEM = pl.BlockSpec(memory_space=pltpu.VMEM)
IN_SMEM = pl.BlockSpec(memory_space=pltpu.SMEM)


def dot_nn(a, b):
    return lax.dot_general(a, b, (((1,), (0,)), ((), ())), preferred_element_type=F32)


def dot_nt(a, b):
    return lax.dot_general(a, b, (((1,), (1,)), ((), ())), preferred_element_type=F32)


def even_exchange(value):
    count = lax.axis_size("region")
    return lax.ppermute(value, "region", [(i, i ^ 1) for i in range(count)])


def odd_exchange(value):
    count = lax.axis_size("region")
    route = [(i, (i + 1) % count if i % 2 else (i - 1) % count) for i in range(count)]
    return lax.ppermute(value, "region", route)


def cut_exchange(value, j):
    count = lax.axis_size("cuts")
    return lax.ppermute(value, "cuts", [(i, i ^ j) for i in range(count)])


def cut_pieces(value):
    count = lax.axis_size("cuts")
    if count != 4:
        return {j: cut_exchange(value, j) for j in range(1, count)}
    inner = [(1, 2), (2, 1)]
    outward = [(1, 0), (2, 3)]
    first = cut_exchange(value, 1)
    across = lax.ppermute(value, "cuts", inner)
    far = lax.ppermute(across, "cuts", outward)
    passed = lax.ppermute(first, "cuts", inner)
    ends = lax.ppermute(value, "cuts", [(0, 3), (3, 0)])
    return {1: first, 3: across + ends, 2: passed + far}


def call(body, scalars, args, outs, scratch, flops, read, aliases=None, far=(), limit=8):
    return pl.pallas_call(
        body,
        out_shape=outs,
        in_specs=[IN_SMEM] * len(scalars)
        + [pl.BlockSpec(memory_space=pltpu.HBM) if i in far else IN_VMEM for i in range(len(args))],
        input_output_aliases={len(scalars) + i: o for i, o in (aliases or {}).items()},
        out_specs=jax.tree.map(lambda _: IN_VMEM, outs),
        scratch_shapes=scratch,
        compiler_params=pltpu.CompilerParams(vmem_limit_bytes=limit * 1024 * 1024),
        cost_estimate=pl.CostEstimate(
            flops=int(flops) // 1000, bytes_accessed=int(read) // 1000, transcendentals=0
        ),
    )(*scalars, *args)


def gated(kern, lag, last):
    return kern * jnp.where(lag <= last, 1.0, 0.0).astype(BF16)


def lag_chain(dot, block, kern, p, last, low, high, add):
    lags = kern.shape[1]
    rows, panels = block.shape[-2:]
    full = None
    for l in range(lags, low, -1):
        top = min(high, l)
        x = block[l - top : l - low].reshape((top - low) * rows, panels)
        y = dot(x, gated(kern[p, l - 1], l, last) if l > 1 else kern[p, l - 1])
        if top == high:
            full = y if full is None else full + y
            if l == max(high, low + 1):
                add(0, full)
        else:
            add(high - top, y)


def turn_body(value, out):
    for i in range(value.shape[0]):
        out[i] = value[i].T


def turned(value):
    count, panels, rows = value.shape
    return call(
        turn_body, (), (value,),
        jax.ShapeDtypeStruct((count, rows, panels), value.dtype), [], 0, 4 * value.size,
    )


def enter_body(cuts, codes, lags, history, out, loc, used):
    turn_body(history, out)

    @pl.when(pl.program_id(0) == 0)
    def _():
        odd_region = lax.rem(lax.axis_index("region"), 2)
        own_cut = lax.axis_index("cuts")
        for p in range(codes.shape[0]):
            used[p] = lags[p]
            shift = lax.div(codes[p], cuts) - 1
            side = jnp.where((shift == 1) == (odd_region == 0), 1, 2)
            side = jnp.where(shift == 0, 0, side)
            loc[p] = side * cuts + (lax.rem(codes[p], cuts) ^ own_cut)


def enter(codes, lags, history, cuts):
    count, panels, rows = history.shape
    parts = 2 if count % 2 == 0 else 1
    return pl.pallas_call(
        functools.partial(enter_body, cuts),
        name="enter",
        grid=(parts,),
        in_specs=[
            IN_SMEM,
            IN_SMEM,
            pl.BlockSpec((count // parts, panels, rows), lambda i: (i, 0, 0)),
        ],
        out_specs=(pl.BlockSpec((count // parts, rows, panels), lambda i: (i, 0, 0)), IN_SMEM, IN_SMEM),
        out_shape=(
            jax.ShapeDtypeStruct((count, rows, panels), history.dtype),
            jax.ShapeDtypeStruct(codes.shape, codes.dtype),
            jax.ShapeDtypeStruct(lags.shape, lags.dtype),
        ),
        compiler_params=pltpu.CompilerParams(vmem_limit_bytes=8 * 1024 * 1024),
        cost_estimate=pl.CostEstimate(flops=0, bytes_accessed=4096, transcendentals=0),
    )(codes, lags, history)


def history_back_body(steps, cuts, first, low, high, loc, used, hist, kern, *refs):
    rows = hist.shape[1]
    if first:
        heaps, (held, done) = refs[:steps], refs[steps:]
        for p in range(low, high):
            pltpu.make_async_copy(kern.at[p], held.at[p - low], done.at[p - low]).start()
        for heap in heaps:
            heap[...] = jnp.zeros_like(heap)
    else:
        heaps, (own, even, odd) = refs[steps : 2 * steps], refs[2 * steps :]
        held = kern

    def pair(q, carry):
        p = low + q
        slot = loc[p]
        if first:
            pltpu.make_async_copy(kern.at[p], held.at[q], done.at[q]).wait()

        def add(at, y):
            for i in range(at, steps):
                heaps[i][slot] += y[(i - at) * rows : (i - at + 1) * rows]

        lag_chain(dot_nn, hist, held, q if first else p, used[p], 0, steps, add)
        return carry

    lax.fori_loop(0, high - low, pair, 0)
    if not first:
        total = heaps[steps - 1]
        own[...] = total[:cuts]
        even[...] = total[cuts : 2 * cuts].astype(BF16)
        odd[...] = total[2 * cuts :].astype(BF16)


def history_back(loc, used, hist, kern, cuts, steps, low, high, heaps):
    _, lags, panels, _ = kern.shape
    rows = hist.shape[1]
    first = heaps is None
    part = (cuts, rows, panels)
    heap = jax.ShapeDtypeStruct((3 * cuts, rows, panels), F32)
    outs = (heap,) * steps
    if not first:
        outs += (
            jax.ShapeDtypeStruct(part, F32),
            jax.ShapeDtypeStruct(part, BF16),
            jax.ShapeDtypeStruct(part, BF16),
        )
    count = high - low
    return call(
        functools.partial(history_back_body, steps, cuts, first, low, high),
        (loc, used),
        [hist, kern] + ([] if first else list(heaps)),
        outs,
        [pltpu.VMEM((count,) + kern.shape[1:], BF16), pltpu.SemaphoreType.DMA((count,))]
        if first
        else [],
        2 * count * lags * steps * rows * panels * panels,
        2 * kern.size,
        aliases=None if first else {2 + i: i for i in range(steps)},
        far=(1,) if first else (),
        limit=40 if first else 8,
    )


def history_front_body(slots, low, high, has_before, loc, used, kern, *refs):
    blocks = refs[: len(slots)]
    refs = refs[len(slots) :]
    after, near = refs[-2:]
    rows = near.shape[2]
    for i, block in enumerate(blocks):
        near[i] = block[...]
    after[...] = refs[0][: high - low] if has_before else jnp.zeros_like(after)

    def pair(p, carry):
        slot = loc[p]
        at = jnp.int32(-1)
        for i, s in enumerate(slots):
            at = jnp.where(slot == s, i, at)

        @pl.when(at >= 0)
        def _():
            def add(i, y):
                after[i:] += y.reshape(high - low - i, rows, y.shape[-1])

            lag_chain(dot_nt, near.at[at], kern, p, used[p], low, high, add)

        return carry

    lax.fori_loop(0, kern.shape[0], pair, 0)


def history_front(loc, used, kern, near, before, low, high):
    pairs, lags, panels, _ = kern.shape
    slots = tuple(near)
    blocks = [near[s] for s in slots]
    rows = blocks[0].shape[1]
    share = len(slots) / 12
    return call(
        functools.partial(history_front_body, slots, low, high, before is not None),
        (loc, used),
        [kern] + blocks + ([] if before is None else [before]),
        jax.ShapeDtypeStruct((high - low, rows, panels), F32),
        [pltpu.VMEM((len(slots), lags, rows, panels), BF16)],
        share * 2 * pairs * lags * (high - low) * rows * panels * panels,
        share * 2 * kern.size,
    )


def fill_near(near, own, side, even, odd):
    cuts = even.shape[0]
    near[0] = own[...]
    near[1:cuts] = side[...]
    near[cuts : 2 * cuts] = even[...]
    near[2 * cuts :] = odd[...]


def step_body(n, at, cuts, pairs, has_front, has_back, final, loc, used, *refs):
    refs = list(refs)
    ahead, mine, incoming, inverse, kern = refs[:5]
    moved, refs = refs[5 : 4 + cuts], refs[4 + cuts :]
    total = ahead[at] + mine[...]
    for part in moved:
        total = total + part[...].astype(F32)
    if has_front:
        near = refs[-1]
        fill_near(near, *refs[:4])
        refs = refs[4:]
        for p in range(pairs):
            total = total + dot_nt(near[loc[p]], kern[p, 0])
    if final:
        blocks, rest = refs[: len(final)], refs[-1]
        refs = refs[len(final) :]
        rest[...] = total
        for block, slot in zip(blocks, final):

            def pair(p, carry, block=block, slot=slot):
                @pl.when(loc[p] == slot)
                def _():
                    def add(_, y):
                        rest[...] += y

                    lag_chain(dot_nt, block, kern, p, used[p], 0, 1, add)

                return carry

            lax.fori_loop(0, pairs, pair, 0)
        total = rest[...]
    excess = (incoming[n].astype(F32) - total).astype(BF16)
    density = dot_nt(excess, inverse[...]).astype(BF16)
    if has_back:
        _, out, out_own, out_even, out_odd, sums = refs[:6]
        out[...] = density
        for p in range(pairs):
            sums[loc[p]] += dot_nn(density, kern[p, 0])
        out_own[...] = sums[:cuts]
        out_even[...] = sums[cuts : 2 * cuts].astype(BF16)
        out_odd[...] = sums[2 * cuts :].astype(BF16)
    else:
        earlier, out = refs[: n], refs[n]
        for m in range(n):
            out[m] = earlier[m][...].astype(F32).T.astype(BF16)
        out[n] = density.astype(F32).T.astype(BF16)


def step_call(
    n, steps, loc, used, ahead, mine, moved, incoming, inverse, kern, near, begun, earlier, final
):
    pairs, _, panels, _ = kern.shape
    cuts = len(moved) + 1
    rows = mine.shape[0]
    has_front = near is not None
    has_back = n + 1 < steps
    part = (cuts, rows, panels)
    heap = (3 * cuts, rows, panels)
    ahead, at = ahead
    args = [ahead, mine, incoming, inverse, kern] + moved
    scratch = []
    aliases = {}
    if has_front:
        args += list(near)
    args += list(final.values())
    if has_back:
        args.append(begun)
        outs = (
            jax.ShapeDtypeStruct((rows, panels), BF16),
            jax.ShapeDtypeStruct(part, F32),
            jax.ShapeDtypeStruct(part, BF16),
            jax.ShapeDtypeStruct(part, BF16),
            jax.ShapeDtypeStruct(heap, F32),
        )
        aliases[len(args) - 1] = 4
    else:
        args += earlier
        outs = jax.ShapeDtypeStruct((steps, panels, rows), BF16)
    if has_front:
        scratch.append(pltpu.VMEM(heap, BF16))
    if final:
        scratch.append(pltpu.VMEM((rows, panels), F32))
    return call(
        functools.partial(step_body, n, at, cuts, pairs, has_front, has_back, tuple(final)),
        (loc, used),
        args,
        outs,
        scratch,
        4 * pairs * rows * panels * panels,
        2 * pairs * panels * panels,
        aliases=aliases,
    )


def later_body(back, front, loc, used, kern, *refs):
    refs = list(refs)
    has_near = bool(front)
    near = refs.pop() if has_near else None
    news = refs[len(refs) - len(back) - len(front) :]
    density = refs.pop(0) if back else None
    if has_near:
        fill_near(near, *refs[:4])
        refs = refs[4:]
    rows = [refs[len(back) + i][at] for i, (_, at) in enumerate(front)]
    for p in range(kern.shape[0]):
        slot = loc[p]
        last = used[p]
        for i, lag in enumerate(back):
            news[i][slot] += dot_nn(density[...], gated(kern[p, lag - 1], lag, last))
        for i, (lag, _) in enumerate(front):
            rows[i] += dot_nt(near[slot], gated(kern[p, lag - 1], lag, last))
    for i in range(len(front)):
        news[len(back) + i][0] = rows[i]


def later_call(loc, used, kern, cuts, density, back, near, front):
    pairs, _, panels, _ = kern.shape
    args = [kern]
    scratch = []
    if back:
        args.append(density)
    if front:
        args += list(near)
        scratch.append(pltpu.VMEM((3 * cuts,) + near[0].shape, BF16))
    args += [sums for _, sums in back] + [sums for _, (sums, _) in front]
    rows = (density if back else near[0]).shape[0]
    outs = [jax.ShapeDtypeStruct(sums.shape, F32) for _, sums in back]
    outs += [jax.ShapeDtypeStruct((1, rows, panels), F32) for _ in front]
    terms = len(back) + len(front)
    return call(
        functools.partial(
            later_body, [lag for lag, _ in back], [(lag, at) for lag, (_, at) in front]
        ),
        (loc, used),
        args,
        tuple(outs),
        scratch,
        2 * terms * pairs * rows * panels * panels,
        2 * terms * pairs * panels * panels,
        aliases={len(args) - len(back) - len(front) + i: i for i in range(len(back))},
    )


def gather_near(value):
    cuts = lax.axis_size("cuts")
    side = []
    for j in range(1, cuts):
        side.append(cut_exchange(value, j))
    side = jnp.stack(side)
    region = jnp.concatenate([value[None], side])
    odd = odd_exchange(region)
    even = even_exchange(region)
    return value, side, even, odd


def total_body(own, even, odd, mine, *parts):
    for j in range(own.shape[0]):
        total = own[j] + even[j].astype(F32) + odd[j].astype(F32)
        if j:
            parts[j - 1][...] = total.astype(BF16)
        else:
            mine[...] = total


def sum_parts(own, even, odd):
    cuts = lax.axis_size("cuts")
    odd = odd_exchange(odd)
    even = even_exchange(even)
    mine, *part = call(
        total_body, (), (own, even, odd),
        (jax.ShapeDtypeStruct(own.shape[1:], F32),)
        + (jax.ShapeDtypeStruct(own.shape[1:], BF16),) * (cuts - 1),
        [], 2 * own.size, 8 * own.size,
    )
    moved = []
    for j in range(1, cuts):
        moved.append(cut_exchange(part[j - 1], j))
    return mine, moved


def every_step(history, incident, self_inverse, lag_kernels, pair_partner, pair_lags):
    steps = incident.shape[0]
    cuts = lax.axis_size("cuts")
    hist, loc, used = enter(pair_partner, pair_lags, history, cuts)
    incoming = turned(incident)

    half = pair_lags.shape[0] // 2
    heaps = history_back(loc, used, hist, lag_kernels, cuts, steps, 0, half, None)
    *heaps, own, even, odd = history_back(
        loc, used, hist, lag_kernels, cuts, steps, half, pair_lags.shape[0], heaps
    )
    begun = {steps - 1 - i: heap for i, heap in enumerate(heaps)}
    mine, moved = sum_parts(own, even, odd)

    pieces = {0: hist, **cut_pieces(hist)}
    blocks = {}
    for j, piece in pieces.items():
        odd = odd_exchange(piece)
        even = even_exchange(piece)
        blocks.update({j: piece, cuts + j: even, 2 * cuts + j: odd})
    *_, j_late, j_final = pieces
    final = {slot: blocks.pop(slot) for slot in range(j_final, 3 * cuts, cuts)}
    late = {slot: blocks.pop(slot) for slot in (cuts + j_late, 2 * cuts + j_late)}
    sums = history_front(loc, used, lag_kernels, blocks, None, 0, steps)
    sums = history_front(loc, used, lag_kernels, late, sums, 0, steps)
    ahead = {n: (sums, steps - 1 - n) for n in range(steps)}

    near = None
    densities = []
    for n in range(steps - 1):
        density, own, even, odd, _ = step_call(
            n, steps, loc, used, ahead[n], mine, moved, incoming, self_inverse, lag_kernels,
            near, begun.get(n + 1), None, {} if n else final,
        )
        densities.append(density)
        before, near = near, gather_near(density)
        mine, moved = sum_parts(own, even, odd)
        if n == 0:
            sums = history_front(loc, used, lag_kernels, final, sums, 1, steps)
            ahead = {m: (sums, steps - 1 - m) for m in range(1, steps)}
        back = [(m - n, begun[m]) for m in range(n + 2, steps)]
        front = [(m - n + 1, ahead[m]) for m in range(n + 1, steps)] if n else []
        if back or front:
            news = later_call(loc, used, lag_kernels, cuts, density, back, before, front)
            for i, m in enumerate(range(n + 2, steps)):
                begun[m] = news[i]
            if n:
                for i, m in enumerate(range(n + 1, steps)):
                    ahead[m] = (news[len(back) + i], 0)
    return step_call(
        steps - 1, steps, loc, used, ahead[steps - 1], mine, moved, incoming, self_inverse,
        lag_kernels, near, None, densities, {},
    )


def solution(mesh):
    return jax.shard_map(
        every_step,
        mesh=mesh,
        in_specs=(
            P(None, ("region", "cuts"), None),
            P(None, ("region", "cuts"), None),
            P(("region", "cuts"), None),
            P(("region", "cuts"), None, None, None),
            P(("region", "cuts")),
            P(("region", "cuts")),
        ),
        out_specs=P(None, ("region", "cuts"), None),
        check_vma=False,
    )
```

time: 171 us -> 160 us (0.936)
  waiting for transfers between devices: 82.9 us -> 61.7 us
  starting transfers between devices: 48.9 us -> 56.7 us
  Pallas kernels: 34.5 us -> 37.4 us
    ppermute x22, waiting for transfers between devices: 42.9 us -> 20.4 us  [cut_exchange(): return lax.ppermute(value, 'cuts', [(i, i ^ j) for i in range(count)])]
    ppermute x1, waiting for transfers between devices: 7.89 us -> 0.21 us  [cut_pieces(): ends = lax.ppermute(value, 'cuts', [(0, 3), (3, 0)])]
    ppermute x11, waiting for transfers between devices: 32 us -> 38.8 us  [odd_exchange(): return lax.ppermute(value, 'region', route)]
    ppermute x11, starting transfers between devices: 9.59 us -> 14.3 us  [odd_exchange(): return lax.ppermute(value, 'region', route)]
    ppermute x1, starting transfers between devices: 1.46 us -> 4.38 us  [cut_pieces(): ends = lax.ppermute(value, 'cuts', [(0, 3), (3, 0)])]
    pallas_call x12 -> x17, Pallas kernels: 33 us -> 35.9 us  [call(): pl.pallas_call(body, out_shape=outs, in_specs=[IN_SMEM] * len(scalars) +...]
    ppermute x1, waiting for transfers between devices: 0.02 us -> 2.29 us  [cut_pieces(): far = lax.ppermute(across, 'cuts', outward)]
  transfers between devices with their start and end apart: 48 -> 48, of which waited for: 26 -> 23; matrix products, arithmetic and copies ran while one was open for 1% -> 0% of each run, Pallas kernels for 14% -> 16%
where the time goes in v2:
time: 160 us
  waiting for transfers between devices  61.7 us (39%)
  starting transfers between devices  56.7 us (35%)
  Pallas kernels  37.4 us (23%)
  local copies, waits for them, and re-layouts  2.97 us (2%)
    ppermute x11, waiting for transfers between devices, odd_exchange(): return lax.ppermute(value, 'region', route)  38.8 us
    pallas_call x17, Pallas kernels, call(): pl.pallas_call(body, out_shape=outs, in_specs=[IN_SMEM] * len(scalars) +...  35.9 us
    ppermute x22, starting transfers between devices, cut_exchange(): return lax.ppermute(value, 'cuts', [(i, i ^ j) for i in range(count)])  33.1 us
    ppermute x22, waiting for transfers between devices, cut_exchange(): return lax.ppermute(value, 'cuts', [(i, i ^ j) for i in range(count)])  20.4 us
    ppermute x11, starting transfers between devices, odd_exchange(): return lax.ppermute(value, 'region', route)  14.3 us
    ppermute x1, starting transfers between devices, cut_pieces(): ends = lax.ppermute(value, 'cuts', [(0, 3), (3, 0)])  4.38 us
  transfers between devices with their start and end apart: 48, of which 23 were waited for; matrix products, arithmetic and copies ran while one was open for 0% of the time, Pallas kernels for 16%

profile of v2, /device:TPU:0, one launch (start us, length us, event | category | flops | bytes accessed | tf_op | source)
XLA Modules:
  0.0 159.8 jit_solution(6726113567488998940)
XLA Ops:
  2.4 1.5 enter.1
  3.9 3.1 %collective-permute-start = (bf16[8,128,256]{2,1,0:T(8,128)(2,1)S(1)}, bf16[8,128,256]{2,1,0:T(8,128)(2,1)S(1)}, u32[]{:S(2)}, u32[]{:S(2)}) collective-permute-start(bf16[8,128,256]{2,1,0:T(8,128)(2,1)S(1)} %get-tuple-element.53.refs_0_.hist), channel_id=1, source_target_pairs={{0,1},{1,0},{2,3},{3,2},{4,5},{5,4},{6,7},{7,6},{8,9},{9,8},{10,11... | collective-permute-start | bytes 1572872 | tf_op jit(solution)/shard_map/ppermute | solution.py:38
  7.7 4.4 %collective-permute-start.6 = (bf16[8,128,256]{2,1,0:T(8,128)(2,1)S(1)}, bf16[8,128,256]{2,1,0:T(8,128)(2,1)S(1)}, u32[]{:S(2)}, u32[]{:S(2)}) collective-permute-start(bf16[8,128,256]{2,1,0:T(8,128)(2,1)S(1)} %get-tuple-element.53.refs_0_.hist), channel_id=1, source_target_pairs={{0,3},{3,0},{4,7},{7,4},{8,11},{11,8},{12,15},{15,12},{16,19},{19,... | collective-permute-start | bytes 1572872 | tf_op jit(solution)/shard_map/ppermute | solution.py:51
  12.1 5.8 %shard_map.67 = (f32[12,128,256]{2,1,0:T(8,128)S(1)}, f32[12,128,256]{2,1,0:T(8,128)S(1)}, f32[12,128,256]{2,1,0:T(8,128)S(1)}, f32[12,128,256]{2,1,0:T(8,128)S(1)}) custom-call(s32[12]{0:T(128)S(1)} %get-tuple-element.51.loc, s32[12]{0:T(128)S(1)} %get-tuple-element.52.used, bf16[8,128,256]{2,1,0:T(8,128)(2,1)S(1)} %get-tuple-element.53.refs_0_.hist, ...), custom_call_target="tpu_custom_call" | custom-call | flops 3221225 | bytes 12582 | tf_op jit(solution)/shard_map/pallas_call | solution.py:56
  18.5 4.4 %shard_map.68 = (f32[12,128,256]{2,1,0:T(8,128)S(1)}, f32[12,128,256]{2,1,0:T(8,128)S(1)}, f32[12,128,256]{2,1,0:T(8,128)S(1)}, f32[12,128,256]{2,1,0:T(8,128)S(...) custom-call(s32[12]{0:T(128)S(1)} %get-tuple-element.51.loc, ...), custom_call_target="tpu_custom_call", output_to_operand_aliasing={{0}: (4, {}), {1}: (5, {}), {2}: (6, {}), {3}: (7, {})} | custom-call | flops 3221225 | bytes 12582 | tf_op jit(solution)/shard_map/pallas_call | solution.py:56
  23.0 2.5 %collective-permute-start.14 = (bf16[4,128,256]{2,1,0:T(8,128)(2,1)S(1)}, bf16[4,128,256]{2,1,0:T(8,128)(2,1)S(1)}, u32[]{:S(2)}, u32[]{:S(2)}) collective-permute-start(bf16[4,128,256]{2,1,0:T(8,128)(2,1)S(1)} %get-tuple-element.60), channel_id=1, source_target_pairs={{0,28},{4,8},{8,4},{12,16},{16,12},{20,24},{24,20},{28,0},{1,29},{... | collective-permute-start | bytes 786440 | tf_op jit(solution)/shard_map/ppermute | solution.py:33
  27.4 1.3 collective-permute-start.3
  28.7 3.5 %collective-permute-done.14.odd = bf16[4,128,256]{2,1,0:T(8,128)(2,1)S(1)} collective-permute-done((bf16[4,128,256]{2,1,0:T(8,128)(2,1)S(1)}, bf16[4,128,256]{2,1,0:T(8,128)(2,1)S(1)}, u32[]{:S(2)}, u32[]{:S(2)}) %collective-permute-start.14) | collective-permute-done | bytes 262176 | tf_op jit(solution)/shard_map/ppermute | solution.py:33
  32.7 10.4 %collective-permute-done.10.refs_2_ = bf16[8,128,256]{2,1,0:T(8,128)(2,1)S(1)} collective-permute-done((bf16[8,128,256]{2,1,0:T(8,128)(2,1)S(1)}, bf16[8,128,256]{2,1,0:T(8,128)(2,1)S(1)}, u32[]{:S(2)}, u32[]{:S(2)}) %collective-permute-start.10) | collective-permute-done | bytes 524320 | tf_op jit(solution)/shard_map/ppermute | solution.py:33
  43.1 1.6 collective-permute-start.12
  45.0 2.3 %collective-permute-done.3 = bf16[8,128,256]{2,1,0:T(8,128)(2,1)S(1)} collective-permute-done((bf16[8,128,256]{2,1,0:T(8,128)(2,1)S(1)}, bf16[8,128,256]{2,1,0:T(8,128)(2,1)S(1)}, u32[]{:S(2)}, u32[]{:S(2)}) %collective-permute-start.3) | collective-permute-done | bytes 524320 | tf_op jit(solution)/shard_map/ppermute | solution.py:49
  47.4 1.7 %collective-permute-start.4 = (bf16[8,128,256]{2,1,0:T(8,128)(2,1)S(1)}, bf16[8,128,256]{2,1,0:T(8,128)(2,1)S(1)}, u32[]{:S(2)}, u32[]{:S(2)}) collective-permute-start(bf16[8,128,256]{2,1,0:T(8,128)(2,1)S(1)} %add.6.refs_0_.refs_8_), channel_id=1, source_target_pairs={{0,4},{4,0},{8,12},{12,8},{16,20},{20,16},{24,28},{28,24},{1,5},{5... | collective-permute-start | bytes 1572872 | tf_op jit(solution)/shard_map/ppermute | solution.py:27
  50.3 7.9 %collective-permute-done.12.refs_5_ = bf16[8,128,256]{2,1,0:T(8,128)(2,1)S(1)} collective-permute-done((bf16[8,128,256]{2,1,0:T(8,128)(2,1)S(1)}, bf16[8,128,256]{2,1,0:T(8,128)(2,1)S(1)}, u32[]{:S(2)}, u32[]{:S(2)}) %collective-permute-start.12) | collective-permute-done | bytes 524320 | tf_op jit(solution)/shard_map/ppermute | solution.py:33
  58.9 1.2 collective-permute-start.16
  60.1 9.3 %collective-permute-done.8.refs_1_ = bf16[8,128,256]{2,1,0:T(8,128)(2,1)S(1)} collective-permute-done((bf16[8,128,256]{2,1,0:T(8,128)(2,1)S(1)}, bf16[8,128,256]{2,1,0:T(8,128)(2,1)S(1)}, u32[]{:S(2)}, u32[]{:S(2)}) %collective-permute-start.8) | collective-permute-done | bytes 524320 | tf_op jit(solution)/shard_map/ppermute | solution.py:33
  69.4 1.3 collective-permute-start.17
  70.9 3.9 %shard_map.64.refs_2_ = f32[4,128,256]{2,1,0:T(8,128)S(1)} custom-call(s32[12]{0:T(128)S(1)} %get-tuple-element.51.loc, s32[12]{0:T(128)S(1)} %get-tuple-element.52.used, bf16[12,8,256,256]{3,2,1,0:T(8,128)(2,1)S(1)} %copy-done, bf16[8,128,256]{2,1,0:T(8,128)(2,1)S(1)} %get-tuple-element.53.refs_0_.hist, ...), custom_call_target="tpu_custom_call" | custom-call | flops 3758096 | bytes 7340 | tf_op jit(solution)/shard_map/pallas_call | solution.py:56
  74.8 2.2 %shard_map.65.refs_3_.refs_0_ = f32[4,128,256]{2,1,0:T(8,128)S(1)} custom-call(s32[12]{0:T(128)S(1)} %get-tuple-element.51.loc, s32[12]{0:T(128)S(1)} %get-tuple-element.52.used, bf16[12,8,256,256]{3,2,1,0:T(8,128)(2,1)S(1)} %copy-done, bf16[8,128,256]{2,1,0:T(8,128)(2,1)S(1)} %collective-permute-done.7.refs_0_, ...), custom_call_target="tpu_custom_call" | custom-call | flops 1073741 | bytes 2097 | tf_op jit(solution)/shard_map/pallas_call | solution.py:56
  77.0 3.6 %collective-permute-done.5.refs_2_.refs_10_ = bf16[8,128,256]{2,1,0:T(8,128)(2,1)S(1)} collective-permute-done((bf16[8,128,256]{2,1,0:T(8,128)(2,1)S(1)}, bf16[8,128,256]{2,1,0:T(8,128)(2,1)S(1)}, u32[]{:S(2)}, u32[]{:S(2)}) %collective-permute-start.5) | collective-permute-done | bytes 524320 | tf_op jit(solution)/shard_map/ppermute | solution.py:33
  80.7 4.7 %shard_map.71 = (bf16[128,256]{1,0:T(8,128)(2,1)S(1)}, f32[4,128,256]{2,1,0:T(8,128)S(1)}, bf16[4,128,256]{2,1,0:T(8,128)(2,1)S(1)}, bf16[4,128,256]{2,1,0:T(8,128)(2,1)S(1)}, f32[12,128,256]{2,1,0:T(8,128)S(1)}) custom-call(s32[12]{0:T(128)S(1)} %get-tuple-element.51.loc, s32[12]{0:T(128)S(1)} %get-tuple-element.52.used, ...), custom_call_target="tpu_custom_call", output_to_operand_aliasing={{4}: (13, {})} | custom-call | flops 402653 | bytes 1572 | tf_op jit(solution)/shard_map/pallas_call | solution.py:56
  85.4 1.4 collective-permute-start.24
  86.8 3.0 %collective-permute-start.25 = (bf16[128,256]{1,0:T(8,128)(2,1)S(1)}, bf16[128,256]{1,0:T(8,128)(2,1)S(1)}, u32[]{:S(2)}, u32[]{:S(2)}) collective-permute-start(bf16[128,256]{1,0:T(8,128)(2,1)S(1)} %get-tuple-element.73.refs_0_.refs_8_.refs_1_.refs_12_), channel_id=1, source_target_pairs={{0,3},{1,2},{2,1},{3,0},{4,7},{5,6},{6,5},{7,4},{8,11},{9,10},{10,... | collective-permute-start | bytes 196616 | tf_op jit(solution)/shard_map/ppermute | solution.py:38
  91.1 1.8 %collective-permute-done.25 = bf16[128,256]{1,0:T(8,128)(2,1)S(1)} collective-permute-done((bf16[128,256]{1,0:T(8,128)(2,1)S(1)}, bf16[128,256]{1,0:T(8,128)(2,1)S(1)}, u32[]{:S(2)}, u32[]{:S(2)}) %collective-permute-start.25) | collective-permute-done | bytes 65568 | tf_op jit(solution)/shard_map/ppermute | solution.py:38
  94.5 4.0 %shard_map.66.refs_0_.refs_6_.refs_7_ = f32[3,128,256]{2,1,0:T(8,128)S(1)} custom-call(s32[12]{0:T(128)S(1)} %get-tuple-element.51.loc, s32[12]{0:T(128)S(1)} %get-tuple-element.52.used, bf16[12,8,256,256]{3,2,1,0:T(8,128)(2,1)S(1)} %copy-done, bf16[8,128,256]{2,1,0:T(8,128)(2,1)S(1)} %add.6.refs_0_.refs_8_, ...), custom_call_target="tpu_custom_call" | custom-call | flops 1207959 | bytes 3145 | tf_op jit(solution)/shard_map/pallas_call | solution.py:56
  98.7 2.7 %collective-permute-start.21 = (bf16[128,256]{1,0:T(8,128)(2,1)S(1)}, bf16[128,256]{1,0:T(8,128)(2,1)S(1)}, u32[]{:S(2)}, u32[]{:S(2)}) collective-permute-start(bf16[128,256]{1,0:T(8,128)(2,1)S(1)} %get-tuple-element.71), channel_id=1, source_target_pairs={{0,2},{1,3},{2,0},{3,1},{4,6},{5,7},{6,4},{7,5},{8,10},{9,11},{10,... | collective-permute-start | bytes 196616 | tf_op jit(solution)/shard_map/ppermute | solution.py:38
  101.4 1.7 %collective-permute-start.22 = (bf16[128,256]{1,0:T(8,128)(2,1)S(1)}, bf16[128,256]{1,0:T(8,128)(2,1)S(1)}, u32[]{:S(2)}, u32[]{:S(2)}) collective-permute-start(bf16[128,256]{1,0:T(8,128)(2,1)S(1)} %get-tuple-element.72), channel_id=1, source_target_pairs={{0,3},{1,2},{2,1},{3,0},{4,7},{5,6},{6,5},{7,4},{8,11},{9,10},{10,... | collective-permute-start | bytes 196616 | tf_op jit(solution)/shard_map/ppermute | solution.py:38
  103.3 2.7 %collective-permute-done.21.refs_6_ = bf16[128,256]{1,0:T(8,128)(2,1)S(1)} collective-permute-done((bf16[128,256]{1,0:T(8,128)(2,1)S(1)}, bf16[128,256]{1,0:T(8,128)(2,1)S(1)}, u32[]{:S(2)}, u32[]{:S(2)}) %collective-permute-start.21) | collective-permute-done | bytes 65568 | tf_op jit(solution)/shard_map/ppermute | solution.py:38
  106.0 1.5 collective-permute-done.22.refs_7_
  107.6 2.1 %shard_map.74 = (bf16[128,256]{1,0:T(8,128)(2,1)S(1)}, f32[4,128,256]{2,1,0:T(8,128)S(1)}, bf16[4,128,256]{2,1,0:T(8,128)(2,1)S(1)}, bf16[4,128,256]{2,1,0:T(8,128)(2,1)S(1)}, f32[12,128,256]{2,1,0:T(8,128)S(1)}) custom-call(s32[12]{0:T(128)S(1)} %get-tuple-element.51.loc, s32[12]{0:T(128)S(1)} %get-tuple-element.52.used, ...), custom_call_target="tpu_custom_call", output_to_operand_aliasing={{4}: (14, {})} | custom-call | flops 402653 | bytes 1572 | tf_op jit(solution)/shard_map/pallas_call | solution.py:56
  112.0 2.1 %collective-permute-start.30 = (bf16[128,256]{1,0:T(8,128)(2,1)S(1)}, bf16[128,256]{1,0:T(8,128)(2,1)S(1)}, u32[]{:S(2)}, u32[]{:S(2)}) collective-permute-start(bf16[128,256]{1,0:T(8,128)(2,1)S(1)} %get-tuple-element.77.refs_0_.refs_8_.refs_13_), channel_id=1, source_target_pairs={{0,3},{1,2},{2,1},{3,0},{4,7},{5,6},{6,5},{7,4},{8,11},{9,10},{10,... | collective-permute-start | bytes 196616 | tf_op jit(solution)/shard_map/ppermute | solution.py:38
  114.1 2.1 %collective-permute-start.34 = (bf16[4,128,256]{2,1,0:T(8,128)(2,1)S(1)}, bf16[4,128,256]{2,1,0:T(8,128)(2,1)S(1)}, u32[]{:S(2)}, u32[]{:S(2)}) collective-permute-start(bf16[4,128,256]{2,1,0:T(8,128)(2,1)S(1)} %get-tuple-element.83), channel_id=1, source_target_pairs={{0,28},{4,8},{8,4},{12,16},{16,12},{20,24},{24,20},{28,0},{1,29},{... | collective-permute-start | bytes 786440 | tf_op jit(solution)/shard_map/ppermute | solution.py:33
  116.2 2.8 %collective-permute-done.29 = bf16[128,256]{1,0:T(8,128)(2,1)S(1)} collective-permute-done((bf16[128,256]{1,0:T(8,128)(2,1)S(1)}, bf16[128,256]{1,0:T(8,128)(2,1)S(1)}, u32[]{:S(2)}, u32[]{:S(2)}) %collective-permute-start.29) | collective-permute-done | bytes 65568 | tf_op jit(solution)/shard_map/ppermute | solution.py:38
  119.2 1.9 %collective-permute-start.32 = (bf16[4,128,256]{2,1,0:T(8,128)(2,1)S(1)}, bf16[4,128,256]{2,1,0:T(8,128)(2,1)S(1)}, u32[]{:S(2)}, u32[]{:S(2)}) collective-permute-start(bf16[4,128,256]{2,1,0:T(8,128)(2,1)S(1)} %pad_maximum_fusion.1), channel_id=1, source_target_pairs={{0,28},{4,8},{8,4},{12,16},{16,12},{20,24},{24,20},{28,0},{1,29},{... | collective-permute-start | bytes 786440 | tf_op jit(solution)/shard_map/ppermute | solution.py:33
  121.1 1.9 %shard_map.75 = (f32[12,128,256]{2,1,0:T(8,128)S(1)}, f32[1,128,256]{2,1,0:T(8,128)S(1)}, f32[1,128,256]{2,1,0:T(8,128)S(1)}) custom-call(s32[12]{0:T(128)S(1)} %get-tuple-element.51.loc, s32[12]{0:T(128)S(1)} %get-tuple-element.52.used, bf16[12,8,256,256]{3,2,1,0:T(8,128)(2,1)S(1)} %copy-done, ...), custom_call_target="tpu_custom_call", output_to_operand_aliasing={{0}: (8, {})} | custom-call | flops 603979 | bytes 4718 | tf_op jit(solution)/shard_map/pallas_call | solution.py:56
  124.1 1.9 %collective-permute-start.36 = (bf16[128,256]{1,0:T(8,128)(2,1)S(1)}, bf16[128,256]{1,0:T(8,128)(2,1)S(1)}, u32[]{:S(2)}, u32[]{:S(2)}) collective-permute-start(bf16[128,256]{1,0:T(8,128)(2,1)S(1)} %get-tuple-element.86), channel_id=1, source_target_pairs={{0,2},{1,3},{2,0},{3,1},{4,6},{5,7},{6,4},{7,5},{8,10},{9,11},{10,... | collective-permute-start | bytes 196616 | tf_op jit(solution)/shard_map/ppermute | solution.py:38
  126.0 2.0 %collective-permute-start.37 = (bf16[128,256]{1,0:T(8,128)(2,1)S(1)}, bf16[128,256]{1,0:T(8,128)(2,1)S(1)}, u32[]{:S(2)}, u32[]{:S(2)}) collective-permute-start(bf16[128,256]{1,0:T(8,128)(2,1)S(1)} %get-tuple-element.87), channel_id=1, source_target_pairs={{0,3},{1,2},{2,1},{3,0},{4,7},{5,6},{6,5},{7,4},{8,11},{9,10},{10,... | collective-permute-start | bytes 196616 | tf_op jit(solution)/shard_map/ppermute | solution.py:38
  128.1 4.6 %collective-permute-done.36.refs_6_ = bf16[128,256]{1,0:T(8,128)(2,1)S(1)} collective-permute-done((bf16[128,256]{1,0:T(8,128)(2,1)S(1)}, bf16[128,256]{1,0:T(8,128)(2,1)S(1)}, u32[]{:S(2)}, u32[]{:S(2)}) %collective-permute-start.36) | collective-permute-done | bytes 65568 | tf_op jit(solution)/shard_map/ppermute | solution.py:38
  132.7 2.1 %shard_map.78 = (bf16[128,256]{1,0:T(8,128)(2,1)S(1)}, f32[4,128,256]{2,1,0:T(8,128)S(1)}, bf16[4,128,256]{2,1,0:T(8,128)(2,1)S(1)}, bf16[4,128,256]{2,1,0:T(8,128)(2,1)S(1)}, f32[12,128,256]{2,1,0:T(8,128)S(1)}) custom-call(s32[12]{0:T(128)S(1)} %get-tuple-element.51.loc, s32[12]{0:T(128)S(1)} %get-tuple-element.52.used, ...), custom_call_target="tpu_custom_call", output_to_operand_aliasing={{4}: (14, {})} | custom-call | flops 402653 | bytes 1572 | tf_op jit(solution)/shard_map/pallas_call | solution.py:56
  134.8 2.1 %collective-permute-start.45 = (bf16[128,256]{1,0:T(8,128)(2,1)S(1)}, bf16[128,256]{1,0:T(8,128)(2,1)S(1)}, u32[]{:S(2)}, u32[]{:S(2)}) collective-permute-start(bf16[128,256]{1,0:T(8,128)(2,1)S(1)} %get-tuple-element.96.refs_8_.refs_14_), channel_id=1, source_target_pairs={{0,3},{1,2},{2,1},{3,0},{4,7},{5,6},{6,5},{7,4},{8,11},{9,10},{10,... | collective-permute-start | bytes 196616 | tf_op jit(solution)/shard_map/ppermute | solution.py:38
  137.2 2.0 %collective-permute-start.44 = (bf16[128,256]{1,0:T(8,128)(2,1)S(1)}, bf16[128,256]{1,0:T(8,128)(2,1)S(1)}, u32[]{:S(2)}, u32[]{:S(2)}) collective-permute-start(bf16[128,256]{1,0:T(8,128)(2,1)S(1)} %get-tuple-element.96.refs_8_.refs_14_), channel_id=1, source_target_pairs={{0,2},{1,3},{2,0},{3,1},{4,6},{5,7},{6,4},{7,5},{8,10},{9,11},{10,... | collective-permute-start | bytes 196616 | tf_op jit(solution)/shard_map/ppermute | solution.py:38
  139.3 1.2 collective-permute-start.39
  142.9 2.3 %collective-permute-start.47 = (bf16[4,128,256]{2,1,0:T(8,128)(2,1)S(1)}, bf16[4,128,256]{2,1,0:T(8,128)(2,1)S(1)}, u32[]{:S(2)}, u32[]{:S(2)}) collective-permute-start(bf16[4,128,256]{2,1,0:T(8,128)(2,1)S(1)} %pad_maximum_fusion.2), channel_id=1, source_target_pairs={{0,28},{4,8},{8,4},{12,16},{16,12},{20,24},{24,20},{28,0},{1,29},{... | collective-permute-start | bytes 786440 | tf_op jit(solution)/shard_map/ppermute | solution.py:33
  145.2 1.2 shard_map.76.refs_0_
  146.5 2.3 %collective-permute-done.39.odd = bf16[4,128,256]{2,1,0:T(8,128)(2,1)S(1)} collective-permute-done((bf16[4,128,256]{2,1,0:T(8,128)(2,1)S(1)}, bf16[4,128,256]{2,1,0:T(8,128)(2,1)S(1)}, u32[]{:S(2)}, u32[]{:S(2)}) %collective-permute-start.39) | collective-permute-done | bytes 262176 | tf_op jit(solution)/shard_map/ppermute | solution.py:33
  149.5 2.0 %collective-permute-start.41 = (bf16[128,256]{1,0:T(8,128)(2,1)S(1)}, bf16[128,256]{1,0:T(8,128)(2,1)S(1)}, u32[]{:S(2)}, u32[]{:S(2)}) collective-permute-start(bf16[128,256]{1,0:T(8,128)(2,1)S(1)} %get-tuple-element.94), channel_id=1, source_target_pairs={{0,2},{1,3},{2,0},{3,1},{4,6},{5,7},{6,4},{7,5},{8,10},{9,11},{10,... | collective-permute-start | bytes 196616 | tf_op jit(solution)/shard_map/ppermute | solution.py:38
  151.5 1.8 %collective-permute-start.42 = (bf16[128,256]{1,0:T(8,128)(2,1)S(1)}, bf16[128,256]{1,0:T(8,128)(2,1)S(1)}, u32[]{:S(2)}, u32[]{:S(2)}) collective-permute-start(bf16[128,256]{1,0:T(8,128)(2,1)S(1)} %get-tuple-element.95), channel_id=1, source_target_pairs={{0,3},{1,2},{2,1},{3,0},{4,7},{5,6},{6,5},{7,4},{8,11},{9,10},{10,... | collective-permute-start | bytes 196616 | tf_op jit(solution)/shard_map/ppermute | solution.py:38
  154.4 2.4 %collective-permute-done.41.refs_6_ = bf16[128,256]{1,0:T(8,128)(2,1)S(1)} collective-permute-done((bf16[128,256]{1,0:T(8,128)(2,1)S(1)}, bf16[128,256]{1,0:T(8,128)(2,1)S(1)}, u32[]{:S(2)}, u32[]{:S(2)}) %collective-permute-start.41) | collective-permute-done | bytes 65568 | tf_op jit(solution)/shard_map/ppermute | solution.py:38
  157.6 2.1 %shard_map.80 = bf16[4,256,128]{2,1,0:T(8,128)(2,1)} custom-call(s32[12]{0:T(128)S(1)} %get-tuple-element.51.loc, s32[12]{0:T(128)S(1)} %get-tuple-element.52.used, f32[1,128,256]{2,1,0:T(8,128)S(1)} %shard_map.76.refs_0_, f32[128,256]{1,0:T(8,128)S(1)} %get-tuple-element.92.refs_1_, bf16[4,128,256]{2,1,0:T(8,128)(2,1)S(1)} %shard_map.70.refs_2_, ...), custom_call_target="tpu_custom_call" | custom-call | flops 402653 | bytes 1572 | tf_op jit(solution)/shard_map/pallas_call | solution.py:56
  (86 shorter events, 20.9 us)
Async XLA Ops:
  3.9 22.8 %collective-permute-start = (bf16[8,128,256]{2,1,0:T(8,128)(2,1)S(1)}, bf16[8,128,256]{2,1,0:T(8,128)(2,1)S(1)}, u32[]{:S(2)}, u32[]{:S(2)}) collective-permute-start(bf16[8,128,256]{2,1,0:T(8,128)(2,1)S(1)} %get-tuple-element.53.refs_0_.hist), channel_id=1, source_target_pairs={{0,1},{1,0},{2,3},{3,2},{4,5},{5,4},{6,7},{7,6},{8,9},{9,8},{10,11... | collective-permute-start | bytes 1572872 | tf_op jit(solution)/shard_map/ppermute | solution.py:38
  7.0 20.4 %collective-permute-start.2 = (bf16[8,128,256]{2,1,0:T(8,128)(2,1)S(1)}, bf16[8,128,256]{2,1,0:T(8,128)(2,1)S(1)}, u32[]{:S(2)}, u32[]{:S(2)}) collective-permute-start(bf16[8,128,256]{2,1,0:T(8,128)(2,1)S(1)} %get-tuple-element.53.refs_0_.hist), channel_id=1, source_target_pairs={{1,2},{2,1},{5,6},{6,5},{9,10},{10,9},{13,14},{14,13},{17,18},{18,... | collective-permute-start | bytes 1572872 | tf_op jit(solution)/shard_map/ppermute | solution.py:48
  7.7 24.8 %collective-permute-start.6 = (bf16[8,128,256]{2,1,0:T(8,128)(2,1)S(1)}, bf16[8,128,256]{2,1,0:T(8,128)(2,1)S(1)}, u32[]{:S(2)}, u32[]{:S(2)}) collective-permute-start(bf16[8,128,256]{2,1,0:T(8,128)(2,1)S(1)} %get-tuple-element.53.refs_0_.hist), channel_id=1, source_target_pairs={{0,3},{3,0},{4,7},{7,4},{8,11},{11,8},{12,15},{15,12},{16,19},{19,... | collective-permute-start | bytes 1572872 | tf_op jit(solution)/shard_map/ppermute | solution.py:51
  22.9 2.6 %collective-permute-start.13 = (bf16[4,128,256]{2,1,0:T(8,128)(2,1)S(1)}, bf16[4,128,256]{2,1,0:T(8,128)(2,1)S(1)}, u32[]{:S(2)}, u32[]{:S(2)}) collective-permute-start(bf16[4,128,256]{2,1,0:T(8,128)(2,1)S(1)} %get-tuple-element.59), channel_id=1, source_target_pairs={{0,4},{4,0},{8,12},{12,8},{16,20},{20,16},{24,28},{28,24},{1,5},{5... | collective-permute-start | bytes 786440 | tf_op jit(solution)/shard_map/ppermute | solution.py:27
  23.0 9.2 %collective-permute-start.14 = (bf16[4,128,256]{2,1,0:T(8,128)(2,1)S(1)}, bf16[4,128,256]{2,1,0:T(8,128)(2,1)S(1)}, u32[]{:S(2)}, u32[]{:S(2)}) collective-permute-start(bf16[4,128,256]{2,1,0:T(8,128)(2,1)S(1)} %get-tuple-element.60), channel_id=1, source_target_pairs={{0,28},{4,8},{8,4},{12,16},{16,12},{20,24},{24,20},{28,0},{1,29},{... | collective-permute-start | bytes 786440 | tf_op jit(solution)/shard_map/ppermute | solution.py:33
  25.5 17.6 %collective-permute-start.10 = (bf16[8,128,256]{2,1,0:T(8,128)(2,1)S(1)}, bf16[8,128,256]{2,1,0:T(8,128)(2,1)S(1)}, u32[]{:S(2)}, u32[]{:S(2)}) collective-permute-start(bf16[8,128,256]{2,1,0:T(8,128)(2,1)S(1)} %get-tuple-element.53.refs_0_.hist), channel_id=1, source_target_pairs={{0,28},{4,8},{8,4},{12,16},{16,12},{20,24},{24,20},{28,0},{1,29},{... | collective-permute-start | bytes 1572872 | tf_op jit(solution)/shard_map/ppermute | solution.py:33
  26.7 18.2 %collective-permute-start.1 = (bf16[8,128,256]{2,1,0:T(8,128)(2,1)S(1)}, bf16[8,128,256]{2,1,0:T(8,128)(2,1)S(1)}, u32[]{:S(2)}, u32[]{:S(2)}) collective-permute-start(bf16[8,128,256]{2,1,0:T(8,128)(2,1)S(1)} %collective-permute-done.refs_3_), channel_id=1, source_target_pairs={{1,2},{2,1},{5,6},{6,5},{9,10},{10,9},{13,14},{14,13},{17,18},{18,... | collective-permute-start | bytes 1572872 | tf_op jit(solution)/shard_map/ppermute | solution.py:50
  27.4 19.8 %collective-permute-start.3 = (bf16[8,128,256]{2,1,0:T(8,128)(2,1)S(1)}, bf16[8,128,256]{2,1,0:T(8,128)(2,1)S(1)}, u32[]{:S(2)}, u32[]{:S(2)}) collective-permute-start(bf16[8,128,256]{2,1,0:T(8,128)(2,1)S(1)} %collective-permute-done.2), channel_id=1, source_target_pairs={{1,0},{2,3},{5,4},{6,7},{9,8},{10,11},{13,12},{14,15},{17,16},{18,... | collective-permute-start | bytes 1572872 | tf_op jit(solution)/shard_map/ppermute | solution.py:49
  32.2 15.2 %collective-permute-start.9 = (bf16[8,128,256]{2,1,0:T(8,128)(2,1)S(1)}, bf16[8,128,256]{2,1,0:T(8,128)(2,1)S(1)}, u32[]{:S(2)}, u32[]{:S(2)}) collective-permute-start(bf16[8,128,256]{2,1,0:T(8,128)(2,1)S(1)} %get-tuple-element.53.refs_0_.hist), channel_id=1, source_target_pairs={{0,4},{4,0},{8,12},{12,8},{16,20},{20,16},{24,28},{28,24},{1,5},{5... | collective-permute-start | bytes 1572872 | tf_op jit(solution)/shard_map/ppermute | solution.py:27
  32.5 16.6 %collective-permute-start.11 = (bf16[8,128,256]{2,1,0:T(8,128)(2,1)S(1)}, bf16[8,128,256]{2,1,0:T(8,128)(2,1)S(1)}, u32[]{:S(2)}, u32[]{:S(2)}) collective-permute-start(bf16[8,128,256]{2,1,0:T(8,128)(2,1)S(1)} %collective-permute-done.refs_3_), channel_id=1, source_target_pairs={{0,4},{4,0},{8,12},{12,8},{16,20},{20,16},{24,28},{28,24},{1,5},{5... | collective-permute-start | bytes 1572872 | tf_op jit(solution)/shard_map/ppermute | solution.py:27
  43.1 15.1 %collective-permute-start.12 = (bf16[8,128,256]{2,1,0:T(8,128)(2,1)S(1)}, bf16[8,128,256]{2,1,0:T(8,128)(2,1)S(1)}, u32[]{:S(2)}, u32[]{:S(2)}) collective-permute-start(bf16[8,128,256]{2,1,0:T(8,128)(2,1)S(1)} %collective-permute-done.refs_3_), channel_id=1, source_target_pairs={{0,28},{4,8},{8,4},{12,16},{16,12},{20,24},{24,20},{28,0},{1,29},{... | collective-permute-start | bytes 1572872 | tf_op jit(solution)/shard_map/ppermute | solution.py:33
  44.9 14.0 %collective-permute-start.7 = (bf16[8,128,256]{2,1,0:T(8,128)(2,1)S(1)}, bf16[8,128,256]{2,1,0:T(8,128)(2,1)S(1)}, u32[]{:S(2)}, u32[]{:S(2)}) collective-permute-start(bf16[8,128,256]{2,1,0:T(8,128)(2,1)S(1)} %add.7.refs_6_), channel_id=1, source_target_pairs={{0,4},{4,0},{8,12},{12,8},{16,20},{20,16},{24,28},{28,24},{1,5},{5... | collective-permute-start | bytes 1572872 | tf_op jit(solution)/shard_map/ppermute | solution.py:27
  47.3 22.2 %collective-permute-start.8 = (bf16[8,128,256]{2,1,0:T(8,128)(2,1)S(1)}, bf16[8,128,256]{2,1,0:T(8,128)(2,1)S(1)}, u32[]{:S(2)}, u32[]{:S(2)}) collective-permute-start(bf16[8,128,256]{2,1,0:T(8,128)(2,1)S(1)} %add.7.refs_6_), channel_id=1, source_target_pairs={{0,28},{4,8},{8,4},{12,16},{16,12},{20,24},{24,20},{28,0},{1,29},{... | collective-permute-start | bytes 1572872 | tf_op jit(solution)/shard_map/ppermute | solution.py:33
  47.4 29.6 %collective-permute-start.4 = (bf16[8,128,256]{2,1,0:T(8,128)(2,1)S(1)}, bf16[8,128,256]{2,1,0:T(8,128)(2,1)S(1)}, u32[]{:S(2)}, u32[]{:S(2)}) collective-permute-start(bf16[8,128,256]{2,1,0:T(8,128)(2,1)S(1)} %add.6.refs_0_.refs_8_), channel_id=1, source_target_pairs={{0,4},{4,0},{8,12},{12,8},{16,20},{20,16},{24,28},{28,24},{1,5},{5... | collective-permute-start | bytes 1572872 | tf_op jit(solution)/shard_map/ppermute | solution.py:27
  49.1 31.6 %collective-permute-start.5 = (bf16[8,128,256]{2,1,0:T(8,128)(2,1)S(1)}, bf16[8,128,256]{2,1,0:T(8,128)(2,1)S(1)}, u32[]{:S(2)}, u32[]{:S(2)}) collective-permute-start(bf16[8,128,256]{2,1,0:T(8,128)(2,1)S(1)} %add.6.refs_0_.refs_8_), channel_id=1, source_target_pairs={{0,28},{4,8},{8,4},{12,16},{16,12},{20,24},{24,20},{28,0},{1,29},{... | collective-permute-start | bytes 1572872 | tf_op jit(solution)/shard_map/ppermute | solution.py:33
  58.2 18.8 %collective-permute-start.15 = (bf16[128,256]{1,0:T(8,128)(2,1)S(1)}, bf16[128,256]{1,0:T(8,128)(2,1)S(1)}, u32[]{:S(2)}, u32[]{:S(2)}) collective-permute-start(bf16[128,256]{1,0:T(8,128)(2,1)S(1)} %get-tuple-element.62), channel_id=1, source_target_pairs={{0,1},{1,0},{2,3},{3,2},{4,5},{5,4},{6,7},{7,6},{8,9},{9,8},{10,11... | collective-permute-start | bytes 196616 | tf_op jit(solution)/shard_map/ppermute | solution.py:38
  58.9 18.1 %collective-permute-start.16 = (bf16[128,256]{1,0:T(8,128)(2,1)S(1)}, bf16[128,256]{1,0:T(8,128)(2,1)S(1)}, u32[]{:S(2)}, u32[]{:S(2)}) collective-permute-start(bf16[128,256]{1,0:T(8,128)(2,1)S(1)} %get-tuple-element.63), channel_id=1, source_target_pairs={{0,2},{1,3},{2,0},{3,1},{4,6},{5,7},{6,4},{7,5},{8,10},{9,11},{10,... | collective-permute-start | bytes 196616 | tf_op jit(solution)/shard_map/ppermute | solution.py:38
  69.4 7.6 %collective-permute-start.17 = (bf16[128,256]{1,0:T(8,128)(2,1)S(1)}, bf16[128,256]{1,0:T(8,128)(2,1)S(1)}, u32[]{:S(2)}, u32[]{:S(2)}) collective-permute-start(bf16[128,256]{1,0:T(8,128)(2,1)S(1)} %get-tuple-element.64), channel_id=1, source_target_pairs={{0,3},{1,2},{2,1},{3,0},{4,7},{5,6},{6,5},{7,4},{8,11},{9,10},{10,... | collective-permute-start | bytes 196616 | tf_op jit(solution)/shard_map/ppermute | solution.py:38
  85.3 5.3 %collective-permute-start.23 = (bf16[128,256]{1,0:T(8,128)(2,1)S(1)}, bf16[128,256]{1,0:T(8,128)(2,1)S(1)}, u32[]{:S(2)}, u32[]{:S(2)}) collective-permute-start(bf16[128,256]{1,0:T(8,128)(2,1)S(1)} %get-tuple-element.73.refs_0_.refs_8_.refs_1_.refs_12_), channel_id=1, source_target_pairs={{0,1},{1,0},{2,3},{3,2},{4,5},{5,4},{6,7},{7,6},{8,9},{9,8},{10,11... | collective-permute-start | bytes 196616 | tf_op jit(solution)/shard_map/ppermute | solution.py:38
  85.4 5.7 %collective-permute-start.24 = (bf16[128,256]{1,0:T(8,128)(2,1)S(1)}, bf16[128,256]{1,0:T(8,128)(2,1)S(1)}, u32[]{:S(2)}, u32[]{:S(2)}) collective-permute-start(bf16[128,256]{1,0:T(8,128)(2,1)S(1)} %get-tuple-element.73.refs_0_.refs_8_.refs_1_.refs_12_), channel_id=1, source_target_pairs={{0,2},{1,3},{2,0},{3,1},{4,6},{5,7},{6,4},{7,5},{8,10},{9,11},{10,... | collective-permute-start | bytes 196616 | tf_op jit(solution)/shard_map/ppermute | solution.py:38
  86.8 6.1 %collective-permute-start.25 = (bf16[128,256]{1,0:T(8,128)(2,1)S(1)}, bf16[128,256]{1,0:T(8,128)(2,1)S(1)}, u32[]{:S(2)}, u32[]{:S(2)}) collective-permute-start(bf16[128,256]{1,0:T(8,128)(2,1)S(1)} %get-tuple-element.73.refs_0_.refs_8_.refs_1_.refs_12_), channel_id=1, source_target_pairs={{0,3},{1,2},{2,1},{3,0},{4,7},{5,6},{6,5},{7,4},{8,11},{9,10},{10,... | collective-permute-start | bytes 196616 | tf_op jit(solution)/shard_map/ppermute | solution.py:38
  89.8 8.7 %collective-permute-start.18 = (bf16[4,128,256]{2,1,0:T(8,128)(2,1)S(1)}, bf16[4,128,256]{2,1,0:T(8,128)(2,1)S(1)}, u32[]{:S(2)}, u32[]{:S(2)}) collective-permute-start(bf16[4,128,256]{2,1,0:T(8,128)(2,1)S(1)} %get-tuple-element.67), channel_id=1, source_target_pairs={{0,4},{4,0},{8,12},{12,8},{16,20},{20,16},{24,28},{28,24},{1,5},{5... | collective-permute-start | bytes 786440 | tf_op jit(solution)/shard_map/ppermute | solution.py:27
  89.8 8.7 %collective-permute-start.19 = (bf16[4,128,256]{2,1,0:T(8,128)(2,1)S(1)}, bf16[4,128,256]{2,1,0:T(8,128)(2,1)S(1)}, u32[]{:S(2)}, u32[]{:S(2)}) collective-permute-start(bf16[4,128,256]{2,1,0:T(8,128)(2,1)S(1)} %get-tuple-element.68), channel_id=1, source_target_pairs={{0,28},{4,8},{8,4},{12,16},{16,12},{20,24},{24,20},{28,0},{1,29},{... | collective-permute-start | bytes 786440 | tf_op jit(solution)/shard_map/ppermute | solution.py:33
  92.9 10.2 %collective-permute-start.26 = (bf16[4,128,256]{2,1,0:T(8,128)(2,1)S(1)}, bf16[4,128,256]{2,1,0:T(8,128)(2,1)S(1)}, u32[]{:S(2)}, u32[]{:S(2)}) collective-permute-start(bf16[4,128,256]{2,1,0:T(8,128)(2,1)S(1)} %pad_maximum_fusion), channel_id=1, source_target_pairs={{0,4},{4,0},{8,12},{12,8},{16,20},{20,16},{24,28},{28,24},{1,5},{5... | collective-permute-start | bytes 786440 | tf_op jit(solution)/shard_map/ppermute | solution.py:27
  93.0 10.3 %collective-permute-start.27 = (bf16[4,128,256]{2,1,0:T(8,128)(2,1)S(1)}, bf16[4,128,256]{2,1,0:T(8,128)(2,1)S(1)}, u32[]{:S(2)}, u32[]{:S(2)}) collective-permute-start(bf16[4,128,256]{2,1,0:T(8,128)(2,1)S(1)} %pad_maximum_fusion), channel_id=1, source_target_pairs={{0,28},{4,8},{8,4},{12,16},{16,12},{20,24},{24,20},{28,0},{1,29},{... | collective-permute-start | bytes 786440 | tf_op jit(solution)/shard_map/ppermute | solution.py:33
  98.6 4.7 %collective-permute-start.20 = (bf16[128,256]{1,0:T(8,128)(2,1)S(1)}, bf16[128,256]{1,0:T(8,128)(2,1)S(1)}, u32[]{:S(2)}, u32[]{:S(2)}) collective-permute-start(bf16[128,256]{1,0:T(8,128)(2,1)S(1)} %get-tuple-element.70), channel_id=1, source_target_pairs={{0,1},{1,0},{2,3},{3,2},{4,5},{5,4},{6,7},{7,6},{8,9},{9,8},{10,11... | collective-permute-start | bytes 196616 | tf_op jit(solution)/shard_map/ppermute | solution.py:38
  98.7 7.4 %collective-permute-start.21 = (bf16[128,256]{1,0:T(8,128)(2,1)S(1)}, bf16[128,256]{1,0:T(8,128)(2,1)S(1)}, u32[]{:S(2)}, u32[]{:S(2)}) collective-permute-start(bf16[128,256]{1,0:T(8,128)(2,1)S(1)} %get-tuple-element.71), channel_id=1, source_target_pairs={{0,2},{1,3},{2,0},{3,1},{4,6},{5,7},{6,4},{7,5},{8,10},{9,11},{10,... | collective-permute-start | bytes 196616 | tf_op jit(solution)/shard_map/ppermute | solution.py:38
  101.4 6.2 %collective-permute-start.22 = (bf16[128,256]{1,0:T(8,128)(2,1)S(1)}, bf16[128,256]{1,0:T(8,128)(2,1)S(1)}, u32[]{:S(2)}, u32[]{:S(2)}) collective-permute-start(bf16[128,256]{1,0:T(8,128)(2,1)S(1)} %get-tuple-element.72), channel_id=1, source_target_pairs={{0,3},{1,2},{2,1},{3,0},{4,7},{5,6},{6,5},{7,4},{8,11},{9,10},{10,... | collective-permute-start | bytes 196616 | tf_op jit(solution)/shard_map/ppermute | solution.py:38
  109.7 6.6 %collective-permute-start.28 = (bf16[128,256]{1,0:T(8,128)(2,1)S(1)}, bf16[128,256]{1,0:T(8,128)(2,1)S(1)}, u32[]{:S(2)}, u32[]{:S(2)}) collective-permute-start(bf16[128,256]{1,0:T(8,128)(2,1)S(1)} %get-tuple-element.77.refs_0_.refs_8_.refs_13_), channel_id=1, source_target_pairs={{0,1},{1,0},{2,3},{3,2},{4,5},{5,4},{6,7},{7,6},{8,9},{9,8},{10,11... | collective-permute-start | bytes 196616 | tf_op jit(solution)/shard_map/ppermute | solution.py:38
  110.9 8.2 %collective-permute-start.29 = (bf16[128,256]{1,0:T(8,128)(2,1)S(1)}, bf16[128,256]{1,0:T(8,128)(2,1)S(1)}, u32[]{:S(2)}, u32[]{:S(2)}) collective-permute-start(bf16[128,256]{1,0:T(8,128)(2,1)S(1)} %get-tuple-element.77.refs_0_.refs_8_.refs_13_), channel_id=1, source_target_pairs={{0,2},{1,3},{2,0},{3,1},{4,6},{5,7},{6,4},{7,5},{8,10},{9,11},{10,... | collective-permute-start | bytes 196616 | tf_op jit(solution)/shard_map/ppermute | solution.py:38
  112.0 7.1 %collective-permute-start.30 = (bf16[128,256]{1,0:T(8,128)(2,1)S(1)}, bf16[128,256]{1,0:T(8,128)(2,1)S(1)}, u32[]{:S(2)}, u32[]{:S(2)}) collective-permute-start(bf16[128,256]{1,0:T(8,128)(2,1)S(1)} %get-tuple-element.77.refs_0_.refs_8_.refs_13_), channel_id=1, source_target_pairs={{0,3},{1,2},{2,1},{3,0},{4,7},{5,6},{6,5},{7,4},{8,11},{9,10},{10,... | collective-permute-start | bytes 196616 | tf_op jit(solution)/shard_map/ppermute | solution.py:38
  114.1 8.9 %collective-permute-start.33 = (bf16[4,128,256]{2,1,0:T(8,128)(2,1)S(1)}, bf16[4,128,256]{2,1,0:T(8,128)(2,1)S(1)}, u32[]{:S(2)}, u32[]{:S(2)}) collective-permute-start(bf16[4,128,256]{2,1,0:T(8,128)(2,1)S(1)} %get-tuple-element.82), channel_id=1, source_target_pairs={{0,4},{4,0},{8,12},{12,8},{16,20},{20,16},{24,28},{28,24},{1,5},{5... | collective-permute-start | bytes 786440 | tf_op jit(solution)/shard_map/ppermute | solution.py:27
  114.1 9.4 %collective-permute-start.34 = (bf16[4,128,256]{2,1,0:T(8,128)(2,1)S(1)}, bf16[4,128,256]{2,1,0:T(8,128)(2,1)S(1)}, u32[]{:S(2)}, u32[]{:S(2)}) collective-permute-start(bf16[4,128,256]{2,1,0:T(8,128)(2,1)S(1)} %get-tuple-element.83), channel_id=1, source_target_pairs={{0,28},{4,8},{8,4},{12,16},{16,12},{20,24},{24,20},{28,0},{1,29},{... | collective-permute-start | bytes 786440 | tf_op jit(solution)/shard_map/ppermute | solution.py:33
  119.1 13.5 %collective-permute-start.31 = (bf16[4,128,256]{2,1,0:T(8,128)(2,1)S(1)}, bf16[4,128,256]{2,1,0:T(8,128)(2,1)S(1)}, u32[]{:S(2)}, u32[]{:S(2)}) collective-permute-start(bf16[4,128,256]{2,1,0:T(8,128)(2,1)S(1)} %pad_maximum_fusion.1), channel_id=1, source_target_pairs={{0,4},{4,0},{8,12},{12,8},{16,20},{20,16},{24,28},{28,24},{1,5},{5... | collective-permute-start | bytes 786440 | tf_op jit(solution)/shard_map/ppermute | solution.py:27
  119.2 13.5 %collective-permute-start.32 = (bf16[4,128,256]{2,1,0:T(8,128)(2,1)S(1)}, bf16[4,128,256]{2,1,0:T(8,128)(2,1)S(1)}, u32[]{:S(2)}, u32[]{:S(2)}) collective-permute-start(bf16[4,128,256]{2,1,0:T(8,128)(2,1)S(1)} %pad_maximum_fusion.1), channel_id=1, source_target_pairs={{0,28},{4,8},{8,4},{12,16},{16,12},{20,24},{24,20},{28,0},{1,29},{... | collective-permute-start | bytes 786440 | tf_op jit(solution)/shard_map/ppermute | solution.py:33
  123.6 4.5 %collective-permute-start.35 = (bf16[128,256]{1,0:T(8,128)(2,1)S(1)}, bf16[128,256]{1,0:T(8,128)(2,1)S(1)}, u32[]{:S(2)}, u32[]{:S(2)}) collective-permute-start(bf16[128,256]{1,0:T(8,128)(2,1)S(1)} %get-tuple-element.85), channel_id=1, source_target_pairs={{0,1},{1,0},{2,3},{3,2},{4,5},{5,4},{6,7},{7,6},{8,9},{9,8},{10,11... | collective-permute-start | bytes 196616 | tf_op jit(solution)/shard_map/ppermute | solution.py:38
  124.1 8.6 %collective-permute-start.36 = (bf16[128,256]{1,0:T(8,128)(2,1)S(1)}, bf16[128,256]{1,0:T(8,128)(2,1)S(1)}, u32[]{:S(2)}, u32[]{:S(2)}) collective-permute-start(bf16[128,256]{1,0:T(8,128)(2,1)S(1)} %get-tuple-element.86), channel_id=1, source_target_pairs={{0,2},{1,3},{2,0},{3,1},{4,6},{5,7},{6,4},{7,5},{8,10},{9,11},{10,... | collective-permute-start | bytes 196616 | tf_op jit(solution)/shard_map/ppermute | solution.py:38
  126.0 6.6 %collective-permute-start.37 = (bf16[128,256]{1,0:T(8,128)(2,1)S(1)}, bf16[128,256]{1,0:T(8,128)(2,1)S(1)}, u32[]{:S(2)}, u32[]{:S(2)}) collective-permute-start(bf16[128,256]{1,0:T(8,128)(2,1)S(1)} %get-tuple-element.87), channel_id=1, source_target_pairs={{0,3},{1,2},{2,1},{3,0},{4,7},{5,6},{6,5},{7,4},{8,11},{9,10},{10,... | collective-permute-start | bytes 196616 | tf_op jit(solution)/shard_map/ppermute | solution.py:38
  134.8 6.7 %collective-permute-start.45 = (bf16[128,256]{1,0:T(8,128)(2,1)S(1)}, bf16[128,256]{1,0:T(8,128)(2,1)S(1)}, u32[]{:S(2)}, u32[]{:S(2)}) collective-permute-start(bf16[128,256]{1,0:T(8,128)(2,1)S(1)} %get-tuple-element.96.refs_8_.refs_14_), channel_id=1, source_target_pairs={{0,3},{1,2},{2,1},{3,0},{4,7},{5,6},{6,5},{7,4},{8,11},{9,10},{10,... | collective-permute-start | bytes 196616 | tf_op jit(solution)/shard_map/ppermute | solution.py:38
  136.9 5.2 %collective-permute-start.43 = (bf16[128,256]{1,0:T(8,128)(2,1)S(1)}, bf16[128,256]{1,0:T(8,128)(2,1)S(1)}, u32[]{:S(2)}, u32[]{:S(2)}) collective-permute-start(bf16[128,256]{1,0:T(8,128)(2,1)S(1)} %get-tuple-element.96.refs_8_.refs_14_), channel_id=1, source_target_pairs={{0,1},{1,0},{2,3},{3,2},{4,5},{5,4},{6,7},{7,6},{8,9},{9,8},{10,11... | collective-permute-start | bytes 196616 | tf_op jit(solution)/shard_map/ppermute | solution.py:38
  137.2 5.6 %collective-permute-start.44 = (bf16[128,256]{1,0:T(8,128)(2,1)S(1)}, bf16[128,256]{1,0:T(8,128)(2,1)S(1)}, u32[]{:S(2)}, u32[]{:S(2)}) collective-permute-start(bf16[128,256]{1,0:T(8,128)(2,1)S(1)} %get-tuple-element.96.refs_8_.refs_14_), channel_id=1, source_target_pairs={{0,2},{1,3},{2,0},{3,1},{4,6},{5,7},{6,4},{7,5},{8,10},{9,11},{10,... | collective-permute-start | bytes 196616 | tf_op jit(solution)/shard_map/ppermute | solution.py:38
  139.3 7.2 %collective-permute-start.38 = (bf16[4,128,256]{2,1,0:T(8,128)(2,1)S(1)}, bf16[4,128,256]{2,1,0:T(8,128)(2,1)S(1)}, u32[]{:S(2)}, u32[]{:S(2)}) collective-permute-start(bf16[4,128,256]{2,1,0:T(8,128)(2,1)S(1)} %get-tuple-element.90), channel_id=1, source_target_pairs={{0,4},{4,0},{8,12},{12,8},{16,20},{20,16},{24,28},{28,24},{1,5},{5... | collective-permute-start | bytes 786440 | tf_op jit(solution)/shard_map/ppermute | solution.py:27
  139.3 9.5 %collective-permute-start.39 = (bf16[4,128,256]{2,1,0:T(8,128)(2,1)S(1)}, bf16[4,128,256]{2,1,0:T(8,128)(2,1)S(1)}, u32[]{:S(2)}, u32[]{:S(2)}) collective-permute-start(bf16[4,128,256]{2,1,0:T(8,128)(2,1)S(1)} %get-tuple-element.91), channel_id=1, source_target_pairs={{0,28},{4,8},{8,4},{12,16},{16,12},{20,24},{24,20},{28,0},{1,29},{... | collective-permute-start | bytes 786440 | tf_op jit(solution)/shard_map/ppermute | solution.py:33
  142.8 10.5 %collective-permute-start.46 = (bf16[4,128,256]{2,1,0:T(8,128)(2,1)S(1)}, bf16[4,128,256]{2,1,0:T(8,128)(2,1)S(1)}, u32[]{:S(2)}, u32[]{:S(2)}) collective-permute-start(bf16[4,128,256]{2,1,0:T(8,128)(2,1)S(1)} %pad_maximum_fusion.2), channel_id=1, source_target_pairs={{0,4},{4,0},{8,12},{12,8},{16,20},{20,16},{24,28},{28,24},{1,5},{5... | collective-permute-start | bytes 786440 | tf_op jit(solution)/shard_map/ppermute | solution.py:27
  142.9 11.4 %collective-permute-start.47 = (bf16[4,128,256]{2,1,0:T(8,128)(2,1)S(1)}, bf16[4,128,256]{2,1,0:T(8,128)(2,1)S(1)}, u32[]{:S(2)}, u32[]{:S(2)}) collective-permute-start(bf16[4,128,256]{2,1,0:T(8,128)(2,1)S(1)} %pad_maximum_fusion.2), channel_id=1, source_target_pairs={{0,28},{4,8},{8,4},{12,16},{16,12},{20,24},{24,20},{28,0},{1,29},{... | collective-permute-start | bytes 786440 | tf_op jit(solution)/shard_map/ppermute | solution.py:33
  148.8 5.5 %collective-permute-start.40 = (bf16[128,256]{1,0:T(8,128)(2,1)S(1)}, bf16[128,256]{1,0:T(8,128)(2,1)S(1)}, u32[]{:S(2)}, u32[]{:S(2)}) collective-permute-start(bf16[128,256]{1,0:T(8,128)(2,1)S(1)} %get-tuple-element.93), channel_id=1, source_target_pairs={{0,1},{1,0},{2,3},{3,2},{4,5},{5,4},{6,7},{7,6},{8,9},{9,8},{10,11... | collective-permute-start | bytes 196616 | tf_op jit(solution)/shard_map/ppermute | solution.py:38
  149.5 7.3 %collective-permute-start.41 = (bf16[128,256]{1,0:T(8,128)(2,1)S(1)}, bf16[128,256]{1,0:T(8,128)(2,1)S(1)}, u32[]{:S(2)}, u32[]{:S(2)}) collective-permute-start(bf16[128,256]{1,0:T(8,128)(2,1)S(1)} %get-tuple-element.94), channel_id=1, source_target_pairs={{0,2},{1,3},{2,0},{3,1},{4,6},{5,7},{6,4},{7,5},{8,10},{9,11},{10,... | collective-permute-start | bytes 196616 | tf_op jit(solution)/shard_map/ppermute | solution.py:38
  151.5 6.2 %collective-permute-start.42 = (bf16[128,256]{1,0:T(8,128)(2,1)S(1)}, bf16[128,256]{1,0:T(8,128)(2,1)S(1)}, u32[]{:S(2)}, u32[]{:S(2)}) collective-permute-start(bf16[128,256]{1,0:T(8,128)(2,1)S(1)} %get-tuple-element.95), channel_id=1, source_target_pairs={{0,3},{1,2},{2,1},{3,0},{4,7},{5,6},{6,5},{7,4},{8,11},{9,10},{10,... | collective-permute-start | bytes 196616 | tf_op jit(solution)/shard_map/ppermute | solution.py:38
  (6 other events, 40.6 us)

commit v3 on v2

--- a/solution.py
+++ b/solution.py
@@ -103,39 +103,29 @@
 
 def enter_body(cuts, codes, lags, history, out, loc, used):
     turn_body(history, out)
-
-    @pl.when(pl.program_id(0) == 0)
-    def _():
-        odd_region = lax.rem(lax.axis_index("region"), 2)
-        own_cut = lax.axis_index("cuts")
-        for p in range(codes.shape[0]):
-            used[p] = lags[p]
-            shift = lax.div(codes[p], cuts) - 1
-            side = jnp.where((shift == 1) == (odd_region == 0), 1, 2)
-            side = jnp.where(shift == 0, 0, side)
-            loc[p] = side * cuts + (lax.rem(codes[p], cuts) ^ own_cut)
+    odd_region = lax.rem(lax.axis_index("region"), 2)
+    own_cut = lax.axis_index("cuts")
+    for p in range(codes.shape[0]):
+        used[p] = lags[p]
+        shift = lax.div(codes[p], cuts) - 1
+        side = jnp.where((shift == 1) == (odd_region == 0), 1, 2)
+        side = jnp.where(shift == 0, 0, side)
+        loc[p] = side * cuts + (lax.rem(codes[p], cuts) ^ own_cut)
 
 
 def enter(codes, lags, history, cuts):
     count, panels, rows = history.shape
-    parts = 2 if count % 2 == 0 else 1
     return pl.pallas_call(
         functools.partial(enter_body, cuts),
         name="enter",
-        grid=(parts,),
-        in_specs=[
-            IN_SMEM,
-            IN_SMEM,
-            pl.BlockSpec((count // parts, panels, rows), lambda i: (i, 0, 0)),
-        ],
-        out_specs=(pl.BlockSpec((count // parts, rows, panels), lambda i: (i, 0, 0)), IN_SMEM, IN_SMEM),
+        in_specs=[IN_SMEM, IN_SMEM, IN_VMEM],
+        out_specs=(IN_VMEM, IN_SMEM, IN_SMEM),
         out_shape=(
             jax.ShapeDtypeStruct((count, rows, panels), history.dtype),
             jax.ShapeDtypeStruct(codes.shape, codes.dtype),
             jax.ShapeDtypeStruct(lags.shape, lags.dtype),
         ),
         compiler_params=pltpu.CompilerParams(vmem_limit_bytes=8 * 1024 * 1024),
-        cost_estimate=pl.CostEstimate(flops=0, bytes_accessed=4096, transcendentals=0),
     )(codes, lags, history)
 
 
@@ -454,9 +444,11 @@
         odd = odd_exchange(piece)
         even = even_exchange(piece)
         blocks.update({j: piece, cuts + j: even, 2 * cuts + j: odd})
-    *_, j_late, j_final = pieces
-    final = {slot: blocks.pop(slot) for slot in range(j_final, 3 * cuts, cuts)}
-    late = {slot: blocks.pop(slot) for slot in (cuts + j_late, 2 * cuts + j_late)}
+    *_, j_final = pieces
+    final = {slot: blocks.pop(slot) for slot in range(cuts + j_final, 3 * cuts, cuts)}
+    early = {*range(cuts), cuts, 2 * cuts} - {j_final}
+    late = {slot: block for slot, block in blocks.items() if slot not in early}
+    blocks = {slot: block for slot, block in blocks.items() if slot in early}
     sums = history_front(loc, used, lag_kernels, blocks, None, 0, steps)
     sums = history_front(loc, used, lag_kernels, late, sums, 0, steps)
     ahead = {n: (sums, steps - 1 - n) for n in range(steps)}

time: 160 us -> 165 us (1.031)
  waiting for transfers between devices: 61.7 us -> 64.8 us
  starting transfers between devices: 56.7 us -> 59.7 us
    ppermute x11, waiting for transfers between devices: 38.8 us -> 27.6 us  [odd_exchange(): return lax.ppermute(value, 'region', route)]
    ppermute x1, waiting for transfers between devices: 2.29 us -> 9.48 us  [cut_pieces(): far = lax.ppermute(across, 'cuts', outward)]
    ppermute x1, waiting for transfers between devices: 0.21 us -> 6.62 us  [cut_pieces(): ends = lax.ppermute(value, 'cuts', [(0, 3), (3, 0)])]
    ppermute x22, starting transfers between devices: 33.1 us -> 38.4 us  [cut_exchange(): return lax.ppermute(value, 'cuts', [(i, i ^ j) for i in range(count)])]
  transfers between devices with their start and end apart: 48 -> 48, of which waited for: 23 -> 20; matrix products, arithmetic and copies ran while one was open for 0% -> 0% of each run, Pallas kernels for 16% -> 15%
where the time goes in v3:
time: 165 us
  waiting for transfers between devices  64.8 us (39%)
  starting transfers between devices  59.7 us (36%)
  Pallas kernels  36.6 us (22%)
  local copies, waits for them, and re-layouts  2.98 us (2%)
    ppermute x22, starting transfers between devices, cut_exchange(): return lax.ppermute(value, 'cuts', [(i, i ^ j) for i in range(count)])  38.4 us
    pallas_call x17, Pallas kernels, call(): pl.pallas_call(body, out_shape=outs, in_specs=[IN_SMEM] * len(scalars) +...  35.2 us
    ppermute x11, waiting for transfers between devices, odd_exchange(): return lax.ppermute(value, 'region', route)  27.6 us
    ppermute x22, waiting for transfers between devices, cut_exchange(): return lax.ppermute(value, 'cuts', [(i, i ^ j) for i in range(count)])  21.1 us
    ppermute x11, starting transfers between devices, odd_exchange(): return lax.ppermute(value, 'region', route)  14.4 us
    ppermute x1, waiting for transfers between devices, cut_pieces(): far = lax.ppermute(across, 'cuts', outward)  9.48 us
    ppermute x1, waiting for transfers between devices, cut_pieces(): ends = lax.ppermute(value, 'cuts', [(0, 3), (3, 0)])  6.62 us
  transfers between devices with their start and end apart: 48, of which 20 were waited for; matrix products, arithmetic and copies ran while one was open for 0% of the time, Pallas kernels for 15%

profile of v3, /device:TPU:0, one launch (start us, length us, event | category | flops | bytes accessed | tf_op | source)
XLA Modules:
  0.0 164.9 jit_solution(94132933011506591)
XLA Ops:
  2.4 1.3 enter.1
  4.4 5.9 %collective-permute-start = (bf16[8,128,256]{2,1,0:T(8,128)(2,1)S(1)}, bf16[8,128,256]{2,1,0:T(8,128)(2,1)S(1)}, u32[]{:S(2)}, u32[]{:S(2)}) collective-permute-start(bf16[8,128,256]{2,1,0:T(8,128)(2,1)S(1)} %get-tuple-element.53.refs_0_.hist), channel_id=1, source_target_pairs={{0,1},{1,0},{2,3},{3,2},{4,5},{5,4},{6,7},{7,6},{8,9},{9,8},{10,11... | collective-permute-start | bytes 1572872 | tf_op jit(solution)/shard_map/ppermute | solution.py:38
  10.3 3.2 %collective-permute-start.8 = (bf16[8,128,256]{2,1,0:T(8,128)(2,1)S(1)}, bf16[8,128,256]{2,1,0:T(8,128)(2,1)S(1)}, u32[]{:S(2)}, u32[]{:S(2)}) collective-permute-start(bf16[8,128,256]{2,1,0:T(8,128)(2,1)S(1)} %get-tuple-element.53.refs_0_.hist), channel_id=1, source_target_pairs={{0,3},{3,0},{4,7},{7,4},{8,11},{11,8},{12,15},{15,12},{16,19},{19,... | collective-permute-start | bytes 1572872 | tf_op jit(solution)/shard_map/ppermute | solution.py:51
  13.6 5.8 %shard_map.67 = (f32[12,128,256]{2,1,0:T(8,128)S(1)}, f32[12,128,256]{2,1,0:T(8,128)S(1)}, f32[12,128,256]{2,1,0:T(8,128)S(1)}, f32[12,128,256]{2,1,0:T(8,128)S(1)}) custom-call(s32[12]{0:T(128)S(1)} %get-tuple-element.51.loc, s32[12]{0:T(128)S(1)} %get-tuple-element.52.used, bf16[8,128,256]{2,1,0:T(8,128)(2,1)S(1)} %get-tuple-element.53.refs_0_.hist, ...), custom_call_target="tpu_custom_call" | custom-call | flops 3221225 | bytes 12582 | tf_op jit(solution)/shard_map/pallas_call | solution.py:56
  20.0 4.4 %shard_map.68 = (f32[12,128,256]{2,1,0:T(8,128)S(1)}, f32[12,128,256]{2,1,0:T(8,128)S(1)}, f32[12,128,256]{2,1,0:T(8,128)S(1)}, f32[12,128,256]{2,1,0:T(8,128)S(...) custom-call(s32[12]{0:T(128)S(1)} %get-tuple-element.51.loc, ...), custom_call_target="tpu_custom_call", output_to_operand_aliasing={{0}: (4, {}), {1}: (5, {}), {2}: (6, {}), {3}: (7, {})} | custom-call | flops 3221225 | bytes 12582 | tf_op jit(solution)/shard_map/pallas_call | solution.py:56
  24.5 2.6 %collective-permute-start.14 = (bf16[4,128,256]{2,1,0:T(8,128)(2,1)S(1)}, bf16[4,128,256]{2,1,0:T(8,128)(2,1)S(1)}, u32[]{:S(2)}, u32[]{:S(2)}) collective-permute-start(bf16[4,128,256]{2,1,0:T(8,128)(2,1)S(1)} %get-tuple-element.60), channel_id=1, source_target_pairs={{0,28},{4,8},{8,4},{12,16},{16,12},{20,24},{24,20},{28,0},{1,29},{... | collective-permute-start | bytes 786440 | tf_op jit(solution)/shard_map/ppermute | solution.py:33
  27.7 6.6 %collective-permute-done.8 = bf16[8,128,256]{2,1,0:T(8,128)(2,1)S(1)} collective-permute-done((bf16[8,128,256]{2,1,0:T(8,128)(2,1)S(1)}, bf16[8,128,256]{2,1,0:T(8,128)(2,1)S(1)}, u32[]{:S(2)}, u32[]{:S(2)}) %collective-permute-start.8) | collective-permute-done | bytes 524320 | tf_op jit(solution)/shard_map/ppermute | solution.py:51
  34.3 1.5 collective-permute-start.3
  36.8 1.9 %collective-permute-start.10 = (bf16[8,128,256]{2,1,0:T(8,128)(2,1)S(1)}, bf16[8,128,256]{2,1,0:T(8,128)(2,1)S(1)}, u32[]{:S(2)}, u32[]{:S(2)}) collective-permute-start(bf16[8,128,256]{2,1,0:T(8,128)(2,1)S(1)} %add.7.refs_4_), channel_id=1, source_target_pairs={{0,28},{4,8},{8,4},{12,16},{16,12},{20,24},{24,20},{28,0},{1,29},{... | collective-permute-start | bytes 1572872 | tf_op jit(solution)/shard_map/ppermute | solution.py:33
  39.2 9.5 %collective-permute-done.3 = bf16[8,128,256]{2,1,0:T(8,128)(2,1)S(1)} collective-permute-done((bf16[8,128,256]{2,1,0:T(8,128)(2,1)S(1)}, bf16[8,128,256]{2,1,0:T(8,128)(2,1)S(1)}, u32[]{:S(2)}, u32[]{:S(2)}) %collective-permute-start.3) | collective-permute-done | bytes 524320 | tf_op jit(solution)/shard_map/ppermute | solution.py:49
  48.9 2.2 %collective-permute-done.12.refs_2_ = bf16[8,128,256]{2,1,0:T(8,128)(2,1)S(1)} collective-permute-done((bf16[8,128,256]{2,1,0:T(8,128)(2,1)S(1)}, bf16[8,128,256]{2,1,0:T(8,128)(2,1)S(1)}, u32[]{:S(2)}, u32[]{:S(2)}) %collective-permute-start.12) | collective-permute-done | bytes 524320 | tf_op jit(solution)/shard_map/ppermute | solution.py:33
  51.1 11.2 %collective-permute-done.10.refs_3_ = bf16[8,128,256]{2,1,0:T(8,128)(2,1)S(1)} collective-permute-done((bf16[8,128,256]{2,1,0:T(8,128)(2,1)S(1)}, bf16[8,128,256]{2,1,0:T(8,128)(2,1)S(1)}, u32[]{:S(2)}, u32[]{:S(2)}) %collective-permute-start.10) | collective-permute-done | bytes 524320 | tf_op jit(solution)/shard_map/ppermute | solution.py:33
  63.0 2.2 %collective-permute-start.15 = (bf16[128,256]{1,0:T(8,128)(2,1)S(1)}, bf16[128,256]{1,0:T(8,128)(2,1)S(1)}, u32[]{:S(2)}, u32[]{:S(2)}) collective-permute-start(bf16[128,256]{1,0:T(8,128)(2,1)S(1)} %get-tuple-element.62), channel_id=1, source_target_pairs={{0,1},{1,0},{2,3},{3,2},{4,5},{5,4},{6,7},{7,6},{8,9},{9,8},{10,11... | collective-permute-start | bytes 196616 | tf_op jit(solution)/shard_map/ppermute | solution.py:38
  66.3 7.3 %collective-permute-done.7.refs_1_ = bf16[8,128,256]{2,1,0:T(8,128)(2,1)S(1)} collective-permute-done((bf16[8,128,256]{2,1,0:T(8,128)(2,1)S(1)}, bf16[8,128,256]{2,1,0:T(8,128)(2,1)S(1)}, u32[]{:S(2)}, u32[]{:S(2)}) %collective-permute-start.7) | collective-permute-done | bytes 524320 | tf_op jit(solution)/shard_map/ppermute | solution.py:33
  73.5 2.5 %collective-permute-start.17 = (bf16[128,256]{1,0:T(8,128)(2,1)S(1)}, bf16[128,256]{1,0:T(8,128)(2,1)S(1)}, u32[]{:S(2)}, u32[]{:S(2)}) collective-permute-start(bf16[128,256]{1,0:T(8,128)(2,1)S(1)} %get-tuple-element.64), channel_id=1, source_target_pairs={{0,3},{1,2},{2,1},{3,0},{4,7},{5,6},{6,5},{7,4},{8,11},{9,10},{10,... | collective-permute-start | bytes 196616 | tf_op jit(solution)/shard_map/ppermute | solution.py:38
  76.2 3.0 %shard_map.64.refs_5_ = f32[4,128,256]{2,1,0:T(8,128)S(1)} custom-call(s32[12]{0:T(128)S(1)} %get-tuple-element.51.loc, s32[12]{0:T(128)S(1)} %get-tuple-element.52.used, bf16[12,8,256,256]{3,2,1,0:T(8,128)(2,1)S(1)} %copy-done, bf16[8,128,256]{2,1,0:T(8,128)(2,1)S(1)} %get-tuple-element.53.refs_0_.hist, ...), custom_call_target="tpu_custom_call" | custom-call | flops 2684354 | bytes 5242 | tf_op jit(solution)/shard_map/pallas_call | solution.py:56
  79.1 3.6 %shard_map.65.refs_2_.refs_0_ = f32[4,128,256]{2,1,0:T(8,128)S(1)} custom-call(s32[12]{0:T(128)S(1)} %get-tuple-element.51.loc, s32[12]{0:T(128)S(1)} %get-tuple-element.52.used, bf16[12,8,256,256]{3,2,1,0:T(8,128)(2,1)S(1)} %copy-done, bf16[8,128,256]{2,1,0:T(8,128)(2,1)S(1)} %collective-permute-done.6.refs_0_, ...), custom_call_target="tpu_custom_call" | custom-call | flops 2684354 | bytes 5242 | tf_op jit(solution)/shard_map/pallas_call | solution.py:56
  82.8 2.0 %collective-permute-done.5.refs_1_.refs_9_ = bf16[8,128,256]{2,1,0:T(8,128)(2,1)S(1)} collective-permute-done((bf16[8,128,256]{2,1,0:T(8,128)(2,1)S(1)}, bf16[8,128,256]{2,1,0:T(8,128)(2,1)S(1)}, u32[]{:S(2)}, u32[]{:S(2)}) %collective-permute-start.5) | collective-permute-done | bytes 524320 | tf_op jit(solution)/shard_map/ppermute | solution.py:33
  84.8 4.0 %shard_map.71 = (bf16[128,256]{1,0:T(8,128)(2,1)S(1)}, f32[4,128,256]{2,1,0:T(8,128)S(1)}, bf16[4,128,256]{2,1,0:T(8,128)(2,1)S(1)}, bf16[4,128,256]{2,1,0:T(8,128)(2,1)S(1)}, f32[12,128,256]{2,1,0:T(8,128)S(1)}) custom-call(s32[12]{0:T(128)S(1)} %get-tuple-element.51.loc, s32[12]{0:T(128)S(1)} %get-tuple-element.52.used, ...), custom_call_target="tpu_custom_call", output_to_operand_aliasing={{4}: (12, {})} | custom-call | flops 402653 | bytes 1572 | tf_op jit(solution)/shard_map/pallas_call | solution.py:56
  90.1 1.8 %collective-permute-start.24 = (bf16[128,256]{1,0:T(8,128)(2,1)S(1)}, bf16[128,256]{1,0:T(8,128)(2,1)S(1)}, u32[]{:S(2)}, u32[]{:S(2)}) collective-permute-start(bf16[128,256]{1,0:T(8,128)(2,1)S(1)} %get-tuple-element.73.refs_0_.refs_8_.refs_1_.refs_12_), channel_id=1, source_target_pairs={{0,2},{1,3},{2,0},{3,1},{4,6},{5,7},{6,4},{7,5},{8,10},{9,11},{10,... | collective-permute-start | bytes 196616 | tf_op jit(solution)/shard_map/ppermute | solution.py:38
  91.9 1.4 collective-permute-start.25
  93.2 1.3 collective-permute-start.19
  94.6 2.7 %collective-permute-done.24 = bf16[128,256]{1,0:T(8,128)(2,1)S(1)} collective-permute-done((bf16[128,256]{1,0:T(8,128)(2,1)S(1)}, bf16[128,256]{1,0:T(8,128)(2,1)S(1)}, u32[]{:S(2)}, u32[]{:S(2)}) %collective-permute-start.24) | collective-permute-done | bytes 65568 | tf_op jit(solution)/shard_map/ppermute | solution.py:38
  100.4 3.4 %shard_map.66.refs_0_.refs_6_.refs_7_ = f32[3,128,256]{2,1,0:T(8,128)S(1)} custom-call(s32[12]{0:T(128)S(1)} %get-tuple-element.51.loc, s32[12]{0:T(128)S(1)} %get-tuple-element.52.used, bf16[12,8,256,256]{3,2,1,0:T(8,128)(2,1)S(1)} %copy-done, bf16[8,128,256]{2,1,0:T(8,128)(2,1)S(1)} %collective-permute-done.4.refs_0_.refs_8_, ...), custom_call_target="tpu_custom_call" | custom-call | flops 805306 | bytes 2097 | tf_op jit(solution)/shard_map/pallas_call | solution.py:56
  104.0 2.9 %collective-permute-start.21 = (bf16[128,256]{1,0:T(8,128)(2,1)S(1)}, bf16[128,256]{1,0:T(8,128)(2,1)S(1)}, u32[]{:S(2)}, u32[]{:S(2)}) collective-permute-start(bf16[128,256]{1,0:T(8,128)(2,1)S(1)} %get-tuple-element.71), channel_id=1, source_target_pairs={{0,2},{1,3},{2,0},{3,1},{4,6},{5,7},{6,4},{7,5},{8,10},{9,11},{10,... | collective-permute-start | bytes 196616 | tf_op jit(solution)/shard_map/ppermute | solution.py:38
  106.9 1.5 collective-permute-start.22
  108.4 3.2 %collective-permute-done.21.refs_6_ = bf16[128,256]{1,0:T(8,128)(2,1)S(1)} collective-permute-done((bf16[128,256]{1,0:T(8,128)(2,1)S(1)}, bf16[128,256]{1,0:T(8,128)(2,1)S(1)}, u32[]{:S(2)}, u32[]{:S(2)}) %collective-permute-start.21) | collective-permute-done | bytes 65568 | tf_op jit(solution)/shard_map/ppermute | solution.py:38
  111.6 1.4 collective-permute-done.22.refs_7_
  113.1 2.1 %shard_map.74 = (bf16[128,256]{1,0:T(8,128)(2,1)S(1)}, f32[4,128,256]{2,1,0:T(8,128)S(1)}, bf16[4,128,256]{2,1,0:T(8,128)(2,1)S(1)}, bf16[4,128,256]{2,1,0:T(8,128)(2,1)S(1)}, f32[12,128,256]{2,1,0:T(8,128)S(1)}) custom-call(s32[12]{0:T(128)S(1)} %get-tuple-element.51.loc, s32[12]{0:T(128)S(1)} %get-tuple-element.52.used, ...), custom_call_target="tpu_custom_call", output_to_operand_aliasing={{4}: (14, {})} | custom-call | flops 402653 | bytes 1572 | tf_op jit(solution)/shard_map/pallas_call | solution.py:56
  117.3 2.3 %collective-permute-start.30 = (bf16[128,256]{1,0:T(8,128)(2,1)S(1)}, bf16[128,256]{1,0:T(8,128)(2,1)S(1)}, u32[]{:S(2)}, u32[]{:S(2)}) collective-permute-start(bf16[128,256]{1,0:T(8,128)(2,1)S(1)} %get-tuple-element.77.refs_0_.refs_8_.refs_13_), channel_id=1, source_target_pairs={{0,3},{1,2},{2,1},{3,0},{4,7},{5,6},{6,5},{7,4},{8,11},{9,10},{10,... | collective-permute-start | bytes 196616 | tf_op jit(solution)/shard_map/ppermute | solution.py:38
  119.6 1.6 collective-permute-start.34
  121.2 2.9 %collective-permute-done.29 = bf16[128,256]{1,0:T(8,128)(2,1)S(1)} collective-permute-done((bf16[128,256]{1,0:T(8,128)(2,1)S(1)}, bf16[128,256]{1,0:T(8,128)(2,1)S(1)}, u32[]{:S(2)}, u32[]{:S(2)}) %collective-permute-start.29) | collective-permute-done | bytes 65568 | tf_op jit(solution)/shard_map/ppermute | solution.py:38
  124.2 1.7 %collective-permute-start.32 = (bf16[4,128,256]{2,1,0:T(8,128)(2,1)S(1)}, bf16[4,128,256]{2,1,0:T(8,128)(2,1)S(1)}, u32[]{:S(2)}, u32[]{:S(2)}) collective-permute-start(bf16[4,128,256]{2,1,0:T(8,128)(2,1)S(1)} %pad_maximum_fusion.1), channel_id=1, source_target_pairs={{0,28},{4,8},{8,4},{12,16},{16,12},{20,24},{24,20},{28,0},{1,29},{... | collective-permute-start | bytes 786440 | tf_op jit(solution)/shard_map/ppermute | solution.py:33
  126.0 1.9 %shard_map.75 = (f32[12,128,256]{2,1,0:T(8,128)S(1)}, f32[1,128,256]{2,1,0:T(8,128)S(1)}, f32[1,128,256]{2,1,0:T(8,128)S(1)}) custom-call(s32[12]{0:T(128)S(1)} %get-tuple-element.51.loc, s32[12]{0:T(128)S(1)} %get-tuple-element.52.used, bf16[12,8,256,256]{3,2,1,0:T(8,128)(2,1)S(1)} %copy-done, ...), custom_call_target="tpu_custom_call", output_to_operand_aliasing={{0}: (8, {})} | custom-call | flops 603979 | bytes 4718 | tf_op jit(solution)/shard_map/pallas_call | solution.py:56
  129.3 2.0 %collective-permute-start.36 = (bf16[128,256]{1,0:T(8,128)(2,1)S(1)}, bf16[128,256]{1,0:T(8,128)(2,1)S(1)}, u32[]{:S(2)}, u32[]{:S(2)}) collective-permute-start(bf16[128,256]{1,0:T(8,128)(2,1)S(1)} %get-tuple-element.86), channel_id=1, source_target_pairs={{0,2},{1,3},{2,0},{3,1},{4,6},{5,7},{6,4},{7,5},{8,10},{9,11},{10,... | collective-permute-start | bytes 196616 | tf_op jit(solution)/shard_map/ppermute | solution.py:38
  131.3 2.3 %collective-permute-start.37 = (bf16[128,256]{1,0:T(8,128)(2,1)S(1)}, bf16[128,256]{1,0:T(8,128)(2,1)S(1)}, u32[]{:S(2)}, u32[]{:S(2)}) collective-permute-start(bf16[128,256]{1,0:T(8,128)(2,1)S(1)} %get-tuple-element.87), channel_id=1, source_target_pairs={{0,3},{1,2},{2,1},{3,0},{4,7},{5,6},{6,5},{7,4},{8,11},{9,10},{10,... | collective-permute-start | bytes 196616 | tf_op jit(solution)/shard_map/ppermute | solution.py:38
  134.2 3.4 %collective-permute-done.36.refs_6_ = bf16[128,256]{1,0:T(8,128)(2,1)S(1)} collective-permute-done((bf16[128,256]{1,0:T(8,128)(2,1)S(1)}, bf16[128,256]{1,0:T(8,128)(2,1)S(1)}, u32[]{:S(2)}, u32[]{:S(2)}) %collective-permute-start.36) | collective-permute-done | bytes 65568 | tf_op jit(solution)/shard_map/ppermute | solution.py:38
  137.7 2.1 %shard_map.78 = (bf16[128,256]{1,0:T(8,128)(2,1)S(1)}, f32[4,128,256]{2,1,0:T(8,128)S(1)}, bf16[4,128,256]{2,1,0:T(8,128)(2,1)S(1)}, bf16[4,128,256]{2,1,0:T(8,128)(2,1)S(1)}, f32[12,128,256]{2,1,0:T(8,128)S(1)}) custom-call(s32[12]{0:T(128)S(1)} %get-tuple-element.51.loc, s32[12]{0:T(128)S(1)} %get-tuple-element.52.used, ...), custom_call_target="tpu_custom_call", output_to_operand_aliasing={{4}: (14, {})} | custom-call | flops 402653 | bytes 1572 | tf_op jit(solution)/shard_map/pallas_call | solution.py:56
  139.8 2.2 %collective-permute-start.45 = (bf16[128,256]{1,0:T(8,128)(2,1)S(1)}, bf16[128,256]{1,0:T(8,128)(2,1)S(1)}, u32[]{:S(2)}, u32[]{:S(2)}) collective-permute-start(bf16[128,256]{1,0:T(8,128)(2,1)S(1)} %get-tuple-element.96.refs_8_.refs_14_), channel_id=1, source_target_pairs={{0,3},{1,2},{2,1},{3,0},{4,7},{5,6},{6,5},{7,4},{8,11},{9,10},{10,... | collective-permute-start | bytes 196616 | tf_op jit(solution)/shard_map/ppermute | solution.py:38
  142.0 2.2 %collective-permute-start.44 = (bf16[128,256]{1,0:T(8,128)(2,1)S(1)}, bf16[128,256]{1,0:T(8,128)(2,1)S(1)}, u32[]{:S(2)}, u32[]{:S(2)}) collective-permute-start(bf16[128,256]{1,0:T(8,128)(2,1)S(1)} %get-tuple-element.96.refs_8_.refs_14_), channel_id=1, source_target_pairs={{0,2},{1,3},{2,0},{3,1},{4,6},{5,7},{6,4},{7,5},{8,10},{9,11},{10,... | collective-permute-start | bytes 196616 | tf_op jit(solution)/shard_map/ppermute | solution.py:38
  144.9 1.3 collective-permute-done.45
  146.2 1.3 collective-permute-done.43
  147.6 2.3 %collective-permute-start.47 = (bf16[4,128,256]{2,1,0:T(8,128)(2,1)S(1)}, bf16[4,128,256]{2,1,0:T(8,128)(2,1)S(1)}, u32[]{:S(2)}, u32[]{:S(2)}) collective-permute-start(bf16[4,128,256]{2,1,0:T(8,128)(2,1)S(1)} %pad_maximum_fusion.2), channel_id=1, source_target_pairs={{0,28},{4,8},{8,4},{12,16},{16,12},{20,24},{24,20},{28,0},{1,29},{... | collective-permute-start | bytes 786440 | tf_op jit(solution)/shard_map/ppermute | solution.py:33
  151.1 2.7 %collective-permute-done.39.odd = bf16[4,128,256]{2,1,0:T(8,128)(2,1)S(1)} collective-permute-done((bf16[4,128,256]{2,1,0:T(8,128)(2,1)S(1)}, bf16[4,128,256]{2,1,0:T(8,128)(2,1)S(1)}, u32[]{:S(2)}, u32[]{:S(2)}) %collective-permute-start.39) | collective-permute-done | bytes 262176 | tf_op jit(solution)/shard_map/ppermute | solution.py:33
  154.3 2.4 %collective-permute-start.41 = (bf16[128,256]{1,0:T(8,128)(2,1)S(1)}, bf16[128,256]{1,0:T(8,128)(2,1)S(1)}, u32[]{:S(2)}, u32[]{:S(2)}) collective-permute-start(bf16[128,256]{1,0:T(8,128)(2,1)S(1)} %get-tuple-element.94), channel_id=1, source_target_pairs={{0,2},{1,3},{2,0},{3,1},{4,6},{5,7},{6,4},{7,5},{8,10},{9,11},{10,... | collective-permute-start | bytes 196616 | tf_op jit(solution)/shard_map/ppermute | solution.py:38
  156.6 1.7 %collective-permute-start.42 = (bf16[128,256]{1,0:T(8,128)(2,1)S(1)}, bf16[128,256]{1,0:T(8,128)(2,1)S(1)}, u32[]{:S(2)}, u32[]{:S(2)}) collective-permute-start(bf16[128,256]{1,0:T(8,128)(2,1)S(1)} %get-tuple-element.95), channel_id=1, source_target_pairs={{0,3},{1,2},{2,1},{3,0},{4,7},{5,6},{6,5},{7,4},{8,11},{9,10},{10,... | collective-permute-start | bytes 196616 | tf_op jit(solution)/shard_map/ppermute | solution.py:38
  159.3 2.6 %collective-permute-done.41.refs_6_ = bf16[128,256]{1,0:T(8,128)(2,1)S(1)} collective-permute-done((bf16[128,256]{1,0:T(8,128)(2,1)S(1)}, bf16[128,256]{1,0:T(8,128)(2,1)S(1)}, u32[]{:S(2)}, u32[]{:S(2)}) %collective-permute-start.41) | collective-permute-done | bytes 65568 | tf_op jit(solution)/shard_map/ppermute | solution.py:38
  162.8 2.1 %shard_map.80 = bf16[4,256,128]{2,1,0:T(8,128)(2,1)} custom-call(s32[12]{0:T(128)S(1)} %get-tuple-element.51.loc, s32[12]{0:T(128)S(1)} %get-tuple-element.52.used, f32[1,128,256]{2,1,0:T(8,128)S(1)} %shard_map.76.refs_0_, f32[128,256]{1,0:T(8,128)S(1)} %get-tuple-element.92.refs_1_, bf16[4,128,256]{2,1,0:T(8,128)(2,1)S(1)} %shard_map.70.refs_2_, ...), custom_call_target="tpu_custom_call" | custom-call | flops 402653 | bytes 1572 | tf_op jit(solution)/shard_map/pallas_call | solution.py:56
  (86 shorter events, 21.0 us)
Async XLA Ops:
  3.7 23.3 %collective-permute-start.2 = (bf16[8,128,256]{2,1,0:T(8,128)(2,1)S(1)}, bf16[8,128,256]{2,1,0:T(8,128)(2,1)S(1)}, u32[]{:S(2)}, u32[]{:S(2)}) collective-permute-start(bf16[8,128,256]{2,1,0:T(8,128)(2,1)S(1)} %get-tuple-element.53.refs_0_.hist), channel_id=1, source_target_pairs={{1,2},{2,1},{5,6},{6,5},{9,10},{10,9},{13,14},{14,13},{17,18},{18,... | collective-permute-start | bytes 1572872 | tf_op jit(solution)/shard_map/ppermute | solution.py:48
  4.4 22.6 %collective-permute-start = (bf16[8,128,256]{2,1,0:T(8,128)(2,1)S(1)}, bf16[8,128,256]{2,1,0:T(8,128)(2,1)S(1)}, u32[]{:S(2)}, u32[]{:S(2)}) collective-permute-start(bf16[8,128,256]{2,1,0:T(8,128)(2,1)S(1)} %get-tuple-element.53.refs_0_.hist), channel_id=1, source_target_pairs={{0,1},{1,0},{2,3},{3,2},{4,5},{5,4},{6,7},{7,6},{8,9},{9,8},{10,11... | collective-permute-start | bytes 1572872 | tf_op jit(solution)/shard_map/ppermute | solution.py:38
  10.3 24.0 %collective-permute-start.8 = (bf16[8,128,256]{2,1,0:T(8,128)(2,1)S(1)}, bf16[8,128,256]{2,1,0:T(8,128)(2,1)S(1)}, u32[]{:S(2)}, u32[]{:S(2)}) collective-permute-start(bf16[8,128,256]{2,1,0:T(8,128)(2,1)S(1)} %get-tuple-element.53.refs_0_.hist), channel_id=1, source_target_pairs={{0,3},{3,0},{4,7},{7,4},{8,11},{11,8},{12,15},{15,12},{16,19},{19,... | collective-permute-start | bytes 1572872 | tf_op jit(solution)/shard_map/ppermute | solution.py:51
  24.4 11.6 %collective-permute-start.13 = (bf16[4,128,256]{2,1,0:T(8,128)(2,1)S(1)}, bf16[4,128,256]{2,1,0:T(8,128)(2,1)S(1)}, u32[]{:S(2)}, u32[]{:S(2)}) collective-permute-start(bf16[4,128,256]{2,1,0:T(8,128)(2,1)S(1)} %get-tuple-element.59), channel_id=1, source_target_pairs={{0,4},{4,0},{8,12},{12,8},{16,20},{20,16},{24,28},{28,24},{1,5},{5... | collective-permute-start | bytes 786440 | tf_op jit(solution)/shard_map/ppermute | solution.py:27
  24.5 12.3 %collective-permute-start.14 = (bf16[4,128,256]{2,1,0:T(8,128)(2,1)S(1)}, bf16[4,128,256]{2,1,0:T(8,128)(2,1)S(1)}, u32[]{:S(2)}, u32[]{:S(2)}) collective-permute-start(bf16[4,128,256]{2,1,0:T(8,128)(2,1)S(1)} %get-tuple-element.60), channel_id=1, source_target_pairs={{0,28},{4,8},{8,4},{12,16},{16,12},{20,24},{24,20},{28,0},{1,29},{... | collective-permute-start | bytes 786440 | tf_op jit(solution)/shard_map/ppermute | solution.py:33
  27.0 11.7 %collective-permute-start.11 = (bf16[8,128,256]{2,1,0:T(8,128)(2,1)S(1)}, bf16[8,128,256]{2,1,0:T(8,128)(2,1)S(1)}, u32[]{:S(2)}, u32[]{:S(2)}) collective-permute-start(bf16[8,128,256]{2,1,0:T(8,128)(2,1)S(1)} %get-tuple-element.53.refs_0_.hist), channel_id=1, source_target_pairs={{0,4},{4,0},{8,12},{12,8},{16,20},{20,16},{24,28},{28,24},{1,5},{5... | collective-permute-start | bytes 1572872 | tf_op jit(solution)/shard_map/ppermute | solution.py:27
  27.0 11.7 %collective-permute-start.1 = (bf16[8,128,256]{2,1,0:T(8,128)(2,1)S(1)}, bf16[8,128,256]{2,1,0:T(8,128)(2,1)S(1)}, u32[]{:S(2)}, u32[]{:S(2)}) collective-permute-start(bf16[8,128,256]{2,1,0:T(8,128)(2,1)S(1)} %collective-permute-done.refs_3_), channel_id=1, source_target_pairs={{1,2},{2,1},{5,6},{6,5},{9,10},{10,9},{13,14},{14,13},{17,18},{18,... | collective-permute-start | bytes 1572872 | tf_op jit(solution)/shard_map/ppermute | solution.py:50
  34.3 14.4 %collective-permute-start.3 = (bf16[8,128,256]{2,1,0:T(8,128)(2,1)S(1)}, bf16[8,128,256]{2,1,0:T(8,128)(2,1)S(1)}, u32[]{:S(2)}, u32[]{:S(2)}) collective-permute-start(bf16[8,128,256]{2,1,0:T(8,128)(2,1)S(1)} %collective-permute-done.2), channel_id=1, source_target_pairs={{1,0},{2,3},{5,4},{6,7},{9,8},{10,11},{13,12},{14,15},{17,16},{18,... | collective-permute-start | bytes 1572872 | tf_op jit(solution)/shard_map/ppermute | solution.py:49
  36.0 15.1 %collective-permute-start.12 = (bf16[8,128,256]{2,1,0:T(8,128)(2,1)S(1)}, bf16[8,128,256]{2,1,0:T(8,128)(2,1)S(1)}, u32[]{:S(2)}, u32[]{:S(2)}) collective-permute-start(bf16[8,128,256]{2,1,0:T(8,128)(2,1)S(1)} %get-tuple-element.53.refs_0_.hist), channel_id=1, source_target_pairs={{0,28},{4,8},{8,4},{12,16},{16,12},{20,24},{24,20},{28,0},{1,29},{... | collective-permute-start | bytes 1572872 | tf_op jit(solution)/shard_map/ppermute | solution.py:33
  36.8 25.6 %collective-permute-start.10 = (bf16[8,128,256]{2,1,0:T(8,128)(2,1)S(1)}, bf16[8,128,256]{2,1,0:T(8,128)(2,1)S(1)}, u32[]{:S(2)}, u32[]{:S(2)}) collective-permute-start(bf16[8,128,256]{2,1,0:T(8,128)(2,1)S(1)} %add.7.refs_4_), channel_id=1, source_target_pairs={{0,28},{4,8},{8,4},{12,16},{16,12},{20,24},{24,20},{28,0},{1,29},{... | collective-permute-start | bytes 1572872 | tf_op jit(solution)/shard_map/ppermute | solution.py:33
  38.7 24.3 %collective-permute-start.9 = (bf16[8,128,256]{2,1,0:T(8,128)(2,1)S(1)}, bf16[8,128,256]{2,1,0:T(8,128)(2,1)S(1)}, u32[]{:S(2)}, u32[]{:S(2)}) collective-permute-start(bf16[8,128,256]{2,1,0:T(8,128)(2,1)S(1)} %add.7.refs_4_), channel_id=1, source_target_pairs={{0,4},{4,0},{8,12},{12,8},{16,20},{20,16},{24,28},{28,24},{1,5},{5... | collective-permute-start | bytes 1572872 | tf_op jit(solution)/shard_map/ppermute | solution.py:27
  38.7 26.5 %collective-permute-start.6 = (bf16[8,128,256]{2,1,0:T(8,128)(2,1)S(1)}, bf16[8,128,256]{2,1,0:T(8,128)(2,1)S(1)}, u32[]{:S(2)}, u32[]{:S(2)}) collective-permute-start(bf16[8,128,256]{2,1,0:T(8,128)(2,1)S(1)} %collective-permute-done.refs_3_), channel_id=1, source_target_pairs={{0,4},{4,0},{8,12},{12,8},{16,20},{20,16},{24,28},{28,24},{1,5},{5... | collective-permute-start | bytes 1572872 | tf_op jit(solution)/shard_map/ppermute | solution.py:27
  48.7 24.8 %collective-permute-start.7 = (bf16[8,128,256]{2,1,0:T(8,128)(2,1)S(1)}, bf16[8,128,256]{2,1,0:T(8,128)(2,1)S(1)}, u32[]{:S(2)}, u32[]{:S(2)}) collective-permute-start(bf16[8,128,256]{2,1,0:T(8,128)(2,1)S(1)} %collective-permute-done.refs_3_), channel_id=1, source_target_pairs={{0,28},{4,8},{8,4},{12,16},{16,12},{20,24},{24,20},{28,0},{1,29},{... | collective-permute-start | bytes 1572872 | tf_op jit(solution)/shard_map/ppermute | solution.py:33
  51.1 31.7 %collective-permute-start.4 = (bf16[8,128,256]{2,1,0:T(8,128)(2,1)S(1)}, bf16[8,128,256]{2,1,0:T(8,128)(2,1)S(1)}, u32[]{:S(2)}, u32[]{:S(2)}) collective-permute-start(bf16[8,128,256]{2,1,0:T(8,128)(2,1)S(1)} %add.6.refs_4_), channel_id=1, source_target_pairs={{0,4},{4,0},{8,12},{12,8},{16,20},{20,16},{24,28},{28,24},{1,5},{5... | collective-permute-start | bytes 1572872 | tf_op jit(solution)/shard_map/ppermute | solution.py:27
  62.3 22.5 %collective-permute-start.5 = (bf16[8,128,256]{2,1,0:T(8,128)(2,1)S(1)}, bf16[8,128,256]{2,1,0:T(8,128)(2,1)S(1)}, u32[]{:S(2)}, u32[]{:S(2)}) collective-permute-start(bf16[8,128,256]{2,1,0:T(8,128)(2,1)S(1)} %add.6.refs_4_), channel_id=1, source_target_pairs={{0,28},{4,8},{8,4},{12,16},{16,12},{20,24},{24,20},{28,0},{1,29},{... | collective-permute-start | bytes 1572872 | tf_op jit(solution)/shard_map/ppermute | solution.py:33
  63.0 19.8 %collective-permute-start.15 = (bf16[128,256]{1,0:T(8,128)(2,1)S(1)}, bf16[128,256]{1,0:T(8,128)(2,1)S(1)}, u32[]{:S(2)}, u32[]{:S(2)}) collective-permute-start(bf16[128,256]{1,0:T(8,128)(2,1)S(1)} %get-tuple-element.62), channel_id=1, source_target_pairs={{0,1},{1,0},{2,3},{3,2},{4,5},{5,4},{6,7},{7,6},{8,9},{9,8},{10,11... | collective-permute-start | bytes 196616 | tf_op jit(solution)/shard_map/ppermute | solution.py:38
  65.2 17.6 %collective-permute-start.16 = (bf16[128,256]{1,0:T(8,128)(2,1)S(1)}, bf16[128,256]{1,0:T(8,128)(2,1)S(1)}, u32[]{:S(2)}, u32[]{:S(2)}) collective-permute-start(bf16[128,256]{1,0:T(8,128)(2,1)S(1)} %get-tuple-element.63), channel_id=1, source_target_pairs={{0,2},{1,3},{2,0},{3,1},{4,6},{5,7},{6,4},{7,5},{8,10},{9,11},{10,... | collective-permute-start | bytes 196616 | tf_op jit(solution)/shard_map/ppermute | solution.py:38
  73.5 9.2 %collective-permute-start.17 = (bf16[128,256]{1,0:T(8,128)(2,1)S(1)}, bf16[128,256]{1,0:T(8,128)(2,1)S(1)}, u32[]{:S(2)}, u32[]{:S(2)}) collective-permute-start(bf16[128,256]{1,0:T(8,128)(2,1)S(1)} %get-tuple-element.64), channel_id=1, source_target_pairs={{0,3},{1,2},{2,1},{3,0},{4,7},{5,6},{6,5},{7,4},{8,11},{9,10},{10,... | collective-permute-start | bytes 196616 | tf_op jit(solution)/shard_map/ppermute | solution.py:38
  88.8 5.8 %collective-permute-start.23 = (bf16[128,256]{1,0:T(8,128)(2,1)S(1)}, bf16[128,256]{1,0:T(8,128)(2,1)S(1)}, u32[]{:S(2)}, u32[]{:S(2)}) collective-permute-start(bf16[128,256]{1,0:T(8,128)(2,1)S(1)} %get-tuple-element.73.refs_0_.refs_8_.refs_1_.refs_12_), channel_id=1, source_target_pairs={{0,1},{1,0},{2,3},{3,2},{4,5},{5,4},{6,7},{7,6},{8,9},{9,8},{10,11... | collective-permute-start | bytes 196616 | tf_op jit(solution)/shard_map/ppermute | solution.py:38
  90.1 7.2 %collective-permute-start.24 = (bf16[128,256]{1,0:T(8,128)(2,1)S(1)}, bf16[128,256]{1,0:T(8,128)(2,1)S(1)}, u32[]{:S(2)}, u32[]{:S(2)}) collective-permute-start(bf16[128,256]{1,0:T(8,128)(2,1)S(1)} %get-tuple-element.73.refs_0_.refs_8_.refs_1_.refs_12_), channel_id=1, source_target_pairs={{0,2},{1,3},{2,0},{3,1},{4,6},{5,7},{6,4},{7,5},{8,10},{9,11},{10,... | collective-permute-start | bytes 196616 | tf_op jit(solution)/shard_map/ppermute | solution.py:38
  91.9 6.2 %collective-permute-start.25 = (bf16[128,256]{1,0:T(8,128)(2,1)S(1)}, bf16[128,256]{1,0:T(8,128)(2,1)S(1)}, u32[]{:S(2)}, u32[]{:S(2)}) collective-permute-start(bf16[128,256]{1,0:T(8,128)(2,1)S(1)} %get-tuple-element.73.refs_0_.refs_8_.refs_1_.refs_12_), channel_id=1, source_target_pairs={{0,3},{1,2},{2,1},{3,0},{4,7},{5,6},{6,5},{7,4},{8,11},{9,10},{10,... | collective-permute-start | bytes 196616 | tf_op jit(solution)/shard_map/ppermute | solution.py:38
  93.2 10.6 %collective-permute-start.18 = (bf16[4,128,256]{2,1,0:T(8,128)(2,1)S(1)}, bf16[4,128,256]{2,1,0:T(8,128)(2,1)S(1)}, u32[]{:S(2)}, u32[]{:S(2)}) collective-permute-start(bf16[4,128,256]{2,1,0:T(8,128)(2,1)S(1)} %get-tuple-element.67), channel_id=1, source_target_pairs={{0,4},{4,0},{8,12},{12,8},{16,20},{20,16},{24,28},{28,24},{1,5},{5... | collective-permute-start | bytes 786440 | tf_op jit(solution)/shard_map/ppermute | solution.py:27
  93.2 10.6 %collective-permute-start.19 = (bf16[4,128,256]{2,1,0:T(8,128)(2,1)S(1)}, bf16[4,128,256]{2,1,0:T(8,128)(2,1)S(1)}, u32[]{:S(2)}, u32[]{:S(2)}) collective-permute-start(bf16[4,128,256]{2,1,0:T(8,128)(2,1)S(1)} %get-tuple-element.68), channel_id=1, source_target_pairs={{0,28},{4,8},{8,4},{12,16},{16,12},{20,24},{24,20},{28,0},{1,29},{... | collective-permute-start | bytes 786440 | tf_op jit(solution)/shard_map/ppermute | solution.py:33
  98.1 10.3 %collective-permute-start.26 = (bf16[4,128,256]{2,1,0:T(8,128)(2,1)S(1)}, bf16[4,128,256]{2,1,0:T(8,128)(2,1)S(1)}, u32[]{:S(2)}, u32[]{:S(2)}) collective-permute-start(bf16[4,128,256]{2,1,0:T(8,128)(2,1)S(1)} %pad_maximum_fusion), channel_id=1, source_target_pairs={{0,4},{4,0},{8,12},{12,8},{16,20},{20,16},{24,28},{28,24},{1,5},{5... | collective-permute-start | bytes 786440 | tf_op jit(solution)/shard_map/ppermute | solution.py:27
  98.2 10.2 %collective-permute-start.27 = (bf16[4,128,256]{2,1,0:T(8,128)(2,1)S(1)}, bf16[4,128,256]{2,1,0:T(8,128)(2,1)S(1)}, u32[]{:S(2)}, u32[]{:S(2)}) collective-permute-start(bf16[4,128,256]{2,1,0:T(8,128)(2,1)S(1)} %pad_maximum_fusion), channel_id=1, source_target_pairs={{0,28},{4,8},{8,4},{12,16},{16,12},{20,24},{24,20},{28,0},{1,29},{... | collective-permute-start | bytes 786440 | tf_op jit(solution)/shard_map/ppermute | solution.py:33
  103.9 4.5 %collective-permute-start.20 = (bf16[128,256]{1,0:T(8,128)(2,1)S(1)}, bf16[128,256]{1,0:T(8,128)(2,1)S(1)}, u32[]{:S(2)}, u32[]{:S(2)}) collective-permute-start(bf16[128,256]{1,0:T(8,128)(2,1)S(1)} %get-tuple-element.70), channel_id=1, source_target_pairs={{0,1},{1,0},{2,3},{3,2},{4,5},{5,4},{6,7},{7,6},{8,9},{9,8},{10,11... | collective-permute-start | bytes 196616 | tf_op jit(solution)/shard_map/ppermute | solution.py:38
  104.0 7.6 %collective-permute-start.21 = (bf16[128,256]{1,0:T(8,128)(2,1)S(1)}, bf16[128,256]{1,0:T(8,128)(2,1)S(1)}, u32[]{:S(2)}, u32[]{:S(2)}) collective-permute-start(bf16[128,256]{1,0:T(8,128)(2,1)S(1)} %get-tuple-element.71), channel_id=1, source_target_pairs={{0,2},{1,3},{2,0},{3,1},{4,6},{5,7},{6,4},{7,5},{8,10},{9,11},{10,... | collective-permute-start | bytes 196616 | tf_op jit(solution)/shard_map/ppermute | solution.py:38
  106.9 6.2 %collective-permute-start.22 = (bf16[128,256]{1,0:T(8,128)(2,1)S(1)}, bf16[128,256]{1,0:T(8,128)(2,1)S(1)}, u32[]{:S(2)}, u32[]{:S(2)}) collective-permute-start(bf16[128,256]{1,0:T(8,128)(2,1)S(1)} %get-tuple-element.72), channel_id=1, source_target_pairs={{0,3},{1,2},{2,1},{3,0},{4,7},{5,6},{6,5},{7,4},{8,11},{9,10},{10,... | collective-permute-start | bytes 196616 | tf_op jit(solution)/shard_map/ppermute | solution.py:38
  115.2 6.1 %collective-permute-start.28 = (bf16[128,256]{1,0:T(8,128)(2,1)S(1)}, bf16[128,256]{1,0:T(8,128)(2,1)S(1)}, u32[]{:S(2)}, u32[]{:S(2)}) collective-permute-start(bf16[128,256]{1,0:T(8,128)(2,1)S(1)} %get-tuple-element.77.refs_0_.refs_8_.refs_13_), channel_id=1, source_target_pairs={{0,1},{1,0},{2,3},{3,2},{4,5},{5,4},{6,7},{7,6},{8,9},{9,8},{10,11... | collective-permute-start | bytes 196616 | tf_op jit(solution)/shard_map/ppermute | solution.py:38
  116.2 7.9 %collective-permute-start.29 = (bf16[128,256]{1,0:T(8,128)(2,1)S(1)}, bf16[128,256]{1,0:T(8,128)(2,1)S(1)}, u32[]{:S(2)}, u32[]{:S(2)}) collective-permute-start(bf16[128,256]{1,0:T(8,128)(2,1)S(1)} %get-tuple-element.77.refs_0_.refs_8_.refs_13_), channel_id=1, source_target_pairs={{0,2},{1,3},{2,0},{3,1},{4,6},{5,7},{6,4},{7,5},{8,10},{9,11},{10,... | collective-permute-start | bytes 196616 | tf_op jit(solution)/shard_map/ppermute | solution.py:38
  117.3 6.8 %collective-permute-start.30 = (bf16[128,256]{1,0:T(8,128)(2,1)S(1)}, bf16[128,256]{1,0:T(8,128)(2,1)S(1)}, u32[]{:S(2)}, u32[]{:S(2)}) collective-permute-start(bf16[128,256]{1,0:T(8,128)(2,1)S(1)} %get-tuple-element.77.refs_0_.refs_8_.refs_13_), channel_id=1, source_target_pairs={{0,3},{1,2},{2,1},{3,0},{4,7},{5,6},{6,5},{7,4},{8,11},{9,10},{10,... | collective-permute-start | bytes 196616 | tf_op jit(solution)/shard_map/ppermute | solution.py:38
  119.6 8.2 %collective-permute-start.33 = (bf16[4,128,256]{2,1,0:T(8,128)(2,1)S(1)}, bf16[4,128,256]{2,1,0:T(8,128)(2,1)S(1)}, u32[]{:S(2)}, u32[]{:S(2)}) collective-permute-start(bf16[4,128,256]{2,1,0:T(8,128)(2,1)S(1)} %get-tuple-element.82), channel_id=1, source_target_pairs={{0,4},{4,0},{8,12},{12,8},{16,20},{20,16},{24,28},{28,24},{1,5},{5... | collective-permute-start | bytes 786440 | tf_op jit(solution)/shard_map/ppermute | solution.py:27
  119.6 9.5 %collective-permute-start.34 = (bf16[4,128,256]{2,1,0:T(8,128)(2,1)S(1)}, bf16[4,128,256]{2,1,0:T(8,128)(2,1)S(1)}, u32[]{:S(2)}, u32[]{:S(2)}) collective-permute-start(bf16[4,128,256]{2,1,0:T(8,128)(2,1)S(1)} %get-tuple-element.83), channel_id=1, source_target_pairs={{0,28},{4,8},{8,4},{12,16},{16,12},{20,24},{24,20},{28,0},{1,29},{... | collective-permute-start | bytes 786440 | tf_op jit(solution)/shard_map/ppermute | solution.py:33
  124.2 13.5 %collective-permute-start.31 = (bf16[4,128,256]{2,1,0:T(8,128)(2,1)S(1)}, bf16[4,128,256]{2,1,0:T(8,128)(2,1)S(1)}, u32[]{:S(2)}, u32[]{:S(2)}) collective-permute-start(bf16[4,128,256]{2,1,0:T(8,128)(2,1)S(1)} %pad_maximum_fusion.1), channel_id=1, source_target_pairs={{0,4},{4,0},{8,12},{12,8},{16,20},{20,16},{24,28},{28,24},{1,5},{5... | collective-permute-start | bytes 786440 | tf_op jit(solution)/shard_map/ppermute | solution.py:27
  124.2 13.4 %collective-permute-start.32 = (bf16[4,128,256]{2,1,0:T(8,128)(2,1)S(1)}, bf16[4,128,256]{2,1,0:T(8,128)(2,1)S(1)}, u32[]{:S(2)}, u32[]{:S(2)}) collective-permute-start(bf16[4,128,256]{2,1,0:T(8,128)(2,1)S(1)} %pad_maximum_fusion.1), channel_id=1, source_target_pairs={{0,28},{4,8},{8,4},{12,16},{16,12},{20,24},{24,20},{28,0},{1,29},{... | collective-permute-start | bytes 786440 | tf_op jit(solution)/shard_map/ppermute | solution.py:33
  129.2 5.0 %collective-permute-start.35 = (bf16[128,256]{1,0:T(8,128)(2,1)S(1)}, bf16[128,256]{1,0:T(8,128)(2,1)S(1)}, u32[]{:S(2)}, u32[]{:S(2)}) collective-permute-start(bf16[128,256]{1,0:T(8,128)(2,1)S(1)} %get-tuple-element.85), channel_id=1, source_target_pairs={{0,1},{1,0},{2,3},{3,2},{4,5},{5,4},{6,7},{7,6},{8,9},{9,8},{10,11... | collective-permute-start | bytes 196616 | tf_op jit(solution)/shard_map/ppermute | solution.py:38
  129.3 8.4 %collective-permute-start.36 = (bf16[128,256]{1,0:T(8,128)(2,1)S(1)}, bf16[128,256]{1,0:T(8,128)(2,1)S(1)}, u32[]{:S(2)}, u32[]{:S(2)}) collective-permute-start(bf16[128,256]{1,0:T(8,128)(2,1)S(1)} %get-tuple-element.86), channel_id=1, source_target_pairs={{0,2},{1,3},{2,0},{3,1},{4,6},{5,7},{6,4},{7,5},{8,10},{9,11},{10,... | collective-permute-start | bytes 196616 | tf_op jit(solution)/shard_map/ppermute | solution.py:38
  131.3 6.3 %collective-permute-start.37 = (bf16[128,256]{1,0:T(8,128)(2,1)S(1)}, bf16[128,256]{1,0:T(8,128)(2,1)S(1)}, u32[]{:S(2)}, u32[]{:S(2)}) collective-permute-start(bf16[128,256]{1,0:T(8,128)(2,1)S(1)} %get-tuple-element.87), channel_id=1, source_target_pairs={{0,3},{1,2},{2,1},{3,0},{4,7},{5,6},{6,5},{7,4},{8,11},{9,10},{10,... | collective-permute-start | bytes 196616 | tf_op jit(solution)/shard_map/ppermute | solution.py:38
  139.8 6.3 %collective-permute-start.45 = (bf16[128,256]{1,0:T(8,128)(2,1)S(1)}, bf16[128,256]{1,0:T(8,128)(2,1)S(1)}, u32[]{:S(2)}, u32[]{:S(2)}) collective-permute-start(bf16[128,256]{1,0:T(8,128)(2,1)S(1)} %get-tuple-element.96.refs_8_.refs_14_), channel_id=1, source_target_pairs={{0,3},{1,2},{2,1},{3,0},{4,7},{5,6},{6,5},{7,4},{8,11},{9,10},{10,... | collective-permute-start | bytes 196616 | tf_op jit(solution)/shard_map/ppermute | solution.py:38
  142.0 5.5 %collective-permute-start.43 = (bf16[128,256]{1,0:T(8,128)(2,1)S(1)}, bf16[128,256]{1,0:T(8,128)(2,1)S(1)}, u32[]{:S(2)}, u32[]{:S(2)}) collective-permute-start(bf16[128,256]{1,0:T(8,128)(2,1)S(1)} %get-tuple-element.96.refs_8_.refs_14_), channel_id=1, source_target_pairs={{0,1},{1,0},{2,3},{3,2},{4,5},{5,4},{6,7},{7,6},{8,9},{9,8},{10,11... | collective-permute-start | bytes 196616 | tf_op jit(solution)/shard_map/ppermute | solution.py:38
  142.0 5.5 %collective-permute-start.44 = (bf16[128,256]{1,0:T(8,128)(2,1)S(1)}, bf16[128,256]{1,0:T(8,128)(2,1)S(1)}, u32[]{:S(2)}, u32[]{:S(2)}) collective-permute-start(bf16[128,256]{1,0:T(8,128)(2,1)S(1)} %get-tuple-element.96.refs_8_.refs_14_), channel_id=1, source_target_pairs={{0,2},{1,3},{2,0},{3,1},{4,6},{5,7},{6,4},{7,5},{8,10},{9,11},{10,... | collective-permute-start | bytes 196616 | tf_op jit(solution)/shard_map/ppermute | solution.py:38
  144.3 6.8 %collective-permute-start.38 = (bf16[4,128,256]{2,1,0:T(8,128)(2,1)S(1)}, bf16[4,128,256]{2,1,0:T(8,128)(2,1)S(1)}, u32[]{:S(2)}, u32[]{:S(2)}) collective-permute-start(bf16[4,128,256]{2,1,0:T(8,128)(2,1)S(1)} %get-tuple-element.90), channel_id=1, source_target_pairs={{0,4},{4,0},{8,12},{12,8},{16,20},{20,16},{24,28},{28,24},{1,5},{5... | collective-permute-start | bytes 786440 | tf_op jit(solution)/shard_map/ppermute | solution.py:27
  144.3 9.5 %collective-permute-start.39 = (bf16[4,128,256]{2,1,0:T(8,128)(2,1)S(1)}, bf16[4,128,256]{2,1,0:T(8,128)(2,1)S(1)}, u32[]{:S(2)}, u32[]{:S(2)}) collective-permute-start(bf16[4,128,256]{2,1,0:T(8,128)(2,1)S(1)} %get-tuple-element.91), channel_id=1, source_target_pairs={{0,28},{4,8},{8,4},{12,16},{16,12},{20,24},{24,20},{28,0},{1,29},{... | collective-permute-start | bytes 786440 | tf_op jit(solution)/shard_map/ppermute | solution.py:33
  147.5 10.8 %collective-permute-start.46 = (bf16[4,128,256]{2,1,0:T(8,128)(2,1)S(1)}, bf16[4,128,256]{2,1,0:T(8,128)(2,1)S(1)}, u32[]{:S(2)}, u32[]{:S(2)}) collective-permute-start(bf16[4,128,256]{2,1,0:T(8,128)(2,1)S(1)} %pad_maximum_fusion.2), channel_id=1, source_target_pairs={{0,4},{4,0},{8,12},{12,8},{16,20},{20,16},{24,28},{28,24},{1,5},{5... | collective-permute-start | bytes 786440 | tf_op jit(solution)/shard_map/ppermute | solution.py:27
  147.6 11.7 %collective-permute-start.47 = (bf16[4,128,256]{2,1,0:T(8,128)(2,1)S(1)}, bf16[4,128,256]{2,1,0:T(8,128)(2,1)S(1)}, u32[]{:S(2)}, u32[]{:S(2)}) collective-permute-start(bf16[4,128,256]{2,1,0:T(8,128)(2,1)S(1)} %pad_maximum_fusion.2), channel_id=1, source_target_pairs={{0,28},{4,8},{8,4},{12,16},{16,12},{20,24},{24,20},{28,0},{1,29},{... | collective-permute-start | bytes 786440 | tf_op jit(solution)/shard_map/ppermute | solution.py:33
  153.8 5.4 %collective-permute-start.40 = (bf16[128,256]{1,0:T(8,128)(2,1)S(1)}, bf16[128,256]{1,0:T(8,128)(2,1)S(1)}, u32[]{:S(2)}, u32[]{:S(2)}) collective-permute-start(bf16[128,256]{1,0:T(8,128)(2,1)S(1)} %get-tuple-element.93), channel_id=1, source_target_pairs={{0,1},{1,0},{2,3},{3,2},{4,5},{5,4},{6,7},{7,6},{8,9},{9,8},{10,11... | collective-permute-start | bytes 196616 | tf_op jit(solution)/shard_map/ppermute | solution.py:38
  154.3 7.6 %collective-permute-start.41 = (bf16[128,256]{1,0:T(8,128)(2,1)S(1)}, bf16[128,256]{1,0:T(8,128)(2,1)S(1)}, u32[]{:S(2)}, u32[]{:S(2)}) collective-permute-start(bf16[128,256]{1,0:T(8,128)(2,1)S(1)} %get-tuple-element.94), channel_id=1, source_target_pairs={{0,2},{1,3},{2,0},{3,1},{4,6},{5,7},{6,4},{7,5},{8,10},{9,11},{10,... | collective-permute-start | bytes 196616 | tf_op jit(solution)/shard_map/ppermute | solution.py:38
  156.6 6.2 %collective-permute-start.42 = (bf16[128,256]{1,0:T(8,128)(2,1)S(1)}, bf16[128,256]{1,0:T(8,128)(2,1)S(1)}, u32[]{:S(2)}, u32[]{:S(2)}) collective-permute-start(bf16[128,256]{1,0:T(8,128)(2,1)S(1)} %get-tuple-element.95), channel_id=1, source_target_pairs={{0,3},{1,2},{2,1},{3,0},{4,7},{5,6},{6,5},{7,4},{8,11},{9,10},{10,... | collective-permute-start | bytes 196616 | tf_op jit(solution)/shard_map/ppermute | solution.py:38
  (6 other events, 54.5 us)
